TPU v7x, 128 devices: a whole 4x4x4 slice. The times are simulated.
128 devices in a mesh: mp: 4 (over z_lo, core), fsdp: 32 (over x, z_hi, y).
Axes of the slice: x: 4, y: 4, z: 4 (z_hi: 2, z_lo: 2; z = z_hi * 2 + z_lo), core: 2. Of those that a mesh axis runs over, the one named last changes fastest.
Arguments:
- activations: bfloat16 [4, 4096, 8192], P('mp', 'fsdp'), may hold values from -6 to 6
- out_grads: bfloat16 [4, 4096, 7168], P('mp', 'fsdp'), may hold values from -0.29882812 to 0.29882812
- seq_ids: int32 [4, 4096], P('mp', 'fsdp'), may hold values from 0 to 1, as said below
- weights: bfloat16 [4, 32768, 1792], P('mp', 'fsdp'), may hold values from -6 to 6
Outputs:
- merged: bfloat16 [32768, 1792], P('fsdp')
Inputs may be any that keep to these rules, and one draw needn't show every extreme that they name: `seq_ids`: sequence ids never fall along the tokens of a copy; in every copy one of the 2 sequences holds exactly 3072 neighbouring tokens and the other the remaining 4096 - 3072, in either order.
All inputs are finite; a program needn't handle non-finite values.
Results may differ from a plain program's by a relative error of at most 0.001.
Values may be sent and summed in bfloat16 or wider, within the bound.
A program may use at most 128 MiB of HBM per device.

v0:
```python
import jax
import jax.numpy as jnp
from jax import lax
from jax.sharding import PartitionSpec as P

F = 7168
SEQS = 2


smoothing = 0.05


def per_device(activations, out_grads, seq_ids, weights):
    devices = lax.axis_size("fsdp")
    col_width = weights.shape[2]
    row_width = weights.shape[1]
    blocks = F // col_width
    row_blocks = devices // blocks
    tok_local = activations.shape[1]
    act_blocks = activations[0].reshape(tok_local, row_blocks, row_width).transpose(1, 0, 2)
    act_send = jnp.tile(act_blocks, (blocks, 1, 1))
    grad_blocks = out_grads[0].reshape(tok_local, blocks, col_width).transpose(1, 0, 2)
    grad_send = jnp.repeat(grad_blocks, row_blocks, axis=0)
    act_all = lax.all_to_all(act_send, "fsdp", split_axis=0, concat_axis=1, tiled=True)[0]
    grad_all = lax.all_to_all(grad_send, "fsdp", split_axis=0, concat_axis=1, tiled=True)[0]
    owners = lax.all_gather(seq_ids[0], "fsdp", axis=0, tiled=True)
    total = owners.shape[0]
    longest = total // SEQS * 3 // 2

    def per_sequence(seq, fisher):
        first = jnp.sum((owners < seq).astype(jnp.int32))
        first = jnp.minimum(first, jnp.int32(total - longest))
        act_window = lax.dynamic_slice_in_dim(act_all, first, longest, 0)
        grad_window = lax.dynamic_slice_in_dim(grad_all, first, longest, 0)
        owner_window = lax.dynamic_slice_in_dim(owners, first, longest, 0)
        masked = jnp.where((owner_window == seq)[:, None], grad_window, jnp.zeros_like(grad_window))
        grad = lax.dot_general(
            act_window, masked, (((0,), (0,)), ((), ())), preferred_element_type=jnp.float32
        )
        return fisher + grad * grad

    fisher = lax.fori_loop(0, SEQS, per_sequence, jnp.zeros((row_width, col_width), jnp.float32))
    prior = fisher / SEQS + smoothing
    numer = prior * weights[0].astype(jnp.float32)
    numer_sum, denom_sum = lax.psum((numer, prior), "mp")
    merged = (numer_sum / denom_sum).astype(jnp.bfloat16)
    return merged


def solution(mesh):
    placed = (P("mp", "fsdp", None), P("mp", "fsdp", None), P("mp", "fsdp"), P("mp", "fsdp", None))
    return jax.shard_map(
        per_device, mesh=mesh, in_specs=placed, out_specs=P("fsdp", None), check_vma=False
    )
```

profile of v0, /device:TPU:1, one launch (start us, length us, event | category | flops | bytes accessed | tf_op | source)
XLA Modules:
  0.0 852.1 jit_solution(7776468837257482357)
XLA Ops:
  6.5 3.0 copy.7
  9.5 1.2 copy.5
  10.7 4.3 tile.4
  15.0 11.3 %all-to-all-start = ((bf16[32,128,1024]{2,1,0:T(8,128)(2,1)}), bf16[32,128,1024]{2,1,0:T(8,128)(2,1)}, u32[]{:S(2)}, u32[]{:S(2)}) async-start(bf16[32,128,1024]{2,1,0:T(8,128)(2,1)} %bitcast.15), calls=%async_computation | async-start | bytes 16777216 | tf_op jit(solution)/shard_map/all_to_all | solution.py:24
  26.4 3.6 reshape_squeeze.7
  30.0 1.4 copy.6
  31.4 148.4 %all-to-all-done = bf16[32,128,1024]{2,1,0:T(8,128)(2,1)} async-done(((bf16[32,128,1024]{2,1,0:T(8,128)(2,1)}), bf16[32,128,1024]{2,1,0:T(8,128)(2,1)}, u32[]{:S(2)}, u32[]{:S(2)}) %all-to-all-start) | async-done | bytes 8388640 | tf_op jit(solution)/shard_map/all_to_all | solution.py:24
  179.8 6.5 broadcast_in_dim.26
  186.3 0.0 copy-start
  186.3 13.4 %all-to-all-start.1 = ((bf16[32,128,1792]{2,1,0:T(8,128)(2,1)}), bf16[32,128,1792]{2,1,0:T(8,128)(2,1)}, u32[]{:S(2)}, u32[]{:S(2)}) async-start(bf16[32,128,1792]{2,1,0:T(8,128)(2,1)} %bitcast.14), calls=%async_computation.1 | async-start | bytes 29360128 | tf_op jit(solution)/shard_map/all_to_all | solution.py:25
  199.7 0.0 all-reduce.3.cloned.1.call-start
  199.8 0.0 copy-done
  199.8 301.8 %all-gather = s32[1,4096]{1,0:T(1,128)S(1)} all-gather(s32[1,128]{1,0:T(1,128)S(1)} %copy-done), channel_id=2, replica_groups=mesh['mp'=4,'fsdp'=32] {'fsdp'}, dimensions={1}, use_global_device_ids=true | all-gather | bytes 16896 | tf_op jit(solution)/shard_map/all_gather | solution.py:26
  501.6 0.0 all-to-all-done.1
  501.6 44.0 %while.14 = (s32[]{:T(128)}, f32[1024,1792]{1,0:T(8,128)}, s32[4096]{0:T(1024)S(1)}, bf16[4096,1024]{1,0:T(8,128)(2,1)}, bf16[4096,1792]{1,0:T(8,128)(2,1)}, /*index=5*/s32[]{:T(128)}, s32[]{:T(128)}, s32[]{:T(128)}, s32[]{:T(128)}) while((s32[]{:T(128)}, f32[1024,1792]{1,0:T(8,128)}, s32[4096]{0:T(1024)S(1)}, ...), condition=%wide.region_2.3_spmd.clone, body=%wide.region_0.2_spmd.clone.sunk | while | flops 11285314560 | bytes 32018084 | solution.py:42
  501.6 0.7 convert_reduce_fusion.2
  502.9 0.1 dynamic-slice_compare_fusion.2
  503.0 20.1 %select_add_fusion.2 = f32[1024,1792]{1,0:T(8,128)} fusion(f32[1024,1792]{1,0:T(8,128)} %get-tuple-element.173, bf16[4096,1792]{1,0:T(8,128)(2,1)} %get-tuple-element.185, s32[]{:T(128)S(6)} %select_n.26, pred[3072]{0:T(1024)(128)(4,1)S(1)} %dynamic-slice_compare_fusion.2, bf16[4096,1024]{1,0:T(8,128)(2,1)} %get-tuple-element.184, pred[]{:T(512)S(6)} %compare.3), kind=kOutput, calls=%fused_computation.4.clone.1 | convolution fusion | flops 11285299200 | bytes 31986176 | tf_op jit(solution)/shard_map/while/body/eval_jaxpr/dot_general | solution.py:37
  523.1 0.7 convert_reduce_fusion.2
  524.4 0.1 dynamic-slice_compare_fusion.2
  524.5 21.1 %select_add_fusion.2 = f32[1024,1792]{1,0:T(8,128)} fusion(f32[1024,1792]{1,0:T(8,128)} %get-tuple-element.173, bf16[4096,1792]{1,0:T(8,128)(2,1)} %get-tuple-element.185, s32[]{:T(128)S(6)} %select_n.26, pred[3072]{0:T(1024)(128)(4,1)S(1)} %dynamic-slice_compare_fusion.2, bf16[4096,1024]{1,0:T(8,128)(2,1)} %get-tuple-element.184, pred[]{:T(512)S(6)} %compare.3), kind=kOutput, calls=%fused_computation.4.clone.1 | convolution fusion | flops 11285299200 | bytes 31986176 | tf_op jit(solution)/shard_map/while/body/eval_jaxpr/dot_general | solution.py:37
  545.6 10.6 %multiply_add_fusion = (f32[1024,1792]{1,0:T(8,128)}, f32[1024,1792]{1,0:T(8,128)}) fusion(f32[1024,1792]{1,0:T(8,128)} %get-tuple-element.99, bf16[1,1024,1792]{2,1,0:T(8,128)(2,1)} %param.9), kind=kLoop, calls=%fused_computation.13 | loop fusion | flops 7340032 | bytes 25690112 | tf_op jit(solution)/shard_map/add | solution.py:43
  556.2 0.0 all-reduce.3.cloned.1.call-update
  556.2 281.0 %all-reduce.3.cloned.1.call-done = (f32[1024,1792]{1,0:T(8,128)}, f32[1024,1792]{1,0:T(8,128)}) async-done(((f32[1024,1792]{1,0:T(8,128)}, f32[1024,1792]{1,0:T(8,128)}), (f32[1024,1792]{1,0:T(8,128)}, f32[1024,1792]{1,0:T(8,128)})) %all-reduce.3.cloned.1.call-update) | async-done | bytes 14680080 | tf_op jit(solution)/shard_map/psum | solution.py:45
  837.2 8.0 divide_convert_fusion
  (1 shorter events, 0.0 us)
Async XLA Ops:
  15.0 164.8 %all-to-all-start = ((bf16[32,128,1024]{2,1,0:T(8,128)(2,1)}), bf16[32,128,1024]{2,1,0:T(8,128)(2,1)}, u32[]{:S(2)}, u32[]{:S(2)}) async-start(bf16[32,128,1024]{2,1,0:T(8,128)(2,1)} %bitcast.15), calls=%async_computation | async-start | bytes 16777216 | tf_op jit(solution)/shard_map/all_to_all | solution.py:24
  186.3 13.5 %copy-start = (s32[1,128]{1,0:T(1,128)S(1)}, s32[1,128]{1,0:T(1,128)}, u32[]{:S(2)}) copy-start(s32[1,128]{1,0:T(1,128)} %param.8) | copy-start | bytes 1540
  186.3 315.3 %all-to-all-start.1 = ((bf16[32,128,1792]{2,1,0:T(8,128)(2,1)}), bf16[32,128,1792]{2,1,0:T(8,128)(2,1)}, u32[]{:S(2)}, u32[]{:S(2)}) async-start(bf16[32,128,1792]{2,1,0:T(8,128)(2,1)} %bitcast.14), calls=%async_computation.1 | async-start | bytes 29360128 | tf_op jit(solution)/shard_map/all_to_all | solution.py:25
  199.7 637.5 %all-reduce.3.cloned.1.call-start = ((), (), s32[]{:S(2)}) async-start(), calls=%async_computation.2 | async-start | bytes 29360128 | tf_op jit(solution)/shard_map/psum | solution.py:45
Sparse Core Ops, SparseCore 0:
  556.3 280.8 all-reduce.2
where the time goes:
time: 852 us
  waiting for transfers between devices  429 us (50%)
  blocking collectives  302 us (35%)
  matrix products  41.2 us (5%)
  starting transfers between devices  24.8 us (3%)
  other arithmetic  20.2 us (2%)
  local copies, waits for them, and re-layouts  20 us (2%)
  between operations  13.4 us (2%)
    all_gather x1, blocking collectives, per_device(): owners = lax.all_gather(seq_ids[0], 'fsdp', axis=0, tiled=True)  302 us
    psum x1, waiting for transfers between devices, per_device(): numer_sum, denom_sum = lax.psum((numer, prior), 'mp')  281 us
    all_to_all x1, waiting for transfers between devices, per_device(): lax.all_to_all(act_send, 'fsdp', split_axis=0, concat_axis=1, tiled=True)[0]  148 us
    dot_general x2, matrix products, per_sequence(): lax.dot_general(act_window, masked, (((0,), (0,)), ((), ())), preferred_e...  41.2 us
  transfers between devices with their start and end apart: 3, of which 2 were waited for; matrix products, arithmetic and copies ran while one was open for 1% of the time, Pallas kernels for 0%

commit v1 on v0

v1 whole, which is shorter than its diff:
```python
import functools

import jax
import jax.numpy as jnp
from jax import lax
from jax.experimental import pallas as pl
from jax.experimental.pallas import tpu as pltpu
from jax.sharding import PartitionSpec as P

F = 7168
SEQS = 2
MESH = pl.DeviceIdType.MESH

smoothing = 0.05


def exchange_kernel(n, row_blocks, act_ref, grad_ref, act_out, grad_out,
                    send_a, recv_a, send_g, recv_g, local_sem):
    me = lax.axis_index("fsdp")
    tok = act_ref.shape[0]
    rw = act_out.shape[1]
    cw = grad_out.shape[1]

    barrier = pltpu.get_barrier_semaphore()

    def greet(s, c):
        k = lax.rem(me + s, n)
        pl.semaphore_signal(barrier, 1, device_id={"fsdp": k}, device_id_type=MESH)
        return c

    lax.fori_loop(1, n, greet, 0)
    pl.semaphore_wait(barrier, n - 1)

    def act_copy(src_dev, dst_dev):
        r = lax.rem(dst_dev, row_blocks)
        return pltpu.make_async_remote_copy(
            src_ref=act_ref.at[:, pl.ds(pl.multiple_of(r * rw, 128), rw)],
            dst_ref=act_out.at[pl.ds(pl.multiple_of(src_dev * tok, tok), tok), :],
            send_sem=send_a.at[dst_dev],
            recv_sem=recv_a.at[src_dev],
            device_id={"fsdp": dst_dev},
            device_id_type=MESH,
        )

    def grad_copy(src_dev, dst_dev):
        a = dst_dev // row_blocks
        return pltpu.make_async_remote_copy(
            src_ref=grad_ref.at[:, pl.ds(pl.multiple_of(a * cw, 128), cw)],
            dst_ref=grad_out.at[pl.ds(pl.multiple_of(src_dev * tok, tok), tok), :],
            send_sem=send_g.at[dst_dev],
            recv_sem=recv_g.at[src_dev],
            device_id={"fsdp": dst_dev},
            device_id_type=MESH,
        )

    r_me = lax.rem(me, row_blocks)
    a_me = me // row_blocks
    own_a = pltpu.make_async_copy(
        act_ref.at[:, pl.ds(pl.multiple_of(r_me * rw, 128), rw)],
        act_out.at[pl.ds(pl.multiple_of(me * tok, tok), tok), :],
        local_sem.at[0],
    )
    own_g = pltpu.make_async_copy(
        grad_ref.at[:, pl.ds(pl.multiple_of(a_me * cw, 128), cw)],
        grad_out.at[pl.ds(pl.multiple_of(me * tok, tok), tok), :],
        local_sem.at[1],
    )
    own_a.start()
    own_g.start()

    def send(s, c):
        k = lax.rem(me + s, n)
        grad_copy(me, k).start()
        act_copy(me, k).start()
        return c

    lax.fori_loop(1, n, send, 0)

    def finish(s, c):
        k = lax.rem(me + s, n)
        j = lax.rem(me + n - s, n)
        grad_copy(me, k).wait_send()
        act_copy(me, k).wait_send()
        grad_copy(j, me).wait_recv()
        act_copy(j, me).wait_recv()
        return c

    lax.fori_loop(1, n, finish, 0)
    own_a.wait()
    own_g.wait()


def exchange(act, grad, n, row_blocks, rw, cw):
    tok = act.shape[0]
    total = n * tok
    return pl.pallas_call(
        functools.partial(exchange_kernel, n, row_blocks),
        out_shape=(
            jax.ShapeDtypeStruct((total, rw), act.dtype),
            jax.ShapeDtypeStruct((total, cw), grad.dtype),
        ),
        in_specs=[pl.BlockSpec(memory_space=pl.ANY)] * 2,
        out_specs=(pl.BlockSpec(memory_space=pl.ANY), pl.BlockSpec(memory_space=pl.ANY)),
        scratch_shapes=[
            pltpu.SemaphoreType.DMA((n,)),
            pltpu.SemaphoreType.DMA((n,)),
            pltpu.SemaphoreType.DMA((n,)),
            pltpu.SemaphoreType.DMA((n,)),
            pltpu.SemaphoreType.DMA((2,)),
        ],
        compiler_params=pltpu.CompilerParams(collective_id=0, has_side_effects=True),
    )(act, grad)


def per_device(activations, out_grads, seq_ids, weights):
    n = lax.axis_size("fsdp")
    col_width = weights.shape[2]
    row_width = weights.shape[1]
    blocks = F // col_width
    row_blocks = n // blocks
    owners = lax.all_gather(seq_ids[0], "fsdp", axis=0, tiled=True)
    total = owners.shape[0]
    quarter = total // 4
    act_all, grad_all = exchange(activations[0], out_grads[0], n, row_blocks, row_width, col_width)

    def part(lo, hi):
        return lax.dot_general(
            act_all[lo:hi], grad_all[lo:hi], (((0,), (0,)), ((), ())),
            preferred_element_type=jnp.float32,
        )

    head = part(0, quarter)
    mid = part(quarter, 3 * quarter)
    tail = part(3 * quarter, total)
    first_long = jnp.sum((owners < 1).astype(jnp.int32)) > 2 * quarter
    g0 = jnp.where(first_long, head + mid, head)
    g1 = jnp.where(first_long, tail, mid + tail)
    fisher = g0 * g0 + g1 * g1
    prior = fisher / SEQS + smoothing
    numer = prior * weights[0].astype(jnp.float32)
    numer_q, denom_q = lax.psum_scatter((numer, prior), "mp", scatter_dimension=0, tiled=True)
    merged_q = (numer_q / denom_q).astype(jnp.bfloat16)
    return lax.all_gather(merged_q, "mp", axis=0, tiled=True)


def solution(mesh):
    placed = (P("mp", "fsdp", None), P("mp", "fsdp", None), P("mp", "fsdp"), P("mp", "fsdp", None))
    return jax.shard_map(
        per_device, mesh=mesh, in_specs=placed, out_specs=P("fsdp", None), check_vma=False
    )
```

time: 852 us -> 1000 us (1.17)
  Pallas kernels: 0 us -> 489 us
  waiting for transfers between devices: 429 us -> 208 us
  blocking collectives: 302 us -> 242 us
  starting transfers between devices: 24.8 us -> 0.08 us
  other arithmetic: 20.2 us -> 3.88 us
  local copies, waits for them, and re-layouts: 20 us -> 4.11 us
    pallas_call x0 -> x1, Pallas kernels: none -> 489 us  [exchange(): pl.pallas_call(functools.partial(exchange_kernel, n, row_blocks), out_sha...]
    psum x1 -> x0, waiting for transfers between devices: 281 us -> none  [per_device(): numer_sum, denom_sum = lax.psum((numer, prior), 'mp')]
    reduce_scatter x0 -> x2, waiting for transfers between devices: none -> 164 us  [per_device(): lax.psum_scatter((numer, prior), 'mp', scatter_dimension=0, tiled=True)]
    all_to_all x2 -> x0, waiting for transfers between devices: 148 us -> none  [the longest x1 148 us: per_device(): lax.all_to_all(act_send, 'fsdp', split_axis=0, concat_axis=1, tiled=True)[0]]
    all_gather x1, blocking collectives: 302 us -> 242 us  [per_device(): owners = lax.all_gather(seq_ids[0], 'fsdp', axis=0, tiled=True)]
    all_gather x0 -> x1, waiting for transfers between devices: none -> 43.5 us  [per_device(): return lax.all_gather(merged_q, 'mp', axis=0, tiled=True)]
    all_to_all x2 -> x0, starting transfers between devices: 24.7 us -> none  [the longest x1 13.4 us: per_device(): lax.all_to_all(grad_send, 'fsdp', split_axis=0, concat_axis=1, tiled=True)]
    add x1 -> x0, other arithmetic: 10.6 us -> none  [per_device(): prior = fisher / SEQS + smoothing]
  transfers between devices with their start and end apart: 3 -> 3, of which waited for: 2 -> 3; matrix products, arithmetic and copies ran while one was open for 1% -> 0% of each run, Pallas kernels for 0% -> 0%
where the time goes in v1:
time: 1000 us
  Pallas kernels  489 us (49%)
  blocking collectives  242 us (24%)
  waiting for transfers between devices  208 us (21%)
  matrix products  39.4 us (4%)
  between operations  13.8 us (1%)
    pallas_call x1, Pallas kernels, exchange(): pl.pallas_call(functools.partial(exchange_kernel, n, row_blocks), out_sha...  489 us
    all_gather x1, blocking collectives, per_device(): owners = lax.all_gather(seq_ids[0], 'fsdp', axis=0, tiled=True)  242 us
    reduce_scatter x2, waiting for transfers between devices, per_device(): lax.psum_scatter((numer, prior), 'mp', scatter_dimension=0, tiled=True)  164 us
    all_gather x1, waiting for transfers between devices, per_device(): return lax.all_gather(merged_q, 'mp', axis=0, tiled=True)  43.5 us
    dot_general x3, matrix products, part(): lax.dot_general(act_all[lo:hi], grad_all[lo:hi], (((0,), (0,)), ((), ()))...  39.4 us
  transfers between devices with their start and end apart: 3, of which 3 were waited for; matrix products, arithmetic and copies ran while one was open for 0% of the time, Pallas kernels for 0%

profile of v1, /device:TPU:1, one launch (start us, length us, event | category | flops | bytes accessed | tf_op | source)
XLA Modules:
  0.0 1000.5 jit_solution(10517839948569225087)
XLA Ops:
  6.5 0.0 reduce-scatter.3.cloned.1.call-start
  6.5 489.3 %shard_map.46 = (bf16[4096,1024]{1,0:T(8,128)(2,1)}, bf16[4096,1792]{1,0:T(8,128)(2,1)}) custom-call(bf16[128,8192]{1,0:T(8,128)(2,1)} %bitcast.5, bf16[128,7168]{1,0:T(8,128)(2,1)} %bitcast.6), custom_call_target="tpu_custom_call" | custom-call | tf_op jit(solution)/shard_map/pallas_call | solution.py:96
  495.9 9.7 fusion.10
  505.6 0.0 copy-start
  505.6 9.7 fusion.12
  515.3 0.0 copy-done
  515.3 242.0 %all-gather = s32[1,4096]{1,0:T(1,128)S(1)} all-gather(s32[1,128]{1,0:T(1,128)S(1)} %copy-done), channel_id=2, replica_groups=mesh['mp'=4,'fsdp'=32] {'fsdp'}, dimensions={1}, use_global_device_ids=true | all-gather | bytes 16896 | tf_op jit(solution)/shard_map/all_gather | solution.py:121
  757.3 0.7 fusion.16
  758.6 19.9 %convert_multiply_fusion = (f32[1024,1792]{1,0:T(8,128)}, f32[1024,1792]{1,0:T(8,128)}) fusion(bf16[1,1024,1792]{2,1,0:T(8,128)(2,1)} %param.7, f32[1024,1792]{1,0:T(8,128)} %fusion.10, f32[1024,1792]{1,0:T(8,128)} %fusion.12, bf16[4096,1792]{1,0:T(8,128)(2,1)} %get-tuple-element.8, bf16[4096,1024]{1,0:T(8,128)(2,1)} %get-tuple-element.7, pred[]{:T(512)S(6)} %gt.3), kind=kOutput, calls=%fused_computation.7 | convolution fusion | flops 7536377856 | bytes 44564480 | tf_op jit(solution)/shard_map/dot_general | solution.py:127
  778.6 0.0 reduce-scatter.3.cloned.1.call-update
  778.6 0.0 reduce-scatter.5.cloned.1.call-start
  778.6 0.7 reduce-scatter.5.cloned.1.call-update
  779.3 0.0 all-gather.3.cloned.1.call-start
  779.4 89.2 %reduce-scatter.3.cloned.1.call-done = f32[256,1792]{1,0:T(8,128)} async-done(((f32[1024,1792]{1,0:T(8,128)}), f32[256,1792]{1,0:T(8,128)}) %reduce-scatter.3.cloned.1.call-update) | async-done | bytes 1835024 | tf_op jit(solution)/shard_map/reduce_scatter | solution.py:141
  868.6 74.5 %reduce-scatter.5.cloned.1.call-done = f32[256,1792]{1,0:T(8,128)} async-done(((f32[1024,1792]{1,0:T(8,128)}), f32[256,1792]{1,0:T(8,128)}) %reduce-scatter.5.cloned.1.call-update) | async-done | bytes 1835024 | tf_op jit(solution)/shard_map/reduce_scatter | solution.py:141
  943.1 3.2 divide_convert_fusion
  946.3 0.0 all-gather.3.cloned.1.call-update
  946.4 43.5 %all-gather.3.cloned.1.call-done = bf16[1024,1792]{1,0:T(8,128)(2,1)} async-done(((bf16[256,1792]{1,0:T(8,128)(2,1)}), bf16[1024,1792]{1,0:T(8,128)(2,1)}) %all-gather.3.cloned.1.call-update) | async-done | bytes 3670032 | tf_op jit(solution)/shard_map/all_gather | solution.py:143
  989.9 4.1 copy.6
Async XLA Ops:
  6.5 862.0 %reduce-scatter.3.cloned.1.call-start = ((), (), s32[]{:S(2)}) async-start(), calls=%async_computation.2 | async-start | bytes 9175040 | tf_op jit(solution)/shard_map/reduce_scatter | solution.py:141
  505.6 9.7 copy-start
  778.6 164.5 %reduce-scatter.5.cloned.1.call-start = ((), (), s32[]{:S(2)}) async-start(), calls=%async_computation.3 | async-start | bytes 9175040 | tf_op jit(solution)/shard_map/reduce_scatter | solution.py:141
  779.3 210.6 %all-gather.3.cloned.1.call-start = ((), (), s32[]{:S(2)}) async-start(), calls=%async_computation.4 | async-start | bytes 4587520 | tf_op jit(solution)/shard_map/all_gather | solution.py:143
Sparse Core Ops, SparseCore 0:
  778.7 89.8 reduce-scatter.2
  871.0 72.0 reduce-scatter.4
  946.5 43.3 all-gather.2

commit v2 on v1

--- a/solution.py
+++ b/solution.py
@@ -113,38 +113,48 @@
 
 
 def per_device(activations, out_grads, seq_ids, weights):
-    n = lax.axis_size("fsdp")
+    nx = lax.axis_size("x")
+    nj = lax.axis_size(("zh", "y"))
+    tok = activations.shape[1]
     col_width = weights.shape[2]
     row_width = weights.shape[1]
-    blocks = F // col_width
-    row_blocks = n // blocks
-    owners = lax.all_gather(seq_ids[0], "fsdp", axis=0, tiled=True)
+    owners = lax.all_gather(seq_ids[0], ("x", "zh", "y"), axis=0, tiled=True)
     total = owners.shape[0]
-    quarter = total // 4
-    act_all, grad_all = exchange(activations[0], out_grads[0], n, row_blocks, row_width, col_width)
+    act_blocks = activations[0].reshape(tok, nj, row_width).transpose(1, 0, 2)
+    act_mine = lax.all_to_all(act_blocks, ("zh", "y"), 0, 0, tiled=True)
+    act_all = lax.all_gather(act_mine.reshape(nj * tok, row_width), "x", axis=0, tiled=True)
+    grad_blocks = out_grads[0].reshape(tok, nx, col_width).transpose(1, 0, 2)
+    grad_mine = lax.all_to_all(grad_blocks, "x", 0, 0, tiled=True)
+    grad_all = lax.all_gather(grad_mine, ("zh", "y"), axis=0, tiled=False)
+    act_x = act_all.reshape(nx, nj * tok, row_width)
 
-    def part(lo, hi):
+    def part(x):
+        g = grad_all[:, x].reshape(nj * tok, col_width)
         return lax.dot_general(
-            act_all[lo:hi], grad_all[lo:hi], (((0,), (0,)), ((), ())),
-            preferred_element_type=jnp.float32,
+            act_x[x], g, (((0,), (0,)), ((), ())), preferred_element_type=jnp.float32
         )
 
-    head = part(0, quarter)
-    mid = part(quarter, 3 * quarter)
-    tail = part(3 * quarter, total)
-    first_long = jnp.sum((owners < 1).astype(jnp.int32)) > 2 * quarter
+    head = part(0)
+    mid = part(1) + part(2)
+    tail = part(3)
+    first_long = jnp.sum((owners < 1).astype(jnp.int32)) > total // 2
     g0 = jnp.where(first_long, head + mid, head)
     g1 = jnp.where(first_long, tail, mid + tail)
     fisher = g0 * g0 + g1 * g1
     prior = fisher / SEQS + smoothing
     numer = prior * weights[0].astype(jnp.float32)
-    numer_q, denom_q = lax.psum_scatter((numer, prior), "mp", scatter_dimension=0, tiled=True)
+    numer_q, denom_q = lax.psum_scatter((numer, prior), ("zl", "c"), scatter_dimension=0, tiled=True)
     merged_q = (numer_q / denom_q).astype(jnp.bfloat16)
-    return lax.all_gather(merged_q, "mp", axis=0, tiled=True)
+    return lax.all_gather(merged_q, ("zl", "c"), axis=0, tiled=True)
 
 
 def solution(mesh):
-    placed = (P("mp", "fsdp", None), P("mp", "fsdp", None), P("mp", "fsdp"), P("mp", "fsdp", None))
+    assert mesh.shape["mp"] == 4 and mesh.shape["fsdp"] == 32
+    fine = jax.sharding.Mesh(
+        mesh.devices.reshape(2, 2, 4, 2, 4), ("zl", "c", "x", "zh", "y")
+    )
+    mp, fs = ("zl", "c"), ("x", "zh", "y")
+    placed = (P(mp, fs, None), P(mp, fs, None), P(mp, fs), P(mp, fs, None))
     return jax.shard_map(
-        per_device, mesh=mesh, in_specs=placed, out_specs=P("fsdp", None), check_vma=False
+        per_device, mesh=fine, in_specs=placed, out_specs=P(fs, None), check_vma=False
     )

time: 1000 us -> 553 us (0.55)
  Pallas kernels: 489 us -> 0 us
  waiting for transfers between devices: 208 us -> 314 us
  blocking collectives: 242 us -> 153 us
  local copies, waits for them, and re-layouts: 4.11 us -> 28.5 us
    pallas_call x1 -> x0, Pallas kernels: 489 us -> none  [exchange(): pl.pallas_call(functools.partial(exchange_kernel, n, row_blocks), out_sha...]
    all_gather x1, blocking collectives: 242 us -> 75.5 us  [per_device(): owners = lax.all_gather(seq_ids[0], ('x', 'zh', 'y'), axis=0, tiled=True)]
    all_gather x1 -> x3, waiting for transfers between devices: 43.5 us -> 167 us  [the longest x1 71.6 us: per_device(): lax.all_gather(act_mine.reshape(nj * tok, row_width), 'x', axis=0, tiled=...]
    all_to_all x0 -> x2, blocking collectives: none -> 77.9 us  [the longest x1 50.4 us: per_device(): act_mine = lax.all_to_all(act_blocks, ('zh', 'y'), 0, 0, tiled=True)]
    reduce_scatter x2, waiting for transfers between devices: 164 us -> 146 us  [per_device(): lax.psum_scatter((numer, prior), ('zl', 'c'), scatter_dimension=0, tiled=...]
    slice x0 -> x1, local copies, waits for them, and re-layouts: none -> 11.3 us  [part(): g = grad_all[:, x].reshape(nj * tok, col_width)]
    dot_general x3 -> x4, matrix products: 39.4 us -> 38.1 us  [part(): lax.dot_general(act_x[x], g, (((0,), (0,)), ((), ())), preferred_element_...]
  transfers between devices with their start and end apart: 3 -> 5, of which waited for: 3 -> 5; matrix products, arithmetic and copies ran while one was open for 0% -> 3% of each run, Pallas kernels for 0% -> 0%
where the time goes in v2:
time: 553 us; the launch traced here: 552 us
  waiting for transfers between devices  314 us (57%)
  blocking collectives  153 us (28%)
  matrix products  38.1 us (7%)
  local copies, waits for them, and re-layouts  28.5 us (5%)
  between operations  13.8 us (2%)
    reduce_scatter x2, waiting for transfers between devices, per_device(): lax.psum_scatter((numer, prior), ('zl', 'c'), scatter_dimension=0, tiled=...  146 us
    all_gather x1, blocking collectives, per_device(): owners = lax.all_gather(seq_ids[0], ('x', 'zh', 'y'), axis=0, tiled=True)  75.5 us
    all_gather x1, waiting for transfers between devices, per_device(): lax.all_gather(act_mine.reshape(nj * tok, row_width), 'x', axis=0, tiled=...  71.6 us
    all_gather x1, waiting for transfers between devices, per_device(): grad_all = lax.all_gather(grad_mine, ('zh', 'y'), axis=0, tiled=False)  52.2 us
    all_to_all x1, blocking collectives, per_device(): act_mine = lax.all_to_all(act_blocks, ('zh', 'y'), 0, 0, tiled=True)  50.4 us
    all_gather x1, waiting for transfers between devices, per_device(): return lax.all_gather(merged_q, ('zl', 'c'), axis=0, tiled=True)  43.5 us
    dot_general x4, matrix products, part(): lax.dot_general(act_x[x], g, (((0,), (0,)), ((), ())), preferred_element_...  38.1 us
    all_to_all x1, blocking collectives, per_device(): grad_mine = lax.all_to_all(grad_blocks, 'x', 0, 0, tiled=True)  27.5 us
  transfers between devices with their start and end apart: 5, of which 5 were waited for; matrix products, arithmetic and copies ran while one was open for 3% of the time, Pallas kernels for 0%

profile of v2, /device:TPU:1, one launch (start us, length us, event | category | flops | bytes accessed | tf_op | source)
XLA Modules:
  0.0 552.2 jit_solution(17320321717328853505)
XLA Ops:
  6.5 0.0 all-gather.10.cloned.1.call-start
  6.5 3.9 copy.13
  10.4 27.5 %all_to_all.10 = bf16[4,128,1792]{1,2,0:T(8,128)(2,1)S(1)} all-to-all(bf16[4,128,1792]{1,2,0:T(8,128)(2,1)} %bitcast.23), channel_id=1, replica_groups=mesh['zl'=2,'c'=2,'x'=4,'zh'=2,'y'=4] {'x'}, dimensions={0} | all-to-all | bytes 3670016 | tf_op jit(solution)/shard_map/all_to_all | solution.py:127
  37.9 2.6 copy.14
  40.4 0.0 all-gather.10.cloned.1.call-update
  40.5 0.0 all-gather.6.cloned.1.call-start
  40.5 4.1 copy.11
  44.6 50.4 %all_to_all.11 = bf16[8,128,1024]{1,2,0:T(8,128)(2,1)S(1)} all-to-all(bf16[8,128,1024]{1,2,0:T(8,128)(2,1)} %bitcast.22), channel_id=1, replica_groups=mesh['zl'=2,'c'=2,'x'=4,'zh'=2,'y'=4] {'zh','y'}, dimensions={0} | all-to-all | bytes 4194304 | tf_op jit(solution)/shard_map/all_to_all | solution.py:124
  95.0 0.0 copy-start.5
  95.0 2.6 copy.12
  97.6 0.0 all-gather.6.cloned.1.call-update
  97.7 0.0 reduce-scatter.3.cloned.1.call-start
  97.7 0.0 copy-done.5
  97.7 75.5 %all-gather = s32[1,4096]{1,0:T(1,128)S(1)} all-gather(s32[1,128]{1,0:T(1,128)S(1)} %copy-done.5), channel_id=2, replica_groups=mesh['zl'=2,'c'=2,'x'=4,'zh'=2,'y'=4] {'x','zh','y'}, dimensions={1}, use_global_device_ids=true | all-gather | bytes 16896 | tf_op jit(solution)/shard_map/all_gather | solution.py:121
  173.2 0.7 fusion.12
  174.5 52.2 %all-gather.10.cloned.1.call-done = bf16[32,128,1792]{2,1,0:T(8,128)(2,1)} async-done(((bf16[4,128,1792]{2,1,0:T(8,128)(2,1)}), bf16[32,128,1792]{2,1,0:T(8,128)(2,1)}) %all-gather.10.cloned.1.call-update) | async-done | bytes 14680080 | tf_op jit(solution)/shard_map/all_gather | solution.py:128
  226.8 11.3 %fusion.13 = (bf16[8,1,128,1792]{3,2,1,0:T(8,128)(2,1)}, bf16[8,1,128,1792]{3,2,1,0:T(8,128)(2,1)}, bf16[8,1,128,1792]{3,2,1,0:T(8,128)(2,1)}, bf16[8,1,128,1792]{3,2,1,0:T(8,128)(2,1)}) fusion(bf16[8,4,128,1792]{3,2,1,0:T(8,128)(2,1)} %bitcast.20), kind=kLoop, calls=%fused_computation.18 | loop fusion | bytes 29360128 | tf_op jit(solution)/shard_map/slice | solution.py:132
  238.0 71.6 %all-gather.6.cloned.1.call-done = bf16[4096,1024]{1,0:T(8,128)(2,1)} async-done(((bf16[1024,1024]{1,0:T(8,128)(2,1)}), bf16[4096,1024]{1,0:T(8,128)(2,1)}) %all-gather.6.cloned.1.call-update) | async-done | bytes 8388624 | tf_op jit(solution)/shard_map/all_gather | solution.py:125
  309.7 0.0 copy-start.3
  309.7 0.0 copy-start.4
  309.7 9.8 %fusion.10 = f32[1024,1792]{1,0:T(8,128)} fusion(bf16[1024,1792]{1,0:T(8,128)(2,1)} %bitcast.26, bf16[4096,1024]{1,0:T(8,128)(2,1)} %all-gather.6.cloned.1.call-done), kind=kOutput, calls=%fused_computation.13 | convolution fusion | flops 3758096384 | bytes 13107200 | tf_op jit(solution)/shard_map/dot_general | solution.py:133
  319.5 0.0 copy-done.3
  319.5 0.0 copy-done.4
  319.5 0.0 copy-start.2
  319.5 6.2 %fusion.5 = f32[1024,1792]{1,0:T(8,128)} fusion(bf16[1024,1792]{1,0:T(8,128)(2,1)S(1)} %bitcast.25, bf16[4096,1024]{1,0:T(8,128)(2,1)S(1)} %copy-done.4), kind=kOutput, calls=%fused_computation.8 | convolution fusion | flops 3758096384 | bytes 13107200 | tf_op jit(solution)/shard_map/dot_general | solution.py:133
  325.7 0.0 copy-done.2
  325.7 0.0 copy-start
  325.7 0.0 copy-start.1
  325.7 6.2 %fusion.8 = f32[1024,1792]{1,0:T(8,128)} fusion(bf16[1024,1792]{1,0:T(8,128)(2,1)S(1)} %bitcast.24, bf16[4096,1024]{1,0:T(8,128)(2,1)S(1)} %copy-done.4), kind=kOutput, calls=%fused_computation.11 | convolution fusion | flops 3758096384 | bytes 13107200 | tf_op jit(solution)/shard_map/dot_general | solution.py:133
  331.9 0.0 copy-done
  331.9 0.0 copy-done.1
  331.9 16.0 %convert_multiply_fusion = (f32[1024,1792]{1,0:T(8,128)}, f32[1024,1792]{1,0:T(8,128)}) fusion(bf16[1,1024,1792]{2,1,0:T(8,128)(2,1)S(1)} %copy-done.1, f32[1024,1792]{1,0:T(8,128)} %fusion.5, f32[1024,1792]{1,0:T(8,128)} %fusion.10, f32[1024,1792]{1,0:T(8,128)} %fusion.8, bf16[1024,1792]{1,0:T(8,128)(2,1)S(1)} %bitcast.19, ...), kind=kOutput, calls=%fused_computation.7 | convolution fusion | flops 3780116480 | bytes 46137344 | tf_op jit(solution)/shard_map/dot_general | solution.py:133
  347.8 0.0 reduce-scatter.3.cloned.1.call-update
  347.8 0.0 reduce-scatter.5.cloned.1.call-start
  347.9 0.5 reduce-scatter.5.cloned.1.call-update
  348.4 0.0 all-gather.8.cloned.1.call-start
  348.5 71.9 %reduce-scatter.3.cloned.1.call-done = f32[256,1792]{1,0:T(8,128)} async-done(((f32[1024,1792]{1,0:T(8,128)}), f32[256,1792]{1,0:T(8,128)}) %reduce-scatter.3.cloned.1.call-update) | async-done | bytes 1835024 | tf_op jit(solution)/shard_map/reduce_scatter | solution.py:146
  420.3 74.4 %reduce-scatter.5.cloned.1.call-done = f32[256,1792]{1,0:T(8,128)} async-done(((f32[1024,1792]{1,0:T(8,128)}), f32[256,1792]{1,0:T(8,128)}) %reduce-scatter.5.cloned.1.call-update) | async-done | bytes 1835024 | tf_op jit(solution)/shard_map/reduce_scatter | solution.py:146
  494.7 3.2 divide_convert_fusion
  498.0 0.0 all-gather.8.cloned.1.call-update
  498.0 43.5 %all-gather.8.cloned.1.call-done = bf16[1024,1792]{1,0:T(8,128)(2,1)} async-done(((bf16[256,1792]{1,0:T(8,128)(2,1)}), bf16[1024,1792]{1,0:T(8,128)(2,1)}) %all-gather.8.cloned.1.call-update) | async-done | bytes 3670032 | tf_op jit(solution)/shard_map/all_gather | solution.py:148
  541.5 4.1 copy.16
Async XLA Ops:
  6.5 220.2 %all-gather.10.cloned.1.call-start = ((), (), s32[]{:S(2)}) async-start(), calls=%async_computation.8 | async-start | bytes 16515072 | tf_op jit(solution)/shard_map/all_gather | solution.py:128
  40.5 269.2 %all-gather.6.cloned.1.call-start = ((), (), s32[]{:S(2)}) async-start(), calls=%async_computation.4 | async-start | bytes 10485760 | tf_op jit(solution)/shard_map/all_gather | solution.py:125
  95.0 2.7 copy-start.5
  97.7 322.7 %reduce-scatter.3.cloned.1.call-start = ((), (), s32[]{:S(2)}) async-start(), calls=%async_computation.5 | async-start | bytes 9175040 | tf_op jit(solution)/shard_map/reduce_scatter | solution.py:146
  309.7 9.8 %copy-start.3 = (bf16[8,1,128,1792]{3,2,1,0:T(8,128)(2,1)S(1)}, bf16[8,1,128,1792]{3,2,1,0:T(8,128)(2,1)}, u32[]{:S(2)}) copy-start(bf16[8,1,128,1792]{3,2,1,0:T(8,128)(2,1)} %get-tuple-element.6) | copy-start | bytes 11010052
  309.7 9.8 %copy-start.4 = (bf16[4096,1024]{1,0:T(8,128)(2,1)S(1)}, bf16[4096,1024]{1,0:T(8,128)(2,1)}, u32[]{:S(2)}) copy-start(bf16[4096,1024]{1,0:T(8,128)(2,1)} %all-gather.6.cloned.1.call-done) | copy-start | bytes 25165828
  319.5 6.2 %copy-start.2 = (bf16[8,1,128,1792]{3,2,1,0:T(8,128)(2,1)S(1)}, bf16[8,1,128,1792]{3,2,1,0:T(8,128)(2,1)}, u32[]{:S(2)}) copy-start(bf16[8,1,128,1792]{3,2,1,0:T(8,128)(2,1)} %get-tuple-element.7) | copy-start | bytes 11010052
  325.7 6.2 %copy-start = (bf16[8,1,128,1792]{3,2,1,0:T(8,128)(2,1)S(1)}, bf16[8,1,128,1792]{3,2,1,0:T(8,128)(2,1)}, u32[]{:S(2)}) copy-start(bf16[8,1,128,1792]{3,2,1,0:T(8,128)(2,1)} %get-tuple-element.5) | copy-start | bytes 11010052
  325.7 6.2 %copy-start.1 = (bf16[1,1024,1792]{2,1,0:T(8,128)(2,1)S(1)}, bf16[1,1024,1792]{2,1,0:T(8,128)(2,1)}, u32[]{:S(2)}) copy-start(bf16[1,1024,1792]{2,1,0:T(8,128)(2,1)} %param.7) | copy-start | bytes 11010052
  347.8 146.9 %reduce-scatter.5.cloned.1.call-start = ((), (), s32[]{:S(2)}) async-start(), calls=%async_computation.6 | async-start | bytes 9175040 | tf_op jit(solution)/shard_map/reduce_scatter | solution.py:146
  348.4 193.1 %all-gather.8.cloned.1.call-start = ((), (), s32[]{:S(2)}) async-start(), calls=%async_computation.7 | async-start | bytes 4587520 | tf_op jit(solution)/shard_map/all_gather | solution.py:148
Sparse Core Ops, SparseCore 0:
  40.6 186.1 all-gather.9
  228.4 81.1 all-gather.5
  348.0 72.3 reduce-scatter.2
  422.6 72.0 reduce-scatter.4
  498.1 43.3 all-gather.7

commit v3 on v2

--- a/solution.py
+++ b/solution.py
@@ -143,9 +143,12 @@
     fisher = g0 * g0 + g1 * g1
     prior = fisher / SEQS + smoothing
     numer = prior * weights[0].astype(jnp.float32)
-    numer_q, denom_q = lax.psum_scatter((numer, prior), ("zl", "c"), scatter_dimension=0, tiled=True)
-    merged_q = (numer_q / denom_q).astype(jnp.bfloat16)
-    return lax.all_gather(merged_q, ("zl", "c"), axis=0, tiled=True)
+    both = jnp.stack([numer, prior], axis=0)
+    both = lax.psum_scatter(both, "c", scatter_dimension=1, tiled=True)
+    both = lax.psum_scatter(both, "zl", scatter_dimension=1, tiled=True)
+    merged_q = (both[0] / both[1]).astype(jnp.bfloat16)
+    merged_h = lax.all_gather(merged_q, "zl", axis=0, tiled=True)
+    return lax.all_gather(merged_h, "c", axis=0, tiled=True)
 
 
 def solution(mesh):

time: 553 us -> 551 us (level)
  other arithmetic: 3.88 us -> 19.3 us
  waiting for transfers between devices: 314 us -> 299 us
    reduce_scatter x2, waiting for transfers between devices: 146 us -> 122 us  [the longest x1 94.2 us: per_device(): both = lax.psum_scatter(both, 'zl', scatter_dimension=1, tiled=True)]
    another operation x0 -> x2, other arithmetic: none -> 15.4 us  [per_device(): both = jnp.stack([numer, prior], axis=0)]
    all_gather x1 -> x2, waiting for transfers between devices: 43.5 us -> 52.5 us  [the longest x1 33.8 us: per_device(): merged_h = lax.all_gather(merged_q, 'zl', axis=0, tiled=True)]
    unnamed x15 -> x17, local copies, waits for them, and re-layouts: 12.1 us -> 13.2 us
  transfers between devices with their start and end apart: 5 -> 6, of which waited for: 5 -> 6; matrix products, arithmetic and copies ran while one was open for 3% -> 3% of each run, Pallas kernels for 0% -> 0%
where the time goes in v3:
time: 551 us; the launch traced here: 550 us
  waiting for transfers between devices  299 us (54%)
  blocking collectives  153 us (28%)
  matrix products  34.8 us (6%)
  local copies, waits for them, and re-layouts  29.6 us (5%)
  other arithmetic  19.3 us (4%)
  between operations  14.2 us (3%)
    reduce_scatter x1, waiting for transfers between devices, per_device(): both = lax.psum_scatter(both, 'zl', scatter_dimension=1, tiled=True)  94.2 us
    all_gather x1, blocking collectives, per_device(): owners = lax.all_gather(seq_ids[0], ('x', 'zh', 'y'), axis=0, tiled=True)  75.5 us
    all_gather x1, waiting for transfers between devices, per_device(): lax.all_gather(act_mine.reshape(nj * tok, row_width), 'x', axis=0, tiled=...  71.6 us
    all_gather x1, waiting for transfers between devices, per_device(): grad_all = lax.all_gather(grad_mine, ('zh', 'y'), axis=0, tiled=False)  52.2 us
    all_to_all x1, blocking collectives, per_device(): act_mine = lax.all_to_all(act_blocks, ('zh', 'y'), 0, 0, tiled=True)  50.4 us
    dot_general x4, matrix products, part(): lax.dot_general(act_x[x], g, (((0,), (0,)), ((), ())), preferred_element_...  34.8 us
    all_gather x1, waiting for transfers between devices, per_device(): merged_h = lax.all_gather(merged_q, 'zl', axis=0, tiled=True)  33.8 us
    reduce_scatter x1, waiting for transfers between devices, per_device(): both = lax.psum_scatter(both, 'c', scatter_dimension=1, tiled=True)  28.1 us
  transfers between devices with their start and end apart: 6, of which 6 were waited for; matrix products, arithmetic and copies ran while one was open for 3% of the time, Pallas kernels for 0%

profile of v3, /device:TPU:1, one launch (start us, length us, event | category | flops | bytes accessed | tf_op | source)
XLA Modules:
  0.0 550.3 jit_solution(9236500321865410628)
XLA Ops:
  6.5 0.0 all-gather.11.cloned.1.call-start
  6.5 3.9 copy.13
  10.4 27.5 %all_to_all.10 = bf16[4,128,1792]{1,2,0:T(8,128)(2,1)S(1)} all-to-all(bf16[4,128,1792]{1,2,0:T(8,128)(2,1)} %bitcast.27), channel_id=1, replica_groups=mesh['zl'=2,'c'=2,'x'=4,'zh'=2,'y'=4] {'x'}, dimensions={0} | all-to-all | bytes 3670016 | tf_op jit(solution)/shard_map/all_to_all | solution.py:127
  37.9 2.6 copy.14
  40.5 0.0 all-gather.11.cloned.1.call-update
  40.5 0.0 all-gather.9.cloned.1.call-start
  40.5 4.1 copy.11
  44.6 50.4 %all_to_all.11 = bf16[8,128,1024]{1,2,0:T(8,128)(2,1)S(1)} all-to-all(bf16[8,128,1024]{1,2,0:T(8,128)(2,1)} %bitcast.26), channel_id=1, replica_groups=mesh['zl'=2,'c'=2,'x'=4,'zh'=2,'y'=4] {'zh','y'}, dimensions={0} | all-to-all | bytes 4194304 | tf_op jit(solution)/shard_map/all_to_all | solution.py:124
  95.0 0.0 copy-start.5
  95.0 2.6 copy.12
  97.6 0.0 all-gather.9.cloned.1.call-update
  97.7 0.0 reduce-scatter.3.cloned.1.call-start
  97.7 0.0 copy-done.5
  97.7 75.5 %all-gather = s32[1,4096]{1,0:T(1,128)S(1)} all-gather(s32[1,128]{1,0:T(1,128)S(1)} %copy-done.5), channel_id=2, replica_groups=mesh['zl'=2,'c'=2,'x'=4,'zh'=2,'y'=4] {'x','zh','y'}, dimensions={1}, use_global_device_ids=true | all-gather | bytes 16896 | tf_op jit(solution)/shard_map/all_gather | solution.py:121
  173.2 0.7 fusion.14
  174.5 52.2 %all-gather.11.cloned.1.call-done = bf16[32,128,1792]{2,1,0:T(8,128)(2,1)} async-done(((bf16[4,128,1792]{2,1,0:T(8,128)(2,1)}), bf16[32,128,1792]{2,1,0:T(8,128)(2,1)}) %all-gather.11.cloned.1.call-update) | async-done | bytes 14680080 | tf_op jit(solution)/shard_map/all_gather | solution.py:128
  226.8 11.3 %fusion.15 = (bf16[8,1,128,1792]{3,2,1,0:T(8,128)(2,1)}, bf16[8,1,128,1792]{3,2,1,0:T(8,128)(2,1)}, bf16[8,1,128,1792]{3,2,1,0:T(8,128)(2,1)}, bf16[8,1,128,1792]{3,2,1,0:T(8,128)(2,1)}) fusion(bf16[8,4,128,1792]{3,2,1,0:T(8,128)(2,1)} %bitcast.24), kind=kLoop, calls=%fused_computation.21 | loop fusion | bytes 29360128 | tf_op jit(solution)/shard_map/slice | solution.py:132
  238.0 71.6 %all-gather.9.cloned.1.call-done = bf16[4096,1024]{1,0:T(8,128)(2,1)} async-done(((bf16[1024,1024]{1,0:T(8,128)(2,1)}), bf16[4096,1024]{1,0:T(8,128)(2,1)}) %all-gather.9.cloned.1.call-update) | async-done | bytes 8388624 | tf_op jit(solution)/shard_map/all_gather | solution.py:125
  309.7 0.0 copy-start.3
  309.7 0.0 copy-start.6
  309.7 9.8 %fusion.11 = f32[1024,1792]{1,0:T(8,128)} fusion(bf16[1024,1792]{1,0:T(8,128)(2,1)} %bitcast.31, bf16[4096,1024]{1,0:T(8,128)(2,1)} %all-gather.9.cloned.1.call-done), kind=kOutput, calls=%fused_computation.15 | convolution fusion | flops 3758096384 | bytes 13107200 | tf_op jit(solution)/shard_map/dot_general | solution.py:133
  319.5 0.0 copy-done.3
  319.5 0.0 copy-done.6
  319.5 0.0 copy-start.2
  319.5 6.2 %fusion.6 = f32[1024,1792]{1,0:T(8,128)} fusion(bf16[1024,1792]{1,0:T(8,128)(2,1)S(1)} %bitcast.30, bf16[4096,1024]{1,0:T(8,128)(2,1)S(1)} %copy-done.6), kind=kOutput, calls=%fused_computation.10 | convolution fusion | flops 3758096384 | bytes 13107200 | tf_op jit(solution)/shard_map/dot_general | solution.py:133
  325.7 0.0 copy-done.2
  325.7 0.0 copy-start.1
  325.7 6.2 %fusion.9 = f32[1024,1792]{1,0:T(8,128)} fusion(bf16[1024,1792]{1,0:T(8,128)(2,1)S(1)} %bitcast.29, bf16[4096,1024]{1,0:T(8,128)(2,1)S(1)} %copy-done.6), kind=kOutput, calls=%fused_computation.13 | convolution fusion | flops 3758096384 | bytes 13107200 | tf_op jit(solution)/shard_map/dot_general | solution.py:133
  331.9 0.0 copy-done.1
  331.9 12.7 %fusion.3 = f32[1024,1792]{1,0:T(8,128)S(1)} fusion(f32[1024,1792]{1,0:T(8,128)} %fusion.11, f32[1024,1792]{1,0:T(8,128)} %fusion.6, f32[1024,1792]{1,0:T(8,128)} %fusion.9, bf16[1024,1792]{1,0:T(8,128)(2,1)S(1)} %bitcast.28, pred[]{:T(512)S(6)} %gt.3, bf16[4096,1024]{1,0:T(8,128)(2,1)} %all-gather.9.cloned.1.call-done), kind=kOutput, calls=%fused_computation.6 | convolution fusion | flops 3776446464 | bytes 35127296 | tf_op jit(solution)/shard_map/dot_general | solution.py:133
  344.6 0.0 copy-done.4
  344.6 0.0 copy-start
  344.6 4.1 fusion.5
  348.6 1.1 copy-done
  349.7 11.3 %pad_maximum_fusion = f32[2,1024,1792]{2,1,0:T(8,128)} fusion(f32[1,1024,1792]{2,1,0:T(8,128)} %bitcast.23, f32[1,1024,1792]{2,1,0:T(8,128)} %fusion.5), kind=kLoop, calls=%fused_computation | loop fusion | flops 3670016 | bytes 29360128 | tf_op jit(solution)/shard_map/stack | solution.py:146
  361.0 0.0 reduce-scatter.3.cloned.1.call-update
  361.1 0.0 reduce-scatter.5.cloned.1.call-start
  361.1 28.1 %reduce-scatter.3.cloned.1.call-done = f32[2,512,1792]{2,1,0:T(8,128)} async-done(((f32[2,1024,1792]{2,1,0:T(8,128)}), f32[2,512,1792]{2,1,0:T(8,128)}) %reduce-scatter.3.cloned.1.call-update) | async-done | bytes 7340048 | tf_op jit(solution)/shard_map/reduce_scatter | solution.py:147
  389.2 0.0 reduce-scatter.5.cloned.1.call-update
  389.2 0.0 all-gather.13.cloned.1.call-start
  389.3 94.2 %reduce-scatter.5.cloned.1.call-done = f32[2,256,1792]{2,1,0:T(8,128)} async-done(((f32[2,512,1792]{2,1,0:T(8,128)}), f32[2,256,1792]{2,1,0:T(8,128)}) %reduce-scatter.5.cloned.1.call-update) | async-done | bytes 3670032 | tf_op jit(solution)/shard_map/reduce_scatter | solution.py:148
  483.5 3.2 fusion.13
  486.7 0.0 all-gather.13.cloned.1.call-update
  486.8 0.0 all-gather.15.cloned.1.call-start
  486.8 33.8 %all-gather.13.cloned.1.call-done = bf16[1,512,1792]{2,1,0:T(8,128)(2,1)} async-done(((bf16[1,256,1792]{2,1,0:T(8,128)(2,1)}), bf16[1,512,1792]{2,1,0:T(8,128)(2,1)}) %all-gather.13.cloned.1.call-update) | async-done | bytes 1835024 | tf_op jit(solution)/shard_map/all_gather | solution.py:150
  520.6 0.0 all-gather.15.cloned.1.call-update
  520.7 18.6 %all-gather.15.cloned.1.call-done = bf16[1,1024,1792]{2,1,0:T(8,128)(2,1)} async-done(((bf16[1,512,1792]{2,1,0:T(8,128)(2,1)}), bf16[1,1024,1792]{2,1,0:T(8,128)(2,1)}) %all-gather.15.cloned.1.call-update) | async-done | bytes 3670032 | tf_op jit(solution)/shard_map/all_gather | solution.py:151
  539.3 4.1 copy.16
  (1 shorter events, 0.0 us)
Async XLA Ops:
  6.5 220.2 %all-gather.11.cloned.1.call-start = ((), (), s32[]{:S(2)}) async-start(), calls=%async_computation.7 | async-start | bytes 16515072 | tf_op jit(solution)/shard_map/all_gather | solution.py:128
  40.5 269.2 %all-gather.9.cloned.1.call-start = ((), (), s32[]{:S(2)}) async-start(), calls=%async_computation.4 | async-start | bytes 10485760 | tf_op jit(solution)/shard_map/all_gather | solution.py:125
  95.0 2.7 copy-start.5
  97.7 291.5 %reduce-scatter.3.cloned.1.call-start = ((), (), s32[]{:S(2)}) async-start(), calls=%async_computation.5 | async-start | bytes 22020096 | tf_op jit(solution)/shard_map/reduce_scatter | solution.py:147
  309.7 9.8 %copy-start.3 = (bf16[8,1,128,1792]{3,2,1,0:T(8,128)(2,1)S(1)}, bf16[8,1,128,1792]{3,2,1,0:T(8,128)(2,1)}, u32[]{:S(2)}) copy-start(bf16[8,1,128,1792]{3,2,1,0:T(8,128)(2,1)} %get-tuple-element.6) | copy-start | bytes 11010052
  309.7 9.8 %copy-start.6 = (bf16[4096,1024]{1,0:T(8,128)(2,1)S(1)}, bf16[4096,1024]{1,0:T(8,128)(2,1)}, u32[]{:S(2)}) copy-start(bf16[4096,1024]{1,0:T(8,128)(2,1)} %all-gather.9.cloned.1.call-done) | copy-start | bytes 25165828
  319.5 6.2 %copy-start.2 = (bf16[8,1,128,1792]{3,2,1,0:T(8,128)(2,1)S(1)}, bf16[8,1,128,1792]{3,2,1,0:T(8,128)(2,1)}, u32[]{:S(2)}) copy-start(bf16[8,1,128,1792]{3,2,1,0:T(8,128)(2,1)} %get-tuple-element.7) | copy-start | bytes 11010052
  325.7 6.2 %copy-start.1 = (bf16[8,1,128,1792]{3,2,1,0:T(8,128)(2,1)S(1)}, bf16[8,1,128,1792]{3,2,1,0:T(8,128)(2,1)}, u32[]{:S(2)}) copy-start(bf16[8,1,128,1792]{3,2,1,0:T(8,128)(2,1)} %get-tuple-element.5) | copy-start | bytes 11010052
  331.9 12.7 %copy-start.4 = (bf16[1,1024,1792]{2,1,0:T(8,128)(2,1)S(1)}, bf16[1,1024,1792]{2,1,0:T(8,128)(2,1)}, u32[]{:S(2)}) copy-start(bf16[1,1024,1792]{2,1,0:T(8,128)(2,1)} %param.7) | copy-start | bytes 11010052
  344.6 5.2 copy-start
  361.1 122.5 %reduce-scatter.5.cloned.1.call-start = ((), (), s32[]{:S(2)}) async-start(), calls=%async_computation.6 | async-start | bytes 11010048 | tf_op jit(solution)/shard_map/reduce_scatter | solution.py:148
  389.2 131.4 %all-gather.13.cloned.1.call-start = ((), (), s32[]{:S(2)}) async-start(), calls=%async_computation.8 | async-start | bytes 2752512 | tf_op jit(solution)/shard_map/all_gather | solution.py:150
  486.8 52.5 %all-gather.15.cloned.1.call-start = ((), (), s32[]{:S(2)}) async-start(), calls=%async_computation.9 | async-start | bytes 5505024 | tf_op jit(solution)/shard_map/all_gather | solution.py:151
Sparse Core Ops, SparseCore 0:
  40.6 186.1 all-gather.10
  228.4 81.1 all-gather.8
  361.2 27.9 reduce-scatter.2
  391.5 92.0 reduce-scatter.4
  486.9 33.7 all-gather.12
  522.3 16.9 all-gather.14

commit v4 on v3

--- a/solution.py
+++ b/solution.py
@@ -112,6 +112,82 @@
     )(act, grad)
 
 
+def xgather_kernel(act_ref, act_out, send_sem, recv_sem, local_sem):
+    n = lax.axis_size("x")
+    me = lax.axis_index("x")
+    right, left = lax.rem(me + 1, n), lax.rem(me + n - 1, n)
+    far = lax.rem(me + 2, n)
+    rows = act_ref.shape[0]
+    half = rows // 2
+
+    barrier = pltpu.get_barrier_semaphore()
+    for nb in (left, right):
+        pl.semaphore_signal(barrier, 1, device_id={"x": nb}, device_id_type=MESH)
+    pl.semaphore_wait(barrier, 2)
+
+    own = pltpu.make_async_copy(act_ref, act_out.at[me], local_sem.at[0])
+    own.start()
+    to_right = pltpu.make_async_remote_copy(
+        src_ref=act_ref, dst_ref=act_out.at[me], send_sem=send_sem.at[0],
+        recv_sem=recv_sem.at[0], device_id={"x": right}, device_id_type=MESH)
+    to_left = pltpu.make_async_remote_copy(
+        src_ref=act_ref, dst_ref=act_out.at[me], send_sem=send_sem.at[1],
+        recv_sem=recv_sem.at[1], device_id={"x": left}, device_id_type=MESH)
+    to_right.start()
+    to_left.start()
+    from_left = pltpu.make_async_remote_copy(
+        src_ref=act_ref, dst_ref=act_out.at[left], send_sem=send_sem.at[0],
+        recv_sem=recv_sem.at[0], device_id={"x": left}, device_id_type=MESH)
+    from_right = pltpu.make_async_remote_copy(
+        src_ref=act_ref, dst_ref=act_out.at[right], send_sem=send_sem.at[1],
+        recv_sem=recv_sem.at[1], device_id={"x": right}, device_id_type=MESH)
+    from_left.wait_recv()
+    from_right.wait_recv()
+    relay_left = pltpu.make_async_remote_copy(
+        src_ref=act_out.at[right, pl.ds(0, half)], dst_ref=act_out.at[right, pl.ds(0, half)],
+        send_sem=send_sem.at[2], recv_sem=recv_sem.at[2], device_id={"x": left},
+        device_id_type=MESH)
+    relay_right = pltpu.make_async_remote_copy(
+        src_ref=act_out.at[left, pl.ds(half, half)], dst_ref=act_out.at[left, pl.ds(half, half)],
+        send_sem=send_sem.at[3], recv_sem=recv_sem.at[3], device_id={"x": right},
+        device_id_type=MESH)
+    relay_left.start()
+    relay_right.start()
+    far_first = pltpu.make_async_remote_copy(
+        src_ref=act_out.at[far, pl.ds(0, half)], dst_ref=act_out.at[far, pl.ds(0, half)],
+        send_sem=send_sem.at[2], recv_sem=recv_sem.at[2], device_id={"x": right},
+        device_id_type=MESH)
+    far_second = pltpu.make_async_remote_copy(
+        src_ref=act_out.at[far, pl.ds(half, half)], dst_ref=act_out.at[far, pl.ds(half, half)],
+        send_sem=send_sem.at[3], recv_sem=recv_sem.at[3], device_id={"x": left},
+        device_id_type=MESH)
+    far_first.wait_recv()
+    far_second.wait_recv()
+    to_right.wait_send()
+    to_left.wait_send()
+    relay_left.wait_send()
+    relay_right.wait_send()
+    own.wait()
+
+
+def xgather(act):
+    n = 4
+    rows, cols = act.shape
+    return pl.pallas_call(
+        xgather_kernel,
+        out_shape=jax.ShapeDtypeStruct((n, rows, cols), act.dtype),
+        in_specs=[pl.BlockSpec(memory_space=pl.ANY)],
+        out_specs=pl.BlockSpec(memory_space=pl.ANY),
+        scratch_shapes=[
+            pltpu.SemaphoreType.DMA((4,)),
+            pltpu.SemaphoreType.DMA((4,)),
+            pltpu.SemaphoreType.DMA((1,)),
+        ],
+        compiler_params=pltpu.CompilerParams(collective_id=1, has_side_effects=True),
+        cost_estimate=pl.CostEstimate(flops=0, bytes_accessed=8 * rows * cols * 2, transcendentals=0),
+    )(act)
+
+
 def per_device(activations, out_grads, seq_ids, weights):
     nx = lax.axis_size("x")
     nj = lax.axis_size(("zh", "y"))
@@ -122,11 +198,11 @@
     total = owners.shape[0]
     act_blocks = activations[0].reshape(tok, nj, row_width).transpose(1, 0, 2)
     act_mine = lax.all_to_all(act_blocks, ("zh", "y"), 0, 0, tiled=True)
-    act_all = lax.all_gather(act_mine.reshape(nj * tok, row_width), "x", axis=0, tiled=True)
+    act_all = xgather(act_mine.reshape(nj * tok, row_width))
     grad_blocks = out_grads[0].reshape(tok, nx, col_width).transpose(1, 0, 2)
     grad_mine = lax.all_to_all(grad_blocks, "x", 0, 0, tiled=True)
     grad_all = lax.all_gather(grad_mine, ("zh", "y"), axis=0, tiled=False)
-    act_x = act_all.reshape(nx, nj * tok, row_width)
+    act_x = act_all
 
     def part(x):
         g = grad_all[:, x].reshape(nj * tok, col_width)

time: 551 us -> 493 us (0.89)
  waiting for transfers between devices: 299 us -> 189 us
  Pallas kernels: 0 us -> 64.7 us
  blocking collectives: 153 us -> 136 us
  starting transfers between devices: 0.21 us -> 7.66 us
    all_gather x1 -> x0, waiting for transfers between devices: 71.6 us -> none  [per_device(): lax.all_gather(act_mine.reshape(nj * tok, row_width), 'x', axis=0, tiled=...]
    pallas_call x0 -> x1, Pallas kernels: none -> 64.7 us  [xgather(): pl.pallas_call(xgather_kernel, out_shape=jax.ShapeDtypeStruct((n, rows, c...]
    all_gather x1, waiting for transfers between devices: 52.2 us -> 0.02 us  [per_device(): grad_all = lax.all_gather(grad_mine, ('zh', 'y'), axis=0, tiled=False)]
    all_to_all x1 -> x0, blocking collectives: 50.4 us -> none  [per_device(): act_mine = lax.all_to_all(act_blocks, ('zh', 'y'), 0, 0, tiled=True)]
    all_gather x1, blocking collectives: 75.5 us -> 109 us  [per_device(): owners = lax.all_gather(seq_ids[0], ('x', 'zh', 'y'), axis=0, tiled=True)]
    reduce_scatter x1, waiting for transfers between devices: 28.1 us -> 42.4 us  [per_device(): both = lax.psum_scatter(both, 'c', scatter_dimension=1, tiled=True)]
    all_to_all x0 -> x1, starting transfers between devices: none -> 7.5 us  [per_device(): act_mine = lax.all_to_all(act_blocks, ('zh', 'y'), 0, 0, tiled=True)]
    unnamed x17 -> x11, local copies, waits for them, and re-layouts: 13.2 us -> 13.5 us
  transfers between devices with their start and end apart: 6 -> 6, of which waited for: 6 -> 4; matrix products, arithmetic and copies ran while one was open for 3% -> 1% of each run, Pallas kernels for 0% -> 13%
where the time goes in v4:
time: 493 us
  waiting for transfers between devices  189 us (38%)
  blocking collectives  136 us (28%)
  Pallas kernels  64.7 us (13%)
  matrix products  31.1 us (6%)
  local copies, waits for them, and re-layouts  26.2 us (5%)
  other arithmetic  23.8 us (5%)
  between operations  13.9 us (3%)
  starting transfers between devices  7.66 us (2%)
    all_gather x1, blocking collectives, per_device(): owners = lax.all_gather(seq_ids[0], ('x', 'zh', 'y'), axis=0, tiled=True)  109 us
    reduce_scatter x1, waiting for transfers between devices, per_device(): both = lax.psum_scatter(both, 'zl', scatter_dimension=1, tiled=True)  94.4 us
    pallas_call x1, Pallas kernels, xgather(): pl.pallas_call(xgather_kernel, out_shape=jax.ShapeDtypeStruct((n, rows, c...  64.7 us
    reduce_scatter x1, waiting for transfers between devices, per_device(): both = lax.psum_scatter(both, 'c', scatter_dimension=1, tiled=True)  42.4 us
    all_gather x1, waiting for transfers between devices, per_device(): merged_h = lax.all_gather(merged_q, 'zl', axis=0, tiled=True)  33.8 us
    dot_general x4, matrix products, part(): lax.dot_general(act_x[x], g, (((0,), (0,)), ((), ())), preferred_element_...  31.1 us
    all_to_all x1, blocking collectives, per_device(): grad_mine = lax.all_to_all(grad_blocks, 'x', 0, 0, tiled=True)  27.5 us
    another operation x2, other arithmetic, per_device(): both = jnp.stack([numer, prior], axis=0)  19.9 us
  transfers between devices with their start and end apart: 6, of which 4 were waited for; matrix products, arithmetic and copies ran while one was open for 1% of the time, Pallas kernels for 13%

profile of v4, /device:TPU:1, one launch (start us, length us, event | category | flops | bytes accessed | tf_op | source)
XLA Modules:
  0.0 492.8 jit_solution(12065253957623430212)
XLA Ops:
  6.5 0.0 all-gather.8.cloned.1.call-start
  6.5 3.9 copy.12
  10.4 27.5 %all_to_all.10 = bf16[4,128,1792]{1,2,0:T(8,128)(2,1)S(1)} all-to-all(bf16[4,128,1792]{1,2,0:T(8,128)(2,1)} %bitcast.43), channel_id=1, replica_groups=mesh['zl'=2,'c'=2,'x'=4,'zh'=2,'y'=4] {'x'}, dimensions={0} | all-to-all | bytes 3670016 | tf_op jit(solution)/shard_map/all_to_all | solution.py:203
  37.9 2.5 copy.13
  40.4 0.0 all-gather.8.cloned.1.call-update
  40.4 3.0 copy.14
  43.4 0.0 copy-start.3
  43.4 2.5 copy.16
  45.9 7.5 %all-to-all-start = ((bf16[8,128,1024]{2,1,0:T(8,128)(2,1)}), bf16[8,128,1024]{2,1,0:T(8,128)(2,1)S(1)}, u32[]{:S(2)}, u32[]{:S(2)}) async-start(bf16[8,128,1024]{2,1,0:T(8,128)(2,1)} %bitcast.41), calls=%async_computation | async-start | bytes 4194304 | tf_op jit(solution)/shard_map/all_to_all | solution.py:200
  53.4 0.0 reduce-scatter.3.cloned.1.call-start
  53.4 0.0 copy-done.3
  53.4 108.6 %all-gather = s32[1,4096]{1,0:T(1,128)S(1)} all-gather(s32[1,128]{1,0:T(1,128)S(1)} %copy-done.3), channel_id=2, replica_groups=mesh['zl'=2,'c'=2,'x'=4,'zh'=2,'y'=4] {'x','zh','y'}, dimensions={1}, use_global_device_ids=true | all-gather | bytes 16896 | tf_op jit(solution)/shard_map/all_gather | solution.py:197
  162.0 0.7 fusion.18
  163.4 0.0 all-to-all-done
  163.4 0.0 copy-start.2
  163.4 1.3 copy-done.2
  164.7 64.7 %shard_map.46 = bf16[4,1024,1024]{2,1,0:T(8,128)(2,1)} custom-call(bf16[1024,1024]{1,0:T(8,128)(2,1)} %bitcast.40), custom_call_target="tpu_custom_call" | custom-call | bytes 16777216 | tf_op jit(solution)/shard_map/pallas_call | solution.py:176
  229.4 0.0 all-gather.8.cloned.1.call-done
  229.5 0.0 copy-start.1
  229.5 7.8 %fusion.19 = (bf16[8,1,128,1792]{3,2,1,0:T(8,128)(2,1)}, bf16[8,1,128,1792]{3,2,1,0:T(8,128)(2,1)S(1)}, bf16[8,1,128,1792]{3,2,1,0:T(8,128)(2,1)S(1)}, bf16[8,1,128,1792]{3,2,1,0:T(8,128)(2,1)S(1)}) fusion(bf16[8,4,128,1792]{3,2,1,0:T(8,128)(2,1)} %bitcast.39), kind=kLoop, calls=%fused_computation.26 | loop fusion | bytes 29360128 | tf_op jit(solution)/shard_map/slice | solution.py:208
  237.3 1.2 copy-done.1
  238.4 6.2 %fusion.11 = f32[1024,1792]{1,0:T(8,128)} fusion(bf16[1024,1792]{1,0:T(8,128)(2,1)S(1)} %bitcast.47, bf16[4,1024,1024]{2,1,0:T(8,128)(2,1)S(1)} %copy-done.1), kind=kOutput, calls=%fused_computation.15 | convolution fusion | flops 3758096384 | bytes 13107200 | tf_op jit(solution)/shard_map/dot_general | solution.py:209
  244.6 6.2 %fusion.6 = f32[1024,1792]{1,0:T(8,128)} fusion(bf16[1024,1792]{1,0:T(8,128)(2,1)S(1)} %bitcast.46, bf16[4,1024,1024]{2,1,0:T(8,128)(2,1)S(1)} %copy-done.1), kind=kOutput, calls=%fused_computation.10 | convolution fusion | flops 3758096384 | bytes 13107200 | tf_op jit(solution)/shard_map/dot_general | solution.py:209
  250.8 6.2 %fusion.9 = f32[1024,1792]{1,0:T(8,128)} fusion(bf16[1024,1792]{1,0:T(8,128)(2,1)S(1)} %bitcast.45, bf16[4,1024,1024]{2,1,0:T(8,128)(2,1)S(1)} %copy-done.1), kind=kOutput, calls=%fused_computation.13 | convolution fusion | flops 3758096384 | bytes 13107200 | tf_op jit(solution)/shard_map/dot_general | solution.py:209
  257.0 12.6 %fusion.3 = f32[1024,1792]{1,0:T(8,128)S(1)} fusion(f32[1024,1792]{1,0:T(8,128)} %fusion.11, f32[1024,1792]{1,0:T(8,128)} %fusion.6, f32[1024,1792]{1,0:T(8,128)} %fusion.9, bf16[1024,1792]{1,0:T(8,128)(2,1)} %bitcast.44, pred[]{:T(512)S(6)} %gt.3, bf16[4,1024,1024]{2,1,0:T(8,128)(2,1)S(1)} %copy-done.1), kind=kOutput, calls=%fused_computation.6 | convolution fusion | flops 3776446464 | bytes 35127296 | tf_op jit(solution)/shard_map/dot_general | solution.py:209
  269.6 0.0 copy-start
  269.6 8.6 %fusion.5 = f32[1,1024,1792]{2,1,0:T(8,128)} fusion(f32[1024,1792]{1,0:T(8,128)S(1)} %fusion.3, bf16[1,1024,1792]{2,1,0:T(8,128)(2,1)} %param.7), kind=kLoop, calls=%fused_computation.9 | loop fusion | flops 3670016 | bytes 18350080 | tf_op jit(solution)/shard_map/stack | solution.py:222
  278.1 0.0 copy-done
  278.2 11.3 %pad_maximum_fusion = f32[2,1024,1792]{2,1,0:T(8,128)} fusion(f32[1,1024,1792]{2,1,0:T(8,128)} %bitcast.38, f32[1,1024,1792]{2,1,0:T(8,128)} %fusion.5), kind=kLoop, calls=%fused_computation | loop fusion | flops 3670016 | bytes 29360128 | tf_op jit(solution)/shard_map/stack | solution.py:222
  289.5 0.0 reduce-scatter.3.cloned.1.call-update
  289.5 0.0 reduce-scatter.5.cloned.1.call-start
  289.5 42.4 %reduce-scatter.3.cloned.1.call-done = f32[2,512,1792]{2,1,0:T(8,128)} async-done(((f32[2,1024,1792]{2,1,0:T(8,128)}), f32[2,512,1792]{2,1,0:T(8,128)}) %reduce-scatter.3.cloned.1.call-update) | async-done | bytes 7340048 | tf_op jit(solution)/shard_map/reduce_scatter | solution.py:223
  331.9 0.0 reduce-scatter.5.cloned.1.call-update
  331.9 0.0 all-gather.10.cloned.1.call-start
  332.0 94.4 %reduce-scatter.5.cloned.1.call-done = f32[2,256,1792]{2,1,0:T(8,128)} async-done(((f32[2,512,1792]{2,1,0:T(8,128)}), f32[2,256,1792]{2,1,0:T(8,128)}) %reduce-scatter.5.cloned.1.call-update) | async-done | bytes 3670032 | tf_op jit(solution)/shard_map/reduce_scatter | solution.py:224
  426.4 3.2 fusion.17
  429.6 0.0 all-gather.10.cloned.1.call-update
  429.6 0.0 all-gather.12.cloned.1.call-start
  429.7 33.8 %all-gather.10.cloned.1.call-done = bf16[1,512,1792]{2,1,0:T(8,128)(2,1)} async-done(((bf16[1,256,1792]{2,1,0:T(8,128)(2,1)}), bf16[1,512,1792]{2,1,0:T(8,128)(2,1)}) %all-gather.10.cloned.1.call-update) | async-done | bytes 1835024 | tf_op jit(solution)/shard_map/all_gather | solution.py:226
  463.5 0.0 all-gather.12.cloned.1.call-update
  463.5 18.6 %all-gather.12.cloned.1.call-done = bf16[1,1024,1792]{2,1,0:T(8,128)(2,1)} async-done(((bf16[1,512,1792]{2,1,0:T(8,128)(2,1)}), bf16[1,1024,1792]{2,1,0:T(8,128)(2,1)}) %all-gather.12.cloned.1.call-update) | async-done | bytes 3670032 | tf_op jit(solution)/shard_map/all_gather | solution.py:227
  482.2 4.1 copy.18
Async XLA Ops:
  6.5 222.9 %all-gather.8.cloned.1.call-start = ((), (), s32[]{:S(2)}) async-start(), calls=%async_computation.6 | async-start | bytes 16515072 | tf_op jit(solution)/shard_map/all_gather | solution.py:204
  43.4 10.0 %copy-start.3 = (s32[1,128]{1,0:T(1,128)S(1)}, s32[1,128]{1,0:T(1,128)}, u32[]{:S(2)}) copy-start(s32[1,128]{1,0:T(1,128)} %param.6) | copy-start | bytes 1540
  45.9 117.5 %all-to-all-start = ((bf16[8,128,1024]{2,1,0:T(8,128)(2,1)}), bf16[8,128,1024]{2,1,0:T(8,128)(2,1)S(1)}, u32[]{:S(2)}, u32[]{:S(2)}) async-start(bf16[8,128,1024]{2,1,0:T(8,128)(2,1)} %bitcast.41), calls=%async_computation | async-start | bytes 4194304 | tf_op jit(solution)/shard_map/all_to_all | solution.py:200
  53.4 278.5 %reduce-scatter.3.cloned.1.call-start = ((), (), s32[]{:S(2)}) async-start(), calls=%async_computation.4 | async-start | bytes 22020096 | tf_op jit(solution)/shard_map/reduce_scatter | solution.py:223
  163.4 1.3 copy-start.2
  229.5 9.0 %copy-start.1 = (bf16[4,1024,1024]{2,1,0:T(8,128)(2,1)S(1)}, bf16[4,1024,1024]{2,1,0:T(8,128)(2,1)}, u32[]{:S(2)}) copy-start(bf16[4,1024,1024]{2,1,0:T(8,128)(2,1)} %shard_map.46) | copy-start | bytes 25165828
  269.6 8.6 %copy-start = (f32[1024,1792]{1,0:T(8,128)}, f32[1024,1792]{1,0:T(8,128)S(1)}, u32[]{:S(2)}) copy-start(f32[1024,1792]{1,0:T(8,128)S(1)} %fusion.3) | copy-start | bytes 22020100
  289.5 136.9 %reduce-scatter.5.cloned.1.call-start = ((), (), s32[]{:S(2)}) async-start(), calls=%async_computation.5 | async-start | bytes 11010048 | tf_op jit(solution)/shard_map/reduce_scatter | solution.py:224
  331.9 131.6 %all-gather.10.cloned.1.call-start = ((), (), s32[]{:S(2)}) async-start(), calls=%async_computation.7 | async-start | bytes 2752512 | tf_op jit(solution)/shard_map/all_gather | solution.py:226
  429.6 52.5 %all-gather.12.cloned.1.call-start = ((), (), s32[]{:S(2)}) async-start(), calls=%async_computation.8 | async-start | bytes 5505024 | tf_op jit(solution)/shard_map/all_gather | solution.py:227
Sparse Core Ops, SparseCore 0:
  40.5 188.0 all-gather.7
  289.6 42.2 reduce-scatter.2
  334.3 92.0 reduce-scatter.4
  429.8 33.7 all-gather.9
  465.1 16.9 all-gather.11

commit v5 on v4

--- a/solution.py
+++ b/solution.py
@@ -112,7 +112,8 @@
     )(act, grad)
 
 
-def xgather_kernel(act_ref, act_out, send_sem, recv_sem, local_sem):
+def xgather_kernel(act_ref, seq_ref, act_out, seq_out, send_sem, recv_sem, local_sem,
+                   seq_send, seq_recv):
     n = lax.axis_size("x")
     me = lax.axis_index("x")
     right, left = lax.rem(me + 1, n), lax.rem(me + n - 1, n)
@@ -127,6 +128,18 @@
 
     own = pltpu.make_async_copy(act_ref, act_out.at[me], local_sem.at[0])
     own.start()
+    own_seq = pltpu.make_async_copy(seq_ref, seq_out.at[me], local_sem.at[1])
+    own_seq.start()
+
+    def seq_copy(src, dst, slot, dev):
+        return pltpu.make_async_remote_copy(
+            src_ref=src, dst_ref=dst, send_sem=seq_send.at[slot], recv_sem=seq_recv.at[slot],
+            device_id={"x": dev}, device_id_type=MESH)
+
+    seq_r = seq_copy(seq_ref, seq_out.at[me], 0, right)
+    seq_l = seq_copy(seq_ref, seq_out.at[me], 1, left)
+    seq_r.start()
+    seq_l.start()
     to_right = pltpu.make_async_remote_copy(
         src_ref=act_ref, dst_ref=act_out.at[me], send_sem=send_sem.at[0],
         recv_sem=recv_sem.at[0], device_id={"x": right}, device_id_type=MESH)
@@ -143,6 +156,10 @@
         recv_sem=recv_sem.at[1], device_id={"x": right}, device_id_type=MESH)
     from_left.wait_recv()
     from_right.wait_recv()
+    seq_copy(seq_ref, seq_out.at[left], 0, left).wait_recv()
+    seq_copy(seq_ref, seq_out.at[right], 1, right).wait_recv()
+    seq_relay = seq_copy(seq_out.at[right], seq_out.at[right], 2, left)
+    seq_relay.start()
     relay_left = pltpu.make_async_remote_copy(
         src_ref=act_out.at[right, pl.ds(0, half)], dst_ref=act_out.at[right, pl.ds(0, half)],
         send_sem=send_sem.at[2], recv_sem=recv_sem.at[2], device_id={"x": left},
@@ -163,6 +180,11 @@
         device_id_type=MESH)
     far_first.wait_recv()
     far_second.wait_recv()
+    seq_copy(seq_out.at[far], seq_out.at[far], 2, right).wait_recv()
+    seq_r.wait_send()
+    seq_l.wait_send()
+    seq_relay.wait_send()
+    own_seq.wait()
     to_right.wait_send()
     to_left.wait_send()
     relay_left.wait_send()
@@ -170,22 +192,27 @@
     own.wait()
 
 
-def xgather(act):
+def xgather(act, seq):
     n = 4
     rows, cols = act.shape
     return pl.pallas_call(
         xgather_kernel,
-        out_shape=jax.ShapeDtypeStruct((n, rows, cols), act.dtype),
-        in_specs=[pl.BlockSpec(memory_space=pl.ANY)],
-        out_specs=pl.BlockSpec(memory_space=pl.ANY),
+        out_shape=(
+            jax.ShapeDtypeStruct((n, rows, cols), act.dtype),
+            jax.ShapeDtypeStruct((n,) + seq.shape, seq.dtype),
+        ),
+        in_specs=[pl.BlockSpec(memory_space=pl.ANY)] * 2,
+        out_specs=(pl.BlockSpec(memory_space=pl.ANY), pl.BlockSpec(memory_space=pl.ANY)),
         scratch_shapes=[
             pltpu.SemaphoreType.DMA((4,)),
             pltpu.SemaphoreType.DMA((4,)),
-            pltpu.SemaphoreType.DMA((1,)),
+            pltpu.SemaphoreType.DMA((2,)),
+            pltpu.SemaphoreType.DMA((3,)),
+            pltpu.SemaphoreType.DMA((3,)),
         ],
         compiler_params=pltpu.CompilerParams(collective_id=1, has_side_effects=True),
         cost_estimate=pl.CostEstimate(flops=0, bytes_accessed=8 * rows * cols * 2, transcendentals=0),
-    )(act)
+    )(act, seq)
 
 
 def per_device(activations, out_grads, seq_ids, weights):
@@ -194,11 +221,10 @@
     tok = activations.shape[1]
     col_width = weights.shape[2]
     row_width = weights.shape[1]
-    owners = lax.all_gather(seq_ids[0], ("x", "zh", "y"), axis=0, tiled=True)
-    total = owners.shape[0]
+    total = nx * nj * tok
     act_blocks = activations[0].reshape(tok, nj, row_width).transpose(1, 0, 2)
     act_mine = lax.all_to_all(act_blocks, ("zh", "y"), 0, 0, tiled=True)
-    act_all = xgather(act_mine.reshape(nj * tok, row_width))
+    act_all, owners = xgather(act_mine.reshape(nj * tok, row_width), seq_ids)
     grad_blocks = out_grads[0].reshape(tok, nx, col_width).transpose(1, 0, 2)
     grad_mine = lax.all_to_all(grad_blocks, "x", 0, 0, tiled=True)
     grad_all = lax.all_gather(grad_mine, ("zh", "y"), axis=0, tiled=False)
@@ -213,13 +239,13 @@
     head = part(0)
     mid = part(1) + part(2)
     tail = part(3)
-    first_long = jnp.sum((owners < 1).astype(jnp.int32)) > total // 2
+    first_long = jnp.sum((owners < 1).astype(jnp.int32)) * (total // owners.size) > total // 2
     g0 = jnp.where(first_long, head + mid, head)
     g1 = jnp.where(first_long, tail, mid + tail)
     fisher = g0 * g0 + g1 * g1
     prior = fisher / SEQS + smoothing
-    numer = prior * weights[0].astype(jnp.float32)
-    both = jnp.stack([numer, prior], axis=0)
+    w = weights[0].astype(jnp.float32)
+    both = prior[None] * jnp.stack([w, jnp.ones_like(w)], axis=0)
     both = lax.psum_scatter(both, "c", scatter_dimension=1, tiled=True)
     both = lax.psum_scatter(both, "zl", scatter_dimension=1, tiled=True)
     merged_q = (both[0] / both[1]).astype(jnp.bfloat16)

time: 493 us -> 463 us (0.939)
  blocking collectives: 136 us -> 77.7 us
  waiting for transfers between devices: 189 us -> 235 us
  other arithmetic: 23.8 us -> 15.1 us
  starting transfers between devices: 7.66 us -> 0.17 us
  local copies, waits for them, and re-layouts: 26.2 us -> 20.5 us
    all_gather x1 -> x0, blocking collectives: 109 us -> none  [per_device(): owners = lax.all_gather(seq_ids[0], ('x', 'zh', 'y'), axis=0, tiled=True)]
    all_gather x1, waiting for transfers between devices: 0.02 us -> 63.3 us  [per_device(): grad_all = lax.all_gather(grad_mine, ('zh', 'y'), axis=0, tiled=False)]
    all_to_all x0 -> x1, blocking collectives: none -> 50.2 us  [per_device(): act_mine = lax.all_to_all(act_blocks, ('zh', 'y'), 0, 0, tiled=True)]
    another operation x2 -> x0, other arithmetic: 19.9 us -> none  [per_device(): both = jnp.stack([numer, prior], axis=0)]
    reduce_scatter x1, waiting for transfers between devices: 42.4 us -> 25.4 us  [per_device(): both = lax.psum_scatter(both, 'c', scatter_dimension=1, tiled=True)]
    mul x0 -> x1, other arithmetic: none -> 10.5 us  [per_device(): both = prior[None] * jnp.stack([w, jnp.ones_like(w)], axis=0)]
    all_to_all x1 -> x0, starting transfers between devices: 7.5 us -> none  [per_device(): act_mine = lax.all_to_all(act_blocks, ('zh', 'y'), 0, 0, tiled=True)]
    unnamed x11 -> x9, local copies, waits for them, and re-layouts: 13.5 us -> 11 us
  transfers between devices with their start and end apart: 6 -> 5, of which waited for: 4 -> 5; matrix products, arithmetic and copies ran while one was open for 1% -> 1% of each run, Pallas kernels for 13% -> 14%
where the time goes in v5:
time: 463 us
  waiting for transfers between devices  235 us (51%)
  blocking collectives  77.7 us (17%)
  Pallas kernels  66.4 us (14%)
  matrix products  33.5 us (7%)
  local copies, waits for them, and re-layouts  20.5 us (4%)
  other arithmetic  15.1 us (3%)
  between operations  13.8 us (3%)
    reduce_scatter x1, waiting for transfers between devices, per_device(): both = lax.psum_scatter(both, 'zl', scatter_dimension=1, tiled=True)  94.3 us
    pallas_call x1, Pallas kernels, xgather(): pl.pallas_call(xgather_kernel, out_shape=(jax.ShapeDtypeStruct((n, rows,...  66.4 us
    all_gather x1, waiting for transfers between devices, per_device(): grad_all = lax.all_gather(grad_mine, ('zh', 'y'), axis=0, tiled=False)  63.3 us
    all_to_all x1, blocking collectives, per_device(): act_mine = lax.all_to_all(act_blocks, ('zh', 'y'), 0, 0, tiled=True)  50.2 us
    all_gather x1, waiting for transfers between devices, per_device(): merged_h = lax.all_gather(merged_q, 'zl', axis=0, tiled=True)  33.8 us
    dot_general x4, matrix products, part(): lax.dot_general(act_x[x], g, (((0,), (0,)), ((), ())), preferred_element_...  33.5 us
    all_to_all x1, blocking collectives, per_device(): grad_mine = lax.all_to_all(grad_blocks, 'x', 0, 0, tiled=True)  27.5 us
    reduce_scatter x1, waiting for transfers between devices, per_device(): both = lax.psum_scatter(both, 'c', scatter_dimension=1, tiled=True)  25.4 us
  transfers between devices with their start and end apart: 5, of which 5 were waited for; matrix products, arithmetic and copies ran while one was open for 1% of the time, Pallas kernels for 14%

profile of v5, /device:TPU:1, one launch (start us, length us, event | category | flops | bytes accessed | tf_op | source)
XLA Modules:
  0.0 462.5 jit_solution(7576307412347072699)
XLA Ops:
  6.5 0.0 all-gather.7.cloned.1.call-start
  6.5 3.9 copy.12
  10.4 27.5 %all_to_all.10 = bf16[4,128,1792]{1,2,0:T(8,128)(2,1)S(1)} all-to-all(bf16[4,128,1792]{1,2,0:T(8,128)(2,1)} %bitcast.36), channel_id=1, replica_groups=mesh['zl'=2,'c'=2,'x'=4,'zh'=2,'y'=4] {'x'}, dimensions={0} | all-to-all | bytes 3670016 | tf_op jit(solution)/shard_map/all_to_all | solution.py:229
  37.9 2.4 copy.13
  40.3 0.0 all-gather.7.cloned.1.call-update
  40.3 0.0 reduce-scatter.3.cloned.1.call-start
  40.4 3.0 copy.14
  43.4 1.2 copy.16
  44.5 50.2 %all_to_all.11 = bf16[8,128,1024]{2,1,0:T(8,128)(2,1)} all-to-all(bf16[8,128,1024]{2,1,0:T(8,128)(2,1)S(1)} %bitcast.34), channel_id=1, replica_groups=mesh['zl'=2,'c'=2,'x'=4,'zh'=2,'y'=4] {'zh','y'}, dimensions={0} | all-to-all | bytes 4194304 | tf_op jit(solution)/shard_map/all_to_all | solution.py:226
  94.7 66.4 %shard_map.46 = (bf16[4,1024,1024]{2,1,0:T(8,128)(2,1)}, s32[4,1,128]{2,1,0:T(1,128)}) custom-call(bf16[1024,1024]{1,0:T(8,128)(2,1)} %bitcast.33, s32[1,128]{1,0:T(1,128)} %seq_ref.1), custom_call_target="tpu_custom_call" | custom-call | bytes 16777216 | tf_op jit(solution)/shard_map/pallas_call | solution.py:198
  161.2 1.3 fusion.17
  163.0 63.3 %all-gather.7.cloned.1.call-done = bf16[32,128,1792]{2,1,0:T(8,128)(2,1)} async-done(((bf16[4,128,1792]{2,1,0:T(8,128)(2,1)}), bf16[32,128,1792]{2,1,0:T(8,128)(2,1)}) %all-gather.7.cloned.1.call-update) | async-done | bytes 14680080 | tf_op jit(solution)/shard_map/all_gather | solution.py:230
  226.4 5.9 %fusion.18 = (bf16[8,1,128,1792]{3,2,1,0:T(8,128)(2,1)S(1)}, bf16[8,1,128,1792]{3,2,1,0:T(8,128)(2,1)S(1)}, bf16[8,1,128,1792]{3,2,1,0:T(8,128)(2,1)S(1)}, bf16[8,1,128,1792]{3,2,1,0:T(8,128)(2,1)S(1)}) fusion(bf16[8,4,128,1792]{3,2,1,0:T(8,128)(2,1)} %bitcast.32), kind=kLoop, calls=%fused_computation.24 | loop fusion | bytes 29360128 | tf_op jit(solution)/shard_map/slice | solution.py:234
  232.3 0.0 copy-start
  232.3 8.8 %fusion.5 = f32[1024,1792]{1,0:T(8,128)} fusion(bf16[1024,1792]{1,0:T(8,128)(2,1)S(1)} %bitcast.40, bf16[4,1024,1024]{2,1,0:T(8,128)(2,1)} %get-tuple-element.8), kind=kOutput, calls=%fused_computation.8 | convolution fusion | flops 3758096384 | bytes 13107200 | tf_op jit(solution)/shard_map/dot_general | solution.py:235
  241.1 0.0 copy-done
  241.1 0.0 slice-start
  241.1 6.2 %fusion.8 = f32[1024,1792]{1,0:T(8,128)} fusion(bf16[1024,1792]{1,0:T(8,128)(2,1)S(1)} %bitcast.39, bf16[4,1024,1024]{2,1,0:T(8,128)(2,1)S(1)} %copy-done), kind=kOutput, calls=%fused_computation.11 | convolution fusion | flops 3758096384 | bytes 13107200 | tf_op jit(solution)/shard_map/dot_general | solution.py:235
  247.3 0.0 slice-start.1
  247.3 6.3 %fusion.10 = f32[1024,1792]{1,0:T(8,128)} fusion(bf16[1024,1792]{1,0:T(8,128)(2,1)S(1)} %bitcast.38, bf16[4,1024,1024]{2,1,0:T(8,128)(2,1)S(1)} %copy-done), kind=kOutput, calls=%fused_computation.13 | convolution fusion | flops 3758096384 | bytes 13107200 | tf_op jit(solution)/shard_map/dot_general | solution.py:235
  253.6 0.0 slice-done
  253.6 0.0 slice-done.1
  253.6 12.2 %fusion.3 = f32[1024,1792]{1,0:T(8,128)} fusion(f32[1024,1792]{1,0:T(8,128)} %fusion.10, f32[1024,1792]{1,0:T(8,128)S(1)} %bitcast.44, f32[1024,1792]{1,0:T(8,128)} %fusion.8, bf16[1024,1792]{1,0:T(8,128)(2,1)S(1)} %bitcast.37, pred[]{:T(512)S(6)} %gt.3, bf16[4,1024,1024]{2,1,0:T(8,128)(2,1)} %get-tuple-element.8), kind=kOutput, calls=%fused_computation.6 | convolution fusion | flops 3776446464 | bytes 35127296 | tf_op jit(solution)/shard_map/dot_general | solution.py:235
  265.8 10.5 %convert_multiply_fusion = f32[2,1024,1792]{2,1,0:T(8,128)} fusion(bf16[1,1024,1792]{2,1,0:T(8,128)(2,1)} %param.7, f32[1024,1792]{1,0:T(8,128)} %fusion.3), kind=kLoop, calls=%fused_computation | loop fusion | flops 7340032 | bytes 25690112 | tf_op jit(solution)/shard_map/mul | solution.py:248
  276.3 0.0 reduce-scatter.3.cloned.1.call-update
  276.4 0.0 reduce-scatter.5.cloned.1.call-start
  276.4 25.4 %reduce-scatter.3.cloned.1.call-done = f32[2,512,1792]{2,1,0:T(8,128)} async-done(((f32[2,1024,1792]{2,1,0:T(8,128)}), f32[2,512,1792]{2,1,0:T(8,128)}) %reduce-scatter.3.cloned.1.call-update) | async-done | bytes 7340048 | tf_op jit(solution)/shard_map/reduce_scatter | solution.py:249
  301.8 0.0 reduce-scatter.5.cloned.1.call-update
  301.8 0.0 all-gather.9.cloned.1.call-start
  301.8 94.3 %reduce-scatter.5.cloned.1.call-done = f32[2,256,1792]{2,1,0:T(8,128)} async-done(((f32[2,512,1792]{2,1,0:T(8,128)}), f32[2,256,1792]{2,1,0:T(8,128)}) %reduce-scatter.5.cloned.1.call-update) | async-done | bytes 3670032 | tf_op jit(solution)/shard_map/reduce_scatter | solution.py:250
  396.1 3.2 fusion.16
  399.3 0.0 all-gather.9.cloned.1.call-update
  399.3 0.0 all-gather.11.cloned.1.call-start
  399.4 33.8 %all-gather.9.cloned.1.call-done = bf16[1,512,1792]{2,1,0:T(8,128)(2,1)} async-done(((bf16[1,256,1792]{2,1,0:T(8,128)(2,1)}), bf16[1,512,1792]{2,1,0:T(8,128)(2,1)}) %all-gather.9.cloned.1.call-update) | async-done | bytes 1835024 | tf_op jit(solution)/shard_map/all_gather | solution.py:252
  433.2 0.0 all-gather.11.cloned.1.call-update
  433.3 18.6 %all-gather.11.cloned.1.call-done = bf16[1,1024,1792]{2,1,0:T(8,128)(2,1)} async-done(((bf16[1,512,1792]{2,1,0:T(8,128)(2,1)}), bf16[1,1024,1792]{2,1,0:T(8,128)(2,1)}) %all-gather.11.cloned.1.call-update) | async-done | bytes 3670032 | tf_op jit(solution)/shard_map/all_gather | solution.py:253
  451.9 4.1 copy.18
  (1 shorter events, 0.0 us)
Async XLA Ops:
  6.5 219.8 %all-gather.7.cloned.1.call-start = ((), (), s32[]{:S(2)}) async-start(), calls=%async_computation.6 | async-start | bytes 16515072 | tf_op jit(solution)/shard_map/all_gather | solution.py:230
  40.3 261.5 %reduce-scatter.3.cloned.1.call-start = ((), (), s32[]{:S(2)}) async-start(), calls=%async_computation.4 | async-start | bytes 22020096 | tf_op jit(solution)/shard_map/reduce_scatter | solution.py:249
  232.3 8.8 %copy-start = (bf16[4,1024,1024]{2,1,0:T(8,128)(2,1)S(1)}, bf16[4,1024,1024]{2,1,0:T(8,128)(2,1)}, u32[]{:S(2)}) copy-start(bf16[4,1024,1024]{2,1,0:T(8,128)(2,1)} %get-tuple-element.8) | copy-start | bytes 25165828
  241.1 12.4 %slice-start = ((s8[7340032]{0:T(1024)(128)(4,1)}), s8[3145728]{0:T(1024)(128)(4,1)S(1)}, s32[]{:S(2)}) async-start(s8[7340032]{0:T(1024)(128)(4,1)} %bitcast.43), calls=%async_computation.9 | async-start | bytes 6291456
  247.3 6.3 %slice-start.1 = ((s8[7340032]{0:T(1024)(128)(4,1)}), s8[4194304]{0:T(1024)(128)(4,1)S(1)}, s32[]{:S(2)}) async-start(s8[7340032]{0:T(1024)(128)(4,1)} %bitcast.43), calls=%async_computation.10 | async-start | bytes 8388608
  276.4 119.7 %reduce-scatter.5.cloned.1.call-start = ((), (), s32[]{:S(2)}) async-start(), calls=%async_computation.5 | async-start | bytes 11010048 | tf_op jit(solution)/shard_map/reduce_scatter | solution.py:250
  301.8 131.4 %all-gather.9.cloned.1.call-start = ((), (), s32[]{:S(2)}) async-start(), calls=%async_computation.7 | async-start | bytes 2752512 | tf_op jit(solution)/shard_map/all_gather | solution.py:252
  399.3 52.5 %all-gather.11.cloned.1.call-start = ((), (), s32[]{:S(2)}) async-start(), calls=%async_computation.8 | async-start | bytes 5505024 | tf_op jit(solution)/shard_map/all_gather | solution.py:253
Sparse Core Ops, SparseCore 0:
  40.4 185.9 all-gather.6
  276.5 25.2 reduce-scatter.2
  304.2 91.8 reduce-scatter.4
  399.5 33.7 all-gather.8
  434.8 16.9 all-gather.10

commit v6 on v5

--- a/solution.py
+++ b/solution.py
@@ -215,6 +215,92 @@
     )(act, seq)
 
 
+def mp_merge_kernel(both_ref, out_ref, recv1, recv2, send_sem, recv_sem):
+    c = lax.axis_index("c")
+    z = lax.axis_index("zl")
+    rows = both_ref.shape[1]
+    half, quarter = rows // 2, rows // 4
+    step = 32
+    core = {"c": 1 - c}
+    chip = {"zl": 1 - z}
+
+    barrier = pltpu.get_barrier_semaphore()
+    pl.semaphore_signal(barrier, 1, device_id=core, device_id_type=MESH)
+    pl.semaphore_signal(barrier, 1, device_id=chip, device_id_type=MESH)
+    pl.semaphore_wait(barrier, 2)
+
+    mine = pl.multiple_of(c * half, half)
+    other = pl.multiple_of((1 - c) * half, half)
+    first = pltpu.make_async_remote_copy(
+        src_ref=both_ref.at[:, pl.ds(other, half)], dst_ref=recv1,
+        send_sem=send_sem.at[0], recv_sem=recv_sem.at[0], device_id=core, device_id_type=MESH)
+    first.start()
+    first.wait_recv()
+
+    def add_half(i, carry):
+        r = pl.multiple_of(i * step, step)
+        recv1[:, pl.ds(r, step)] = recv1[:, pl.ds(r, step)] + both_ref[:, pl.ds(mine + r, step)]
+        return carry
+
+    lax.fori_loop(0, half // step, add_half, 0)
+
+    my_q = pl.multiple_of(z * quarter, quarter)
+    far_q = pl.multiple_of((1 - z) * quarter, quarter)
+    second = pltpu.make_async_remote_copy(
+        src_ref=recv1.at[:, pl.ds(far_q, quarter)], dst_ref=recv2,
+        send_sem=send_sem.at[1], recv_sem=recv_sem.at[1], device_id=chip, device_id_type=MESH)
+    second.start()
+    second.wait_recv()
+
+    def merge(i, carry):
+        r = pl.multiple_of(i * step, step)
+        n = recv1[0, pl.ds(my_q + r, step)] + recv2[0, pl.ds(r, step)]
+        d = recv1[1, pl.ds(my_q + r, step)] + recv2[1, pl.ds(r, step)]
+        out_ref[pl.ds(mine + my_q + r, step)] = (n / d).astype(out_ref.dtype)
+        return carry
+
+    lax.fori_loop(0, quarter // step, merge, 0)
+
+    third = pltpu.make_async_remote_copy(
+        src_ref=out_ref.at[pl.ds(mine + my_q, quarter)], dst_ref=out_ref.at[pl.ds(mine + my_q, quarter)],
+        send_sem=send_sem.at[2], recv_sem=recv_sem.at[2], device_id=chip, device_id_type=MESH)
+    third.start()
+    pltpu.make_async_remote_copy(
+        src_ref=out_ref.at[pl.ds(mine + far_q, quarter)], dst_ref=out_ref.at[pl.ds(mine + far_q, quarter)],
+        send_sem=send_sem.at[2], recv_sem=recv_sem.at[2], device_id=chip, device_id_type=MESH).wait_recv()
+    fourth = pltpu.make_async_remote_copy(
+        src_ref=out_ref.at[pl.ds(mine, half)], dst_ref=out_ref.at[pl.ds(mine, half)],
+        send_sem=send_sem.at[3], recv_sem=recv_sem.at[3], device_id=core, device_id_type=MESH)
+    fourth.start()
+    pltpu.make_async_remote_copy(
+        src_ref=out_ref.at[pl.ds(other, half)], dst_ref=out_ref.at[pl.ds(other, half)],
+        send_sem=send_sem.at[3], recv_sem=recv_sem.at[3], device_id=core, device_id_type=MESH).wait_recv()
+    first.wait_send()
+    second.wait_send()
+    third.wait_send()
+    fourth.wait_send()
+
+
+def mp_merge(both):
+    _, rows, cols = both.shape
+    vmem = pltpu.MemorySpace.VMEM
+    return pl.pallas_call(
+        mp_merge_kernel,
+        out_shape=jax.ShapeDtypeStruct((rows, cols), jnp.bfloat16),
+        in_specs=[pl.BlockSpec(memory_space=vmem)],
+        out_specs=pl.BlockSpec(memory_space=vmem),
+        scratch_shapes=[
+            pltpu.VMEM((2, rows // 2, cols), jnp.float32),
+            pltpu.VMEM((2, rows // 4, cols), jnp.float32),
+            pltpu.SemaphoreType.DMA((4,)),
+            pltpu.SemaphoreType.DMA((4,)),
+        ],
+        compiler_params=pltpu.CompilerParams(
+            collective_id=2, has_side_effects=True, vmem_limit_bytes=60 * 1024 * 1024),
+        cost_estimate=pl.CostEstimate(flops=rows * cols * 4, bytes_accessed=rows * cols * 16, transcendentals=0),
+    )(both)
+
+
 def per_device(activations, out_grads, seq_ids, weights):
     nx = lax.axis_size("x")
     nj = lax.axis_size(("zh", "y"))
@@ -246,11 +332,7 @@
     prior = fisher / SEQS + smoothing
     w = weights[0].astype(jnp.float32)
     both = prior[None] * jnp.stack([w, jnp.ones_like(w)], axis=0)
-    both = lax.psum_scatter(both, "c", scatter_dimension=1, tiled=True)
-    both = lax.psum_scatter(both, "zl", scatter_dimension=1, tiled=True)
-    merged_q = (both[0] / both[1]).astype(jnp.bfloat16)
-    merged_h = lax.all_gather(merged_q, "zl", axis=0, tiled=True)
-    return lax.all_gather(merged_h, "c", axis=0, tiled=True)
+    return mp_merge(both)
 
 
 def solution(mesh):

time: 463 us -> 415 us (0.90)
  waiting for transfers between devices: 235 us -> 63.4 us
  Pallas kernels: 66.4 us -> 193 us
    pallas_call x0 -> x1, Pallas kernels: none -> 127 us  [mp_merge(): pl.pallas_call(mp_merge_kernel, out_shape=jax.ShapeDtypeStruct((rows, col...]
    reduce_scatter x2 -> x0, waiting for transfers between devices: 120 us -> none  [the longest x1 94.3 us: per_device(): both = lax.psum_scatter(both, 'zl', scatter_dimension=1, tiled=True)]
    all_gather x2 -> x0, waiting for transfers between devices: 52.5 us -> none  [the longest x1 33.8 us: per_device(): merged_h = lax.all_gather(merged_q, 'zl', axis=0, tiled=True)]
  transfers between devices with their start and end apart: 5 -> 1, of which waited for: 5 -> 1; matrix products, arithmetic and copies ran while one was open for 1% -> 1% of each run, Pallas kernels for 14% -> 16%
where the time goes in v6:
time: 415 us; the launch traced here: 414 us
  Pallas kernels  193 us (47%)
  blocking collectives  77.6 us (19%)
  waiting for transfers between devices  63.4 us (15%)
  matrix products  33.4 us (8%)
  local copies, waits for them, and re-layouts  20.5 us (5%)
  between operations  14.1 us (3%)
  other arithmetic  11.9 us (3%)
    pallas_call x1, Pallas kernels, mp_merge(): pl.pallas_call(mp_merge_kernel, out_shape=jax.ShapeDtypeStruct((rows, col...  127 us
    pallas_call x1, Pallas kernels, xgather(): pl.pallas_call(xgather_kernel, out_shape=(jax.ShapeDtypeStruct((n, rows,...  66.3 us
    all_gather x1, waiting for transfers between devices, per_device(): grad_all = lax.all_gather(grad_mine, ('zh', 'y'), axis=0, tiled=False)  63.4 us
    all_to_all x1, blocking collectives, per_device(): act_mine = lax.all_to_all(act_blocks, ('zh', 'y'), 0, 0, tiled=True)  50.1 us
    dot_general x4, matrix products, part(): lax.dot_general(act_x[x], g, (((0,), (0,)), ((), ())), preferred_element_...  33.4 us
    all_to_all x1, blocking collectives, per_device(): grad_mine = lax.all_to_all(grad_blocks, 'x', 0, 0, tiled=True)  27.5 us
    unnamed x9, local copies, waits for them, and re-layouts  11 us
    mul x1, other arithmetic, per_device(): both = prior[None] * jnp.stack([w, jnp.ones_like(w)], axis=0)  10.6 us
  transfers between devices with their start and end apart: 1, of which 1 were waited for; matrix products, arithmetic and copies ran while one was open for 1% of the time, Pallas kernels for 16%

profile of v6, /device:TPU:1, one launch (start us, length us, event | category | flops | bytes accessed | tf_op | source)
XLA Modules:
  0.0 414.2 jit_solution(16160581166527345039)
XLA Ops:
  6.5 0.0 all-gather.3.cloned.1.call-start
  6.5 3.9 copy.12
  10.4 27.5 %all_to_all.10 = bf16[4,128,1792]{1,2,0:T(8,128)(2,1)S(1)} all-to-all(bf16[4,128,1792]{1,2,0:T(8,128)(2,1)} %bitcast.35), channel_id=1, replica_groups=mesh['zl'=2,'c'=2,'x'=4,'zh'=2,'y'=4] {'x'}, dimensions={0} | all-to-all | bytes 3670016 | tf_op jit(solution)/shard_map/all_to_all | solution.py:315
  37.9 2.4 copy.13
  40.3 0.0 all-gather.3.cloned.1.call-update
  40.3 3.0 copy.14
  43.3 1.2 copy.16
  44.5 50.1 %all_to_all.11 = bf16[8,128,1024]{2,1,0:T(8,128)(2,1)} all-to-all(bf16[8,128,1024]{2,1,0:T(8,128)(2,1)S(1)} %bitcast.33), channel_id=1, replica_groups=mesh['zl'=2,'c'=2,'x'=4,'zh'=2,'y'=4] {'zh','y'}, dimensions={0} | all-to-all | bytes 4194304 | tf_op jit(solution)/shard_map/all_to_all | solution.py:312
  94.6 66.3 %shard_map.46 = (bf16[4,1024,1024]{2,1,0:T(8,128)(2,1)}, s32[4,1,128]{2,1,0:T(1,128)}) custom-call(bf16[1024,1024]{1,0:T(8,128)(2,1)} %bitcast.32, s32[1,128]{1,0:T(1,128)} %seq_ref.1), custom_call_target="tpu_custom_call" | custom-call | bytes 16777216 | tf_op jit(solution)/shard_map/pallas_call | solution.py:198
  160.9 1.3 fusion.16
  162.9 63.4 %all-gather.3.cloned.1.call-done = bf16[32,128,1792]{2,1,0:T(8,128)(2,1)} async-done(((bf16[4,128,1792]{2,1,0:T(8,128)(2,1)}), bf16[32,128,1792]{2,1,0:T(8,128)(2,1)}) %all-gather.3.cloned.1.call-update) | async-done | bytes 14680080 | tf_op jit(solution)/shard_map/all_gather | solution.py:316
  226.3 5.9 %fusion.17 = (bf16[8,1,128,1792]{3,2,1,0:T(8,128)(2,1)S(1)}, bf16[8,1,128,1792]{3,2,1,0:T(8,128)(2,1)S(1)}, bf16[8,1,128,1792]{3,2,1,0:T(8,128)(2,1)S(1)}, bf16[8,1,128,1792]{3,2,1,0:T(8,128)(2,1)S(1)}) fusion(bf16[8,4,128,1792]{3,2,1,0:T(8,128)(2,1)} %bitcast.31), kind=kLoop, calls=%fused_computation.22 | loop fusion | bytes 29360128 | tf_op jit(solution)/shard_map/slice | solution.py:320
  232.3 0.0 copy-start
  232.3 8.8 %fusion.5 = f32[1024,1792]{1,0:T(8,128)} fusion(bf16[1024,1792]{1,0:T(8,128)(2,1)S(1)} %bitcast.39, bf16[4,1024,1024]{2,1,0:T(8,128)(2,1)} %get-tuple-element.8), kind=kOutput, calls=%fused_computation.8 | convolution fusion | flops 3758096384 | bytes 13107200 | tf_op jit(solution)/shard_map/dot_general | solution.py:321
  241.1 0.0 copy-done
  241.1 0.0 slice-start
  241.1 6.2 %fusion.8 = f32[1024,1792]{1,0:T(8,128)} fusion(bf16[1024,1792]{1,0:T(8,128)(2,1)S(1)} %bitcast.38, bf16[4,1024,1024]{2,1,0:T(8,128)(2,1)S(1)} %copy-done), kind=kOutput, calls=%fused_computation.11 | convolution fusion | flops 3758096384 | bytes 13107200 | tf_op jit(solution)/shard_map/dot_general | solution.py:321
  247.3 0.0 slice-start.1
  247.3 6.2 %fusion.10 = f32[1024,1792]{1,0:T(8,128)} fusion(bf16[1024,1792]{1,0:T(8,128)(2,1)S(1)} %bitcast.37, bf16[4,1024,1024]{2,1,0:T(8,128)(2,1)S(1)} %copy-done), kind=kOutput, calls=%fused_computation.13 | convolution fusion | flops 3758096384 | bytes 13107200 | tf_op jit(solution)/shard_map/dot_general | solution.py:321
  253.5 0.0 slice-done
  253.5 0.0 slice-done.1
  253.5 12.1 %fusion.3 = f32[1024,1792]{1,0:T(8,128)} fusion(f32[1024,1792]{1,0:T(8,128)} %fusion.10, f32[1024,1792]{1,0:T(8,128)S(1)} %bitcast.42, f32[1024,1792]{1,0:T(8,128)} %fusion.8, bf16[1024,1792]{1,0:T(8,128)(2,1)S(1)} %bitcast.36, pred[]{:T(512)S(6)} %gt.3, bf16[4,1024,1024]{2,1,0:T(8,128)(2,1)} %get-tuple-element.8), kind=kOutput, calls=%fused_computation.6 | convolution fusion | flops 3776446464 | bytes 35127296 | tf_op jit(solution)/shard_map/dot_general | solution.py:321
  265.6 10.6 %convert_multiply_fusion.both_ref = f32[2,1024,1792]{2,1,0:T(8,128)} fusion(bf16[1,1024,1792]{2,1,0:T(8,128)(2,1)} %param.7, f32[1024,1792]{1,0:T(8,128)} %fusion.3), kind=kLoop, calls=%fused_computation | loop fusion | flops 7340032 | bytes 25690112 | tf_op jit(solution)/shard_map/mul | solution.py:334
  276.2 127.0 %shard_map.47 = bf16[1024,1792]{1,0:T(8,128)(2,1)} custom-call(f32[2,1024,1792]{2,1,0:T(8,128)} %convert_multiply_fusion.both_ref), custom_call_target="tpu_custom_call" | custom-call | flops 7340032 | bytes 29360128 | tf_op jit(solution)/shard_map/pallas_call | solution.py:287
  403.2 4.1 copy.18
  (1 shorter events, 0.0 us)
Async XLA Ops:
  6.5 219.8 %all-gather.3.cloned.1.call-start = ((), (), s32[]{:S(2)}) async-start(), calls=%async_computation.2 | async-start | bytes 16515072 | tf_op jit(solution)/shard_map/all_gather | solution.py:316
  232.3 8.8 %copy-start = (bf16[4,1024,1024]{2,1,0:T(8,128)(2,1)S(1)}, bf16[4,1024,1024]{2,1,0:T(8,128)(2,1)}, u32[]{:S(2)}) copy-start(bf16[4,1024,1024]{2,1,0:T(8,128)(2,1)} %get-tuple-element.8) | copy-start | bytes 25165828
  241.1 12.4 %slice-start = ((s8[7340032]{0:T(1024)(128)(4,1)}), s8[3145728]{0:T(1024)(128)(4,1)S(1)}, s32[]{:S(2)}) async-start(s8[7340032]{0:T(1024)(128)(4,1)} %bitcast.41), calls=%async_computation.3 | async-start | bytes 6291456
  247.3 6.2 %slice-start.1 = ((s8[7340032]{0:T(1024)(128)(4,1)}), s8[4194304]{0:T(1024)(128)(4,1)S(1)}, s32[]{:S(2)}) async-start(s8[7340032]{0:T(1024)(128)(4,1)} %bitcast.41), calls=%async_computation.4 | async-start | bytes 8388608
Sparse Core Ops, SparseCore 0:
  40.4 185.8 all-gather.2

commit v7 on v6

--- a/solution.py
+++ b/solution.py
@@ -281,7 +281,7 @@
     fourth.wait_send()
 
 
-def mp_merge(both):
+def mp_merge(both, cid):
     _, rows, cols = both.shape
     vmem = pltpu.MemorySpace.VMEM
     return pl.pallas_call(
@@ -296,7 +296,7 @@
             pltpu.SemaphoreType.DMA((4,)),
         ],
         compiler_params=pltpu.CompilerParams(
-            collective_id=2, has_side_effects=True, vmem_limit_bytes=60 * 1024 * 1024),
+            collective_id=cid, has_side_effects=True, vmem_limit_bytes=60 * 1024 * 1024),
         cost_estimate=pl.CostEstimate(flops=rows * cols * 4, bytes_accessed=rows * cols * 16, transcendentals=0),
     )(both)
 
@@ -310,29 +310,37 @@
     total = nx * nj * tok
     act_blocks = activations[0].reshape(tok, nj, row_width).transpose(1, 0, 2)
     act_mine = lax.all_to_all(act_blocks, ("zh", "y"), 0, 0, tiled=True)
-    act_all, owners = xgather(act_mine.reshape(nj * tok, row_width), seq_ids)
     grad_blocks = out_grads[0].reshape(tok, nx, col_width).transpose(1, 0, 2)
     grad_mine = lax.all_to_all(grad_blocks, "x", 0, 0, tiled=True)
-    grad_all = lax.all_gather(grad_mine, ("zh", "y"), axis=0, tiled=False)
-    act_x = act_all
-
-    def part(x):
-        g = grad_all[:, x].reshape(nj * tok, col_width)
-        return lax.dot_general(
-            act_x[x], g, (((0,), (0,)), ((), ())), preferred_element_type=jnp.float32
-        )
-
-    head = part(0)
-    mid = part(1) + part(2)
-    tail = part(3)
+    act_all, owners = xgather(act_mine.reshape(nj * tok, row_width), seq_ids)
     first_long = jnp.sum((owners < 1).astype(jnp.int32)) * (total // owners.size) > total // 2
-    g0 = jnp.where(first_long, head + mid, head)
-    g1 = jnp.where(first_long, tail, mid + tail)
-    fisher = g0 * g0 + g1 * g1
-    prior = fisher / SEQS + smoothing
-    w = weights[0].astype(jnp.float32)
-    both = prior[None] * jnp.stack([w, jnp.ones_like(w)], axis=0)
-    return mp_merge(both)
+    w_all = weights[0].astype(jnp.float32)
+    chunks = 2
+    width = col_width // chunks
+    merged = []
+    for k in range(chunks):
+        cols = slice(k * width, (k + 1) * width)
+        grad_all = lax.all_gather(grad_mine[..., cols], ("zh", "y"), axis=0, tiled=False)
+        if merged:
+            merged[-1], grad_all = lax.optimization_barrier((merged[-1], grad_all))
+
+        def part(x):
+            g = grad_all[:, x].reshape(nj * tok, width)
+            return lax.dot_general(
+                act_all[x], g, (((0,), (0,)), ((), ())), preferred_element_type=jnp.float32
+            )
+
+        head = part(0)
+        mid = part(1) + part(2)
+        tail = part(3)
+        g0 = jnp.where(first_long, head + mid, head)
+        g1 = jnp.where(first_long, tail, mid + tail)
+        fisher = g0 * g0 + g1 * g1
+        prior = fisher / SEQS + smoothing
+        w = w_all[:, cols]
+        both = prior[None] * jnp.stack([w, jnp.ones_like(w)], axis=0)
+        merged.append(mp_merge(both, 2 + k))
+    return jnp.concatenate(merged, axis=1)
 
 
 def solution(mesh):

time: 415 us -> 398 us (0.959)
  Pallas kernels: 193 us -> 246 us
  blocking collectives: 77.6 us -> 27.3 us
  waiting for transfers between devices: 63.4 us -> 39.3 us
  matrix products: 33.4 us -> 24.4 us
  starting transfers between devices: 0.01 us -> 7.55 us
  local copies, waits for them, and re-layouts: 20.5 us -> 24.8 us
    all_gather x1 -> x2, waiting for transfers between devices: 63.4 us -> 8.78 us  [per_device(): lax.all_gather(grad_mine[..., cols], ('zh', 'y'), axis=0, tiled=False)]
    all_to_all x1 -> x0, blocking collectives: 50.1 us -> none  [per_device(): act_mine = lax.all_to_all(act_blocks, ('zh', 'y'), 0, 0, tiled=True)]
    pallas_call x1 -> x2, Pallas kernels: 127 us -> 175 us  [mp_merge(): pl.pallas_call(mp_merge_kernel, out_shape=jax.ShapeDtypeStruct((rows, col...]
    all_to_all x0 -> x1, waiting for transfers between devices: none -> 30.5 us  [per_device(): act_mine = lax.all_to_all(act_blocks, ('zh', 'y'), 0, 0, tiled=True)]
    dot_general x4 -> x8, matrix products: 33.4 us -> 24.4 us  [part(): lax.dot_general(act_all[x], g, (((0,), (0,)), ((), ())), preferred_elemen...]
    all_to_all x0 -> x1, starting transfers between devices: none -> 7.5 us  [per_device(): act_mine = lax.all_to_all(act_blocks, ('zh', 'y'), 0, 0, tiled=True)]
    slice x1 -> x5, local copies, waits for them, and re-layouts: 5.93 us -> 10.9 us  [the longest x2 8.15 us: part(): g = grad_all[:, x].reshape(nj * tok, width)]
    mul x1 -> x2, other arithmetic: 10.6 us -> 6.88 us  [per_device(): both = prior[None] * jnp.stack([w, jnp.ones_like(w)], axis=0)]
  transfers between devices with their start and end apart: 1 -> 3, of which waited for: 1 -> 2; matrix products, arithmetic and copies ran while one was open for 1% -> 8% of each run, Pallas kernels for 16% -> 45%
where the time goes in v7:
time: 398 us
  Pallas kernels  246 us (62%)
  waiting for transfers between devices  39.3 us (10%)
  blocking collectives  27.3 us (7%)
  local copies, waits for them, and re-layouts  24.8 us (6%)
  matrix products  24.4 us (6%)
  other arithmetic  14.6 us (4%)
  between operations  14.2 us (4%)
  starting transfers between devices  7.55 us (2%)
    pallas_call x2, Pallas kernels, mp_merge(): pl.pallas_call(mp_merge_kernel, out_shape=jax.ShapeDtypeStruct((rows, col...  175 us
    pallas_call x1, Pallas kernels, xgather(): pl.pallas_call(xgather_kernel, out_shape=(jax.ShapeDtypeStruct((n, rows,...  70.2 us
    all_to_all x1, waiting for transfers between devices, per_device(): act_mine = lax.all_to_all(act_blocks, ('zh', 'y'), 0, 0, tiled=True)  30.5 us
    all_to_all x1, blocking collectives, per_device(): grad_mine = lax.all_to_all(grad_blocks, 'x', 0, 0, tiled=True)  27.3 us
    dot_general x8, matrix products, part(): lax.dot_general(act_all[x], g, (((0,), (0,)), ((), ())), preferred_elemen...  24.4 us
    all_gather x2, waiting for transfers between devices, per_device(): lax.all_gather(grad_mine[..., cols], ('zh', 'y'), axis=0, tiled=False)  8.78 us
    slice x2, local copies, waits for them, and re-layouts, part(): g = grad_all[:, x].reshape(nj * tok, width)  8.15 us
  transfers between devices with their start and end apart: 3, of which 2 were waited for; matrix products, arithmetic and copies ran while one was open for 8% of the time, Pallas kernels for 45%

profile of v7, /device:TPU:1, one launch (start us, length us, event | category | flops | bytes accessed | tf_op | source)
XLA Modules:
  0.0 397.8 jit_solution(5501685336355904099)
XLA Ops:
  6.5 0.0 all-gather.5.cloned.1.call-start
  6.5 3.3 copy.13
  9.8 27.3 %all_to_all.10 = bf16[4,128,1792]{1,2,0:T(8,128)(2,1)S(1)} all-to-all(bf16[4,128,1792]{1,2,0:T(8,128)(2,1)S(1)} %bitcast.64), channel_id=1, replica_groups=mesh['zl'=2,'c'=2,'x'=4,'zh'=2,'y'=4] {'x'}, dimensions={0} | all-to-all | bytes 3670016 | tf_op jit(solution)/shard_map/all_to_all | solution.py:314
  37.1 0.1 fusion.41
  37.2 1.3 copy.14
  38.5 0.0 copy-start.4
  38.5 0.0 all-gather.5.cloned.1.call-update
  38.5 0.0 all-gather.7.cloned.1.call-start
  38.6 1.3 copy.15
  39.9 0.0 all-gather.7.cloned.1.call-update
  39.9 0.5 copy-done.4
  40.4 1.4 copy.16
  41.8 2.5 copy.18
  44.3 7.5 %all-to-all-start = ((bf16[8,128,1024]{2,1,0:T(8,128)(2,1)}), bf16[8,128,1024]{2,1,0:T(8,128)(2,1)S(1)}, u32[]{:S(2)}, u32[]{:S(2)}) async-start(bf16[8,128,1024]{2,1,0:T(8,128)(2,1)} %bitcast.60), calls=%async_computation | async-start | bytes 4194304 | tf_op jit(solution)/shard_map/all_to_all | solution.py:312
  51.8 2.8 bitcast_convert_fusion
  54.6 3.5 slice_bitcast_fusion.1
  58.2 30.5 %all-to-all-done = bf16[8,128,1024]{2,1,0:T(8,128)(2,1)S(1)} async-done(((bf16[8,128,1024]{2,1,0:T(8,128)(2,1)}), bf16[8,128,1024]{2,1,0:T(8,128)(2,1)S(1)}, u32[]{:S(2)}, u32[]{:S(2)}) %all-to-all-start) | async-done | bytes 2097184 | tf_op jit(solution)/shard_map/all_to_all | solution.py:312
  88.7 1.3 copy-done.2
  90.0 70.2 %shard_map.46 = (bf16[4,1024,1024]{2,1,0:T(8,128)(2,1)}, s32[4,1,128]{2,1,0:T(1,128)}) custom-call(bf16[1024,1024]{1,0:T(8,128)(2,1)} %bitcast.59, s32[1,128]{1,0:T(1,128)} %seq_ref.1), custom_call_target="tpu_custom_call" | custom-call | bytes 16777216 | tf_op jit(solution)/shard_map/pallas_call | solution.py:198
  160.2 1.3 fusion.38
  162.0 0.0 all-gather.5.cloned.1.call-done
  162.1 0.0 copy-start.5
  162.1 4.1 %fusion.40 = (bf16[8,1,128,896]{3,2,1,0:T(8,128)(2,1)S(1)}, bf16[8,1,128,896]{3,2,1,0:T(8,128)(2,1)S(1)}, bf16[8,1,128,896]{3,2,1,0:T(8,128)(2,1)S(1)}, bf16[8,1,128,896]{3,2,1,0:T(8,128)(2,1)S(1)}) fusion(bf16[8,4,128,896]{3,2,1,0:T(8,128)(2,1)} %bitcast.63), kind=kLoop, calls=%fused_computation.48 | loop fusion | bytes 14680064 | tf_op jit(solution)/shard_map/slice | solution.py:328
  166.2 1.4 copy-done.5
  167.6 2.4 fusion.12
  170.0 2.4 fusion.16
  172.4 2.4 fusion.20
  174.8 0.0 copy-start.1
  174.9 3.3 fusion.3
  178.1 0.0 copy-done.1
  178.1 3.5 pad_multiply_fusion.1.both_ref
  181.6 107.4 %shard_map.47 = bf16[1024,896]{1,0:T(8,128)(2,1)} custom-call(f32[2,1024,896]{2,1,0:T(8,128)} %pad_multiply_fusion.1.both_ref), custom_call_target="tpu_custom_call" | custom-call | flops 3670016 | bytes 14680064 | tf_op jit(solution)/shard_map/pallas_call | solution.py:287
  289.0 8.8 %all-gather.7.cloned.1.call-done = bf16[32,128,896]{2,1,0:T(8,128)(2,1)} async-done(((bf16[4,128,896]{2,1,0:T(8,128)(2,1)}), bf16[32,128,896]{2,1,0:T(8,128)(2,1)}) %all-gather.7.cloned.1.call-update) | async-done | bytes 7340048 | tf_op jit(solution)/shard_map/all_gather | solution.py:323
  297.8 4.0 %fusion.39 = (bf16[8,1,128,896]{3,2,1,0:T(8,128)(2,1)S(1)}, bf16[8,1,128,896]{3,2,1,0:T(8,128)(2,1)S(1)}, bf16[8,1,128,896]{3,2,1,0:T(8,128)(2,1)S(1)}, bf16[8,1,128,896]{3,2,1,0:T(8,128)(2,1)S(1)}) fusion(bf16[8,4,128,896]{3,2,1,0:T(8,128)(2,1)} %bitcast.62), kind=kLoop, calls=%fused_computation.47 | loop fusion | bytes 14680064 | tf_op jit(solution)/shard_map/slice | solution.py:328
  301.8 0.0 slice-start
  301.8 4.2 %fusion.14 = f32[1024,896]{1,0:T(8,128)S(1)} fusion(bf16[1024,896]{1,0:T(8,128)(2,1)S(1)} %bitcast.73, bf16[4,1024,1024]{2,1,0:T(8,128)(2,1)} %get-tuple-element.10), kind=kOutput, calls=%fused_computation.24 | convolution fusion | flops 1879048192 | bytes 7602176 | tf_op jit(solution)/shard_map/dot_general | solution.py:329
  305.9 0.0 slice-start.1
  306.0 4.2 %fusion.18 = f32[1024,896]{1,0:T(8,128)S(1)} fusion(bf16[1024,896]{1,0:T(8,128)(2,1)S(1)} %bitcast.72, bf16[4,1024,1024]{2,1,0:T(8,128)(2,1)} %get-tuple-element.10), kind=kOutput, calls=%fused_computation.28 | convolution fusion | flops 1879048192 | bytes 7602176 | tf_op jit(solution)/shard_map/dot_general | solution.py:329
  310.1 0.0 slice-done
  310.1 0.0 slice-done.1
  310.2 2.4 fusion.10
  312.6 0.0 copy-start
  312.6 3.3 fusion.8
  315.8 0.0 copy-done
  315.8 3.4 pad_multiply_fusion.both_ref
  319.3 68.0 %shard_map.48 = bf16[1024,896]{1,0:T(8,128)(2,1)} custom-call(f32[2,1024,896]{2,1,0:T(8,128)} %pad_multiply_fusion.both_ref), custom_call_target="tpu_custom_call" | custom-call | flops 3670016 | bytes 14680064 | tf_op jit(solution)/shard_map/pallas_call | solution.py:287
  387.3 0.0 copy-done.3
  387.3 3.6 pad_maximum_fusion
  (3 shorter events, 0.0 us)
Async XLA Ops:
  6.5 155.5 %all-gather.5.cloned.1.call-start = ((), (), s32[]{:S(2)}) async-start(), calls=%async_computation.2 | async-start | bytes 8257536 | tf_op jit(solution)/shard_map/all_gather | solution.py:323
  38.5 1.9 copy-start.4
  38.5 259.2 %all-gather.7.cloned.1.call-start = ((), (), s32[]{:S(2)}) async-start(), calls=%async_computation.3 | async-start | bytes 8257536 | tf_op jit(solution)/shard_map/all_gather | solution.py:323
  44.3 44.4 %all-to-all-start = ((bf16[8,128,1024]{2,1,0:T(8,128)(2,1)}), bf16[8,128,1024]{2,1,0:T(8,128)(2,1)S(1)}, u32[]{:S(2)}, u32[]{:S(2)}) async-start(bf16[8,128,1024]{2,1,0:T(8,128)(2,1)} %bitcast.60), calls=%async_computation | async-start | bytes 4194304 | tf_op jit(solution)/shard_map/all_to_all | solution.py:312
  88.7 1.3 copy-start.2
  162.1 5.5 %copy-start.5 = (bf16[4,1024,1024]{2,1,0:T(8,128)(2,1)S(1)}, bf16[4,1024,1024]{2,1,0:T(8,128)(2,1)}, u32[]{:S(2)}) copy-start(bf16[4,1024,1024]{2,1,0:T(8,128)(2,1)} %get-tuple-element.10) | copy-start | bytes 25165828
  174.8 3.3 copy-start.1
  301.8 8.4 %slice-start = ((s8[8388608]{0:T(1024)(128)(4,1)}), s8[4194304]{0:T(1024)(128)(4,1)S(1)}, s32[]{:S(2)}) async-start(s8[8388608]{0:T(1024)(128)(4,1)} %bitcast.74), calls=%async_computation.4 | async-start | bytes 8388608
  305.9 4.2 %slice-start.1 = ((s8[8388608]{0:T(1024)(128)(4,1)}), s8[4194304]{0:T(1024)(128)(4,1)S(1)}, s32[]{:S(2)}) async-start(s8[8388608]{0:T(1024)(128)(4,1)} %bitcast.74), calls=%async_computation.5 | async-start | bytes 8388608
  312.6 3.3 copy-start
  319.3 68.1 %copy-start.3 = (bf16[1024,896]{1,0:T(8,128)(2,1)S(1)}, bf16[1024,896]{1,0:T(8,128)(2,1)}, u32[]{:S(2)}) copy-start(bf16[1024,896]{1,0:T(8,128)(2,1)} %shard_map.47) | copy-start | bytes 5505028
Sparse Core Ops, SparseCore 0:
  38.6 122.6 all-gather.4
  163.7 134.0 all-gather.6

commit v8 on v0

v8 whole, which is shorter than its diff:
```python
import functools

import jax
import jax.numpy as jnp
from jax import lax
from jax.experimental import pallas as pl
from jax.experimental.pallas import tpu as pltpu
from jax.sharding import PartitionSpec as P

F = 7168
SEQS = 2
MESH = pl.DeviceIdType.MESH

smoothing = 0.05


def mp_merge_kernel(prior_ref, w_ref, out_ref, recv_p, recv_w, recv1, recv2, send_sem, recv_sem):
    c = lax.axis_index("c")
    z = lax.axis_index("zl")
    rows = prior_ref.shape[0]
    half, quarter = rows // 2, rows // 4
    step = 32
    core = {"c": 1 - c}
    chip = {"zl": 1 - z}

    barrier = pltpu.get_barrier_semaphore()
    pl.semaphore_signal(barrier, 1, device_id=core, device_id_type=MESH)
    pl.semaphore_signal(barrier, 1, device_id=chip, device_id_type=MESH)
    pl.semaphore_wait(barrier, 2)

    mine = pl.multiple_of(c * half, half)
    other = pl.multiple_of((1 - c) * half, half)
    first = pltpu.make_async_remote_copy(
        src_ref=prior_ref.at[pl.ds(other, half)], dst_ref=recv_p,
        send_sem=send_sem.at[0], recv_sem=recv_sem.at[0], device_id=core, device_id_type=MESH)
    first_w = pltpu.make_async_remote_copy(
        src_ref=w_ref.at[pl.ds(other, half)], dst_ref=recv_w,
        send_sem=send_sem.at[4], recv_sem=recv_sem.at[4], device_id=core, device_id_type=MESH)
    first_w.start()
    first.start()
    first_w.wait_recv()
    first.wait_recv()

    def add_half(i, carry):
        r = pl.multiple_of(i * step, step)
        p_me = prior_ref[pl.ds(mine + r, step)]
        p_ot = recv_p[pl.ds(r, step)]
        n_me = p_me * w_ref[pl.ds(mine + r, step)].astype(jnp.float32)
        n_ot = p_ot * recv_w[pl.ds(r, step)].astype(jnp.float32)
        recv1[0, pl.ds(r, step)] = n_ot + n_me
        recv1[1, pl.ds(r, step)] = p_ot + p_me
        return carry

    lax.fori_loop(0, half // step, add_half, 0)

    my_q = pl.multiple_of(z * quarter, quarter)
    far_q = pl.multiple_of((1 - z) * quarter, quarter)
    second = pltpu.make_async_remote_copy(
        src_ref=recv1.at[:, pl.ds(far_q, quarter)], dst_ref=recv2,
        send_sem=send_sem.at[1], recv_sem=recv_sem.at[1], device_id=chip, device_id_type=MESH)
    second.start()
    second.wait_recv()

    def merge(i, carry):
        r = pl.multiple_of(i * step, step)
        n = recv1[0, pl.ds(my_q + r, step)] + recv2[0, pl.ds(r, step)]
        d = recv1[1, pl.ds(my_q + r, step)] + recv2[1, pl.ds(r, step)]
        out_ref[pl.ds(mine + my_q + r, step)] = (n / d).astype(out_ref.dtype)
        return carry

    lax.fori_loop(0, quarter // step, merge, 0)

    third = pltpu.make_async_remote_copy(
        src_ref=out_ref.at[pl.ds(mine + my_q, quarter)], dst_ref=out_ref.at[pl.ds(mine + my_q, quarter)],
        send_sem=send_sem.at[2], recv_sem=recv_sem.at[2], device_id=chip, device_id_type=MESH)
    third.start()
    pltpu.make_async_remote_copy(
        src_ref=out_ref.at[pl.ds(mine + far_q, quarter)], dst_ref=out_ref.at[pl.ds(mine + far_q, quarter)],
        send_sem=send_sem.at[2], recv_sem=recv_sem.at[2], device_id=chip, device_id_type=MESH).wait_recv()
    fourth = pltpu.make_async_remote_copy(
        src_ref=out_ref.at[pl.ds(mine, half)], dst_ref=out_ref.at[pl.ds(mine, half)],
        send_sem=send_sem.at[3], recv_sem=recv_sem.at[3], device_id=core, device_id_type=MESH)
    fourth.start()
    pltpu.make_async_remote_copy(
        src_ref=out_ref.at[pl.ds(other, half)], dst_ref=out_ref.at[pl.ds(other, half)],
        send_sem=send_sem.at[3], recv_sem=recv_sem.at[3], device_id=core, device_id_type=MESH).wait_recv()
    first.wait_send()
    first_w.wait_send()
    second.wait_send()
    third.wait_send()
    fourth.wait_send()


def mp_merge(prior, w, cid):
    rows, cols = prior.shape
    vmem = pltpu.MemorySpace.VMEM
    return pl.pallas_call(
        mp_merge_kernel,
        out_shape=jax.ShapeDtypeStruct((rows, cols), jnp.bfloat16),
        in_specs=[pl.BlockSpec(memory_space=vmem)] * 2,
        out_specs=pl.BlockSpec(memory_space=vmem),
        scratch_shapes=[
            pltpu.VMEM((rows // 2, cols), jnp.float32),
            pltpu.VMEM((rows // 2, cols), w.dtype),
            pltpu.VMEM((2, rows // 2, cols), jnp.float32),
            pltpu.VMEM((2, rows // 4, cols), jnp.float32),
            pltpu.SemaphoreType.DMA((5,)),
            pltpu.SemaphoreType.DMA((5,)),
        ],
        compiler_params=pltpu.CompilerParams(
            collective_id=cid, has_side_effects=True, vmem_limit_bytes=60 * 1024 * 1024),
        cost_estimate=pl.CostEstimate(flops=rows * cols * 6, bytes_accessed=rows * cols * 12, transcendentals=0),
    )(prior, w)


def ring_copies(axis, me, n, src, slot, sems, base):
    right, left = lax.rem(me + 1, n), lax.rem(me + n - 1, n)
    far = lax.rem(me + 2, n)
    send, recv = sems
    half = src.shape[0] // 2

    def rc(s, d, k, dev):
        return pltpu.make_async_remote_copy(
            src_ref=s, dst_ref=d, send_sem=send.at[base + k], recv_sem=recv.at[base + k],
            device_id={axis: dev}, device_id_type=MESH)

    whole = pl.ds(0, 2 * half)
    lo, hi = pl.ds(0, half), pl.ds(half, half)
    first = [rc(src, slot(me, whole), 0, right), rc(src, slot(me, whole), 1, left)]
    arrive = [rc(src, slot(left, whole), 0, left), rc(src, slot(right, whole), 1, right)]
    relay = [
        rc(slot(right, lo), slot(right, lo), 2, left),
        rc(slot(left, hi), slot(left, hi), 3, right),
    ]
    land = [
        rc(slot(far, lo), slot(far, lo), 2, right),
        rc(slot(far, hi), slot(far, hi), 3, left),
    ]
    return first, arrive, relay, land


def gather_kernel(act_in, grad_in, seq_ref, act_out, grad_out, seq_out, act_ref, grad_ref,
                  send, recv, local, seq_send, seq_recv, p0_send, p0_recv, q0_send, q0_recv):
    nx = 4
    ny = 4
    x = lax.axis_index("x")
    y = lax.axis_index("y")
    zh = lax.axis_index("zh")
    xr, xl = lax.rem(x + 1, nx), lax.rem(x + nx - 1, nx)
    yr, yl = lax.rem(y + 1, ny), lax.rem(y + ny - 1, ny)

    nj = 2 * ny
    j = zh * ny + y
    rw = act_ref.shape[2]
    cw = grad_ref.shape[2]

    def plane(jd):
        return {"zh": jd // ny, "y": lax.rem(jd, ny)}

    barrier = pltpu.get_barrier_semaphore()
    for s in range(1, nj):
        pl.semaphore_signal(barrier, 1, device_id=plane(lax.rem(j + s, nj)), device_id_type=MESH)
    for s in range(1, nx):
        pl.semaphore_signal(barrier, 1, device_id={"x": lax.rem(x + s, nx)}, device_id_type=MESH)
    pl.semaphore_wait(barrier, nj - 1 + nx - 1)

    def act_p0(s, jd, js):
        return pltpu.make_async_remote_copy(
            src_ref=act_in.at[:, pl.ds(pl.multiple_of(jd * rw, 128), rw)], dst_ref=act_ref.at[js],
            send_sem=p0_send.at[s], recv_sem=p0_recv.at[s], device_id=plane(jd),
            device_id_type=MESH)

    def grad_p0(s, xd, xs):
        return pltpu.make_async_remote_copy(
            src_ref=grad_in.at[:, pl.ds(pl.multiple_of(xd * cw, 128), cw)], dst_ref=grad_ref.at[xs],
            send_sem=q0_send.at[s], recv_sem=q0_recv.at[s], device_id={"x": xd},
            device_id_type=MESH)

    p0_out = [act_p0(s, lax.rem(j + s, nj), j) for s in range(1, nj)]
    p0_in = [act_p0(s, j, lax.rem(j + nj - s, nj)) for s in range(1, nj)]
    q0_out = [grad_p0(s, lax.rem(x + s, nx), x) for s in range(1, nx)]
    q0_in = [grad_p0(s, x, lax.rem(x + nx - s, nx)) for s in range(1, nx)]
    own0 = [
        pltpu.make_async_copy(
            act_in.at[:, pl.ds(pl.multiple_of(j * rw, 128), rw)], act_ref.at[j], local.at[3]),
        pltpu.make_async_copy(
            grad_in.at[:, pl.ds(pl.multiple_of(x * cw, 128), cw)], grad_ref.at[x], local.at[4]),
    ]
    for c in own0 + q0_out + p0_out:
        c.start()
    for c in q0_in:
        c.wait_recv()
    own0[1].wait()

    sems = (send, recv)
    a_first, a_arrive, a_relay, a_land = ring_copies(
        "x", x, nx, act_ref, lambda i, p: act_out.at[i, p], sems, 0)
    g_first, g_arrive, g_relay, g_land = ring_copies(
        "y", y, ny, grad_ref, lambda i, p: grad_out.at[p, zh, i], sems, 4)
    p_first, p_arrive, p_relay, p_land = ring_copies(
        "y", y, ny, grad_out.at[:, 1 - zh, y], lambda i, p: grad_out.at[p, 1 - zh, i], sems, 8)
    swap = pltpu.make_async_remote_copy(
        src_ref=grad_ref, dst_ref=grad_out.at[:, zh, y], send_sem=send.at[12],
        recv_sem=recv.at[12], device_id={"zh": 1 - zh}, device_id_type=MESH)
    swap_in = pltpu.make_async_remote_copy(
        src_ref=grad_ref, dst_ref=grad_out.at[:, 1 - zh, y], send_sem=send.at[12],
        recv_sem=recv.at[12], device_id={"zh": 1 - zh}, device_id_type=MESH)

    own = [
        pltpu.make_async_copy(act_ref, act_out.at[x], local.at[0]),
        pltpu.make_async_copy(grad_ref, grad_out.at[:, zh, y], local.at[1]),
        pltpu.make_async_copy(seq_ref, seq_out.at[x], local.at[2]),
    ]

    def sc(s, d, k, dev):
        return pltpu.make_async_remote_copy(
            src_ref=s, dst_ref=d, send_sem=seq_send.at[k], recv_sem=seq_recv.at[k],
            device_id={"x": dev}, device_id_type=MESH)

    seq_first = [sc(seq_ref, seq_out.at[x], 0, xr), sc(seq_ref, seq_out.at[x], 1, xl)]

    swap.start()
    for c in g_first + seq_first + [own[1], own[2]]:
        c.start()
    for c in p0_in:
        c.wait_recv()
    own0[0].wait()
    for c in a_first + [own[0]]:
        c.start()
    for c in a_arrive:
        c.wait_recv()
    sc(seq_ref, seq_out.at[xl], 0, xl).wait_recv()
    sc(seq_ref, seq_out.at[xr], 1, xr).wait_recv()
    seq_relay = sc(seq_out.at[xr], seq_out.at[xr], 2, xl)
    seq_relay.start()
    for c in a_relay:
        c.start()
    for c in g_arrive:
        c.wait_recv()
    for c in g_relay:
        c.start()
    swap_in.wait_recv()
    for c in p_first:
        c.start()
    for c in p_arrive:
        c.wait_recv()
    for c in p_relay:
        c.start()
    for c in a_land + g_land + p_land:
        c.wait_recv()
    sc(seq_out.at[lax.rem(x + 2, nx)], seq_out.at[lax.rem(x + 2, nx)], 2, xr).wait_recv()
    for c in a_first + a_relay + g_first + g_relay + p_first + p_relay + seq_first:
        c.wait_send()
    seq_relay.wait_send()
    swap.wait_send()
    for c in p0_out + q0_out:
        c.wait_send()
    for c in own:
        c.wait()


def gather_all(act, grad, seq, nj, nx, rw, cw):
    tok = act.shape[0]
    any_space = pl.BlockSpec(memory_space=pl.ANY)
    return pl.pallas_call(
        gather_kernel,
        out_shape=(
            jax.ShapeDtypeStruct((nx, nj, tok, rw), act.dtype),
            jax.ShapeDtypeStruct((nx, 2, nj // 2, tok, cw), grad.dtype),
            jax.ShapeDtypeStruct((nx,) + seq.shape, seq.dtype),
            jax.ShapeDtypeStruct((nj, tok, rw), act.dtype),
            jax.ShapeDtypeStruct((nx, tok, cw), grad.dtype),
        ),
        in_specs=[any_space] * 3,
        out_specs=(any_space,) * 5,
        scratch_shapes=[
            pltpu.SemaphoreType.DMA((13,)),
            pltpu.SemaphoreType.DMA((13,)),
            pltpu.SemaphoreType.DMA((5,)),
            pltpu.SemaphoreType.DMA((3,)),
            pltpu.SemaphoreType.DMA((3,)),
            pltpu.SemaphoreType.DMA((nj,)),
            pltpu.SemaphoreType.DMA((nj,)),
            pltpu.SemaphoreType.DMA((nx,)),
            pltpu.SemaphoreType.DMA((nx,)),
        ],
        compiler_params=pltpu.CompilerParams(collective_id=1, has_side_effects=True),
        cost_estimate=pl.CostEstimate(
            flops=0, bytes_accessed=8 * tok * (nj * rw + 2 * nx * cw), transcendentals=0),
    )(act, grad, seq)


def per_device(activations, out_grads, seq_ids, weights):
    nx = lax.axis_size("x")
    nj = lax.axis_size(("zh", "y"))
    tok = activations.shape[1]
    col_width = weights.shape[2]
    row_width = weights.shape[1]
    total = nx * nj * tok
    act_all, grad_all, owners, _, _ = gather_all(
        activations[0], out_grads[0], seq_ids, nj, nx, row_width, col_width)
    act_all = act_all.reshape(total, row_width)
    grad_all = grad_all.reshape(total, col_width)
    first_long = jnp.sum((owners < 1).astype(jnp.int32)) * (total // owners.size) > total // 2

    def part(lo, hi):
        return lax.dot_general(
            act_all[lo:hi], grad_all[lo:hi], (((0,), (0,)), ((), ())),
            preferred_element_type=jnp.float32,
        )

    quarter = total // 4
    head = part(0, quarter)
    mid = part(quarter, 3 * quarter)
    tail = part(3 * quarter, total)
    g0 = jnp.where(first_long, head + mid, head)
    g1 = jnp.where(first_long, tail, mid + tail)
    fisher = g0 * g0 + g1 * g1
    prior = fisher / SEQS + smoothing
    return mp_merge(prior, weights[0], 2)


def solution(mesh):
    assert mesh.shape["mp"] == 4 and mesh.shape["fsdp"] == 32
    fine = jax.sharding.Mesh(
        mesh.devices.reshape(2, 2, 4, 2, 4), ("zl", "c", "x", "zh", "y")
    )
    mp, fs = ("zl", "c"), ("x", "zh", "y")
    placed = (P(mp, fs, None), P(mp, fs, None), P(mp, fs), P(mp, fs, None))
    return jax.shard_map(
        per_device, mesh=fine, in_specs=placed, out_specs=P(fs, None), check_vma=False
    )
```

time: 852 us -> 335 us (0.39)
  waiting for transfers between devices: 429 us -> 0 us
  blocking collectives: 302 us -> 0 us
  Pallas kernels: 0 us -> 290 us
  starting transfers between devices: 24.8 us -> 0 us
  matrix products: 41.2 us -> 21.9 us
  other arithmetic: 20.2 us -> 1.34 us
  between operations: 13.4 us -> 0.73 us
    all_gather x1 -> x0, blocking collectives: 302 us -> none  [per_device(): owners = lax.all_gather(seq_ids[0], 'fsdp', axis=0, tiled=True)]
    pallas_call x0 -> x2, Pallas kernels: none -> 290 us  [the longest x1 166 us: gather_all(): pl.pallas_call(gather_kernel, out_shape=(jax.ShapeDtypeStruct((nx, nj, to...]
    psum x1 -> x0, waiting for transfers between devices: 281 us -> none  [per_device(): numer_sum, denom_sum = lax.psum((numer, prior), 'mp')]
    all_to_all x2 -> x0, waiting for transfers between devices: 148 us -> none  [the longest x1 148 us: per_device(): lax.all_to_all(act_send, 'fsdp', split_axis=0, concat_axis=1, tiled=True)[0]]
    all_to_all x2 -> x0, starting transfers between devices: 24.7 us -> none  [the longest x1 13.4 us: per_device(): lax.all_to_all(grad_send, 'fsdp', split_axis=0, concat_axis=1, tiled=True)]
    dot_general x2 -> x3, matrix products: 41.2 us -> 21.9 us  [part(): lax.dot_general(act_all[lo:hi], grad_all[lo:hi], (((0,), (0,)), ((), ()))...]
    slice x0 -> x4, local copies, waits for them, and re-layouts: none -> 14.6 us  [the longest x2 9.24 us: part(): grad_all[lo:hi]]
    add x1 -> x0, other arithmetic: 10.6 us -> none  [per_device(): prior = fisher / SEQS + smoothing]
  transfers between devices with their start and end apart: 3 -> 0, of which waited for: 2 -> 0; matrix products, arithmetic and copies ran while one was open for 1% -> 0% of each run, Pallas kernels for 0% -> 0%
where the time goes in v8:
time: 335 us; the launch traced here: 334 us
  Pallas kernels  290 us (87%)
  matrix products  21.9 us (7%)
  local copies, waits for them, and re-layouts  20.4 us (6%)
    pallas_call x1, Pallas kernels, gather_all(): pl.pallas_call(gather_kernel, out_shape=(jax.ShapeDtypeStruct((nx, nj, to...  166 us
    pallas_call x1, Pallas kernels, mp_merge(): pl.pallas_call(mp_merge_kernel, out_shape=jax.ShapeDtypeStruct((rows, col...  124 us
    dot_general x3, matrix products, part(): lax.dot_general(act_all[lo:hi], grad_all[lo:hi], (((0,), (0,)), ((), ()))...  21.9 us
    slice x2, local copies, waits for them, and re-layouts, part(): grad_all[lo:hi]  9.24 us

profile of v8, /device:TPU:1, one launch (start us, length us, event | category | flops | bytes accessed | tf_op | source)
XLA Modules:
  0.0 334.4 jit_solution(1899326083366831950)
XLA Ops:
  0.0 165.6 %shard_map.46 = (bf16[4,8,128,1024]{3,2,1,0:T(8,128)(2,1)}, bf16[4,2,4,128,1792]{4,3,2,1,0:T(8,128)(2,1)}, s32[4,1,128]{2,1,0:T(1,128)}, bf16[8,128,1024]{2,1,0:T(8,128)(2,1)}, bf16[4,128,1792]{2,1,0:T(8,128)(2,1)}) custom-call(bf16[128,8192]{1,0:T(8,128)(2,1)} %bitcast.20, bf16[128,7168]{1,0:T(8,128)(2,1)} %bitcast.23, s32[1,128]{1,0:T(1,128)} %seq_ref.1), custom_call_target="tpu_custom_call" | custom-call | bytes 23068672 | tf_op jit(solution)/shard_map/pallas_call | solution.py:265
  165.6 1.3 fusion.5
  167.6 0.0 copy-start
  167.6 2.9 slice.40
  170.6 1.7 copy-done
  172.3 2.4 fusion.7
  174.7 3.7 %slice.42 = bf16[2,2,4,128,1792]{4,3,2,1,0:T(8,128)(2,1)S(1)} slice(bf16[4,2,4,128,1792]{4,3,2,1,0:T(8,128)(2,1)} %get-tuple-element.10), slice={[1:3], [0:2], [0:4], [0:128], [0:1792]} | slice | bytes 14680064 | tf_op jit(solution)/shard_map/slice | solution.py:308
  178.4 5.5 %fusion.6 = (bf16[1,2,4,128,1792]{4,3,2,1,0:T(8,128)(2,1)}, bf16[1,2,4,128,1792]{4,3,2,1,0:T(8,128)(2,1)S(1)}) fusion(bf16[4,2,4,128,1792]{4,3,2,1,0:T(8,128)(2,1)} %get-tuple-element.10), kind=kLoop, calls=%fused_computation.9 | loop fusion | bytes 14680064 | tf_op jit(solution)/shard_map/slice | solution.py:308
  183.9 0.0 copy-start.1
  183.9 0.0 copy-start.3
  183.9 10.0 %fusion.8 = f32[1024,1792]{1,0:T(8,128)} fusion(bf16[2048,1024]{1,0:T(8,128)(2,1)S(1)} %bitcast.16, bf16[2048,1792]{1,0:T(8,128)(2,1)S(1)} %bitcast.15), kind=kOutput, calls=%fused_computation.11 | convolution fusion | flops 7516192768 | bytes 18874368 | tf_op jit(solution)/shard_map/dot_general | solution.py:307
  194.0 0.0 copy-done.1
  194.0 0.0 copy-done.3
  194.0 0.0 copy-start.2
  194.0 0.0 copy-start.4
  194.0 4.2 %fusion.9 = f32[1024,1792]{1,0:T(8,128)S(1)} fusion(bf16[1024,1024]{1,0:T(8,128)(2,1)S(1)} %bitcast.22, bf16[1024,1792]{1,0:T(8,128)(2,1)S(1)} %bitcast.19), kind=kOutput, calls=%fused_computation.12 | convolution fusion | flops 3758096384 | bytes 13107200 | tf_op jit(solution)/shard_map/dot_general | solution.py:307
  198.1 0.0 copy-done.2
  198.2 0.0 copy-done.4
  198.2 7.7 %fusion.3.prior_ref = f32[1024,1792]{1,0:T(8,128)} fusion(f32[1024,1792]{1,0:T(8,128)S(1)} %copy-done.4, f32[1024,1792]{1,0:T(8,128)S(1)} %fusion.9, pred[]{:T(512)S(6)} %gt.3, bf16[1024,1024]{1,0:T(8,128)(2,1)S(1)} %bitcast.21, bf16[1024,1792]{1,0:T(8,128)(2,1)S(1)} %bitcast.18), kind=kOutput, calls=%fused_computation.5 | convolution fusion | flops 3774611456 | bytes 27787264 | tf_op jit(solution)/shard_map/dot_general | solution.py:307
  205.9 124.3 %shard_map.47 = bf16[1024,1792]{1,0:T(8,128)(2,1)} custom-call(f32[1024,1792]{1,0:T(8,128)} %fusion.3.prior_ref, bf16[1024,1792]{1,0:T(8,128)(2,1)} %bitcast.17), custom_call_target="tpu_custom_call" | custom-call | flops 11010048 | bytes 22020096 | tf_op jit(solution)/shard_map/pallas_call | solution.py:97
  330.2 4.1 %copy.6 = bf16[1024,1792]{1,0:T(8,128)(2,1)} copy(bf16[1024,1792]{1,0:T(8,128)(2,1)} %shard_map.47) | data formatting | bytes 7340032
Async XLA Ops:
  167.6 4.6 %copy-start = (bf16[4,8,128,1024]{3,2,1,0:T(8,128)(2,1)S(1)}, bf16[4,8,128,1024]{3,2,1,0:T(8,128)(2,1)}, u32[]{:S(2)}) copy-start(bf16[4,8,128,1024]{3,2,1,0:T(8,128)(2,1)} %get-tuple-element.9) | copy-start | bytes 25165828
  183.9 10.1 %copy-start.1 = (bf16[1,2,4,128,1792]{4,3,2,1,0:T(8,128)(2,1)S(1)}, bf16[1,2,4,128,1792]{4,3,2,1,0:T(8,128)(2,1)}, u32[]{:S(2)}) copy-start(bf16[1,2,4,128,1792]{4,3,2,1,0:T(8,128)(2,1)} %get-tuple-element.11) | copy-start | bytes 11010052
  183.9 10.1 %copy-start.3 = (bf16[1,8,128,1024]{3,2,1,0:T(8,128)(2,1)S(1)}, bf16[1,8,128,1024]{3,2,1,0:T(8,128)(2,1)}, u32[]{:S(2)}) copy-start(bf16[1,8,128,1024]{3,2,1,0:T(8,128)(2,1)} %get-tuple-element.13) | copy-start | bytes 6291460
  194.0 4.2 %copy-start.2 = (bf16[1,8,128,1024]{3,2,1,0:T(8,128)(2,1)S(1)}, bf16[1,8,128,1024]{3,2,1,0:T(8,128)(2,1)}, u32[]{:S(2)}) copy-start(bf16[1,8,128,1024]{3,2,1,0:T(8,128)(2,1)} %get-tuple-element.14) | copy-start | bytes 6291460
  194.0 4.2 %copy-start.4 = (f32[1024,1792]{1,0:T(8,128)S(1)}, f32[1024,1792]{1,0:T(8,128)}, u32[]{:S(2)}) copy-start(f32[1024,1792]{1,0:T(8,128)} %fusion.8) | copy-start | bytes 22020100

commit v9 on v8

--- a/solution.py
+++ b/solution.py
@@ -140,7 +140,8 @@
 
 
 def gather_kernel(act_in, grad_in, seq_ref, act_out, grad_out, seq_out, act_ref, grad_ref,
-                  send, recv, local, seq_send, seq_recv, p0_send, p0_recv, q0_send, q0_recv):
+                  send, recv, local, seq_send, seq_recv, p0_send, p0_recv, q0_send, q0_recv,
+                  z0_send, z0_recv):
     nx = 4
     ny = 4
     x = lax.axis_index("x")
@@ -162,7 +163,9 @@
         pl.semaphore_signal(barrier, 1, device_id=plane(lax.rem(j + s, nj)), device_id_type=MESH)
     for s in range(1, nx):
         pl.semaphore_signal(barrier, 1, device_id={"x": lax.rem(x + s, nx)}, device_id_type=MESH)
-    pl.semaphore_wait(barrier, nj - 1 + nx - 1)
+        pl.semaphore_signal(
+            barrier, 1, device_id={"x": lax.rem(x + s, nx), "zh": 1 - zh}, device_id_type=MESH)
+    pl.semaphore_wait(barrier, nj - 1 + 2 * (nx - 1))
 
     def act_p0(s, jd, js):
         return pltpu.make_async_remote_copy(
@@ -176,6 +179,15 @@
             send_sem=q0_send.at[s], recv_sem=q0_recv.at[s], device_id={"x": xd},
             device_id_type=MESH)
 
+    def grad_z0(s, xd, xs, zs):
+        return pltpu.make_async_remote_copy(
+            src_ref=grad_in.at[:, pl.ds(pl.multiple_of(xd * cw, 128), cw)],
+            dst_ref=grad_out.at[xs, zs, y],
+            send_sem=z0_send.at[s], recv_sem=z0_recv.at[s],
+            device_id={"x": xd, "zh": 1 - zh}, device_id_type=MESH)
+
+    z0_out = [grad_z0(s, lax.rem(x + s, nx), x, zh) for s in range(nx)]
+    z0_in = [grad_z0(s, x, lax.rem(x + nx - s, nx), 1 - zh) for s in range(nx)]
     p0_out = [act_p0(s, lax.rem(j + s, nj), j) for s in range(1, nj)]
     p0_in = [act_p0(s, j, lax.rem(j + nj - s, nj)) for s in range(1, nj)]
     q0_out = [grad_p0(s, lax.rem(x + s, nx), x) for s in range(1, nx)]
@@ -186,7 +198,7 @@
         pltpu.make_async_copy(
             grad_in.at[:, pl.ds(pl.multiple_of(x * cw, 128), cw)], grad_ref.at[x], local.at[4]),
     ]
-    for c in own0 + q0_out + p0_out:
+    for c in z0_out + own0 + q0_out + p0_out:
         c.start()
     for c in q0_in:
         c.wait_recv()
@@ -199,12 +211,6 @@
         "y", y, ny, grad_ref, lambda i, p: grad_out.at[p, zh, i], sems, 4)
     p_first, p_arrive, p_relay, p_land = ring_copies(
         "y", y, ny, grad_out.at[:, 1 - zh, y], lambda i, p: grad_out.at[p, 1 - zh, i], sems, 8)
-    swap = pltpu.make_async_remote_copy(
-        src_ref=grad_ref, dst_ref=grad_out.at[:, zh, y], send_sem=send.at[12],
-        recv_sem=recv.at[12], device_id={"zh": 1 - zh}, device_id_type=MESH)
-    swap_in = pltpu.make_async_remote_copy(
-        src_ref=grad_ref, dst_ref=grad_out.at[:, 1 - zh, y], send_sem=send.at[12],
-        recv_sem=recv.at[12], device_id={"zh": 1 - zh}, device_id_type=MESH)
 
     own = [
         pltpu.make_async_copy(act_ref, act_out.at[x], local.at[0]),
@@ -219,7 +225,6 @@
 
     seq_first = [sc(seq_ref, seq_out.at[x], 0, xr), sc(seq_ref, seq_out.at[x], 1, xl)]
 
-    swap.start()
     for c in g_first + seq_first + [own[1], own[2]]:
         c.start()
     for c in p0_in:
@@ -239,7 +244,8 @@
         c.wait_recv()
     for c in g_relay:
         c.start()
-    swap_in.wait_recv()
+    for c in z0_in:
+        c.wait_recv()
     for c in p_first:
         c.start()
     for c in p_arrive:
@@ -252,8 +258,7 @@
     for c in a_first + a_relay + g_first + g_relay + p_first + p_relay + seq_first:
         c.wait_send()
     seq_relay.wait_send()
-    swap.wait_send()
-    for c in p0_out + q0_out:
+    for c in p0_out + q0_out + z0_out:
         c.wait_send()
     for c in own:
         c.wait()
@@ -283,6 +288,8 @@
             pltpu.SemaphoreType.DMA((nj,)),
             pltpu.SemaphoreType.DMA((nx,)),
             pltpu.SemaphoreType.DMA((nx,)),
+            pltpu.SemaphoreType.DMA((nx,)),
+            pltpu.SemaphoreType.DMA((nx,)),
         ],
         compiler_params=pltpu.CompilerParams(collective_id=1, has_side_effects=True),
         cost_estimate=pl.CostEstimate(

time: 335 us -> 381 us (1.14)
  Pallas kernels: 290 us -> 335 us
    pallas_call x1, Pallas kernels: 166 us -> 211 us  [gather_all(): pl.pallas_call(gather_kernel, out_shape=(jax.ShapeDtypeStruct((nx, nj, to...]
where the time goes in v9:
time: 381 us; the launch traced here: 379 us
  Pallas kernels  335 us (88%)
  matrix products  21.9 us (6%)
  local copies, waits for them, and re-layouts  20.4 us (5%)
    pallas_call x1, Pallas kernels, gather_all(): pl.pallas_call(gather_kernel, out_shape=(jax.ShapeDtypeStruct((nx, nj, to...  211 us
    pallas_call x1, Pallas kernels, mp_merge(): pl.pallas_call(mp_merge_kernel, out_shape=jax.ShapeDtypeStruct((rows, col...  124 us
    dot_general x3, matrix products, part(): lax.dot_general(act_all[lo:hi], grad_all[lo:hi], (((0,), (0,)), ((), ()))...  21.9 us
    slice x2, local copies, waits for them, and re-layouts, part(): grad_all[lo:hi]  9.24 us

profile of v9, /device:TPU:1, one launch (start us, length us, event | category | flops | bytes accessed | tf_op | source)
XLA Modules:
  0.0 379.2 jit_solution(17456048637889026715)
XLA Ops:
  0.0 210.8 %shard_map.46 = (bf16[4,8,128,1024]{3,2,1,0:T(8,128)(2,1)}, bf16[4,2,4,128,1792]{4,3,2,1,0:T(8,128)(2,1)}, s32[4,1,128]{2,1,0:T(1,128)}, bf16[8,128,1024]{2,1,0:T(8,128)(2,1)}, bf16[4,128,1792]{2,1,0:T(8,128)(2,1)}) custom-call(bf16[128,8192]{1,0:T(8,128)(2,1)} %bitcast.20, bf16[128,7168]{1,0:T(8,128)(2,1)} %bitcast.23, s32[1,128]{1,0:T(1,128)} %seq_ref.1), custom_call_target="tpu_custom_call" | custom-call | bytes 23068672 | tf_op jit(solution)/shard_map/pallas_call | solution.py:270
  210.9 1.3 fusion.5
  212.8 0.0 copy-start
  212.9 2.9 slice.40
  215.8 1.7 copy-done
  217.5 2.4 fusion.7
  219.9 3.7 slice.42
  223.7 5.5 %fusion.6 = (bf16[1,2,4,128,1792]{4,3,2,1,0:T(8,128)(2,1)}, bf16[1,2,4,128,1792]{4,3,2,1,0:T(8,128)(2,1)S(1)}) fusion(bf16[4,2,4,128,1792]{4,3,2,1,0:T(8,128)(2,1)} %get-tuple-element.10), kind=kLoop, calls=%fused_computation.9 | loop fusion | bytes 14680064 | tf_op jit(solution)/shard_map/slice | solution.py:315
  229.1 0.0 copy-start.1
  229.1 0.0 copy-start.3
  229.2 10.0 %fusion.8 = f32[1024,1792]{1,0:T(8,128)} fusion(bf16[2048,1024]{1,0:T(8,128)(2,1)S(1)} %bitcast.16, bf16[2048,1792]{1,0:T(8,128)(2,1)S(1)} %bitcast.15), kind=kOutput, calls=%fused_computation.11 | convolution fusion | flops 7516192768 | bytes 18874368 | tf_op jit(solution)/shard_map/dot_general | solution.py:314
  239.2 0.0 copy-done.1
  239.2 0.0 copy-done.3
  239.2 0.0 copy-start.2
  239.2 0.0 copy-start.4
  239.2 4.2 %fusion.9 = f32[1024,1792]{1,0:T(8,128)S(1)} fusion(bf16[1024,1024]{1,0:T(8,128)(2,1)S(1)} %bitcast.22, bf16[1024,1792]{1,0:T(8,128)(2,1)S(1)} %bitcast.19), kind=kOutput, calls=%fused_computation.12 | convolution fusion | flops 3758096384 | bytes 13107200 | tf_op jit(solution)/shard_map/dot_general | solution.py:314
  243.4 0.0 copy-done.2
  243.4 0.0 copy-done.4
  243.4 7.7 %fusion.3.prior_ref = f32[1024,1792]{1,0:T(8,128)} fusion(f32[1024,1792]{1,0:T(8,128)S(1)} %copy-done.4, f32[1024,1792]{1,0:T(8,128)S(1)} %fusion.9, pred[]{:T(512)S(6)} %gt.3, bf16[1024,1024]{1,0:T(8,128)(2,1)S(1)} %bitcast.21, bf16[1024,1792]{1,0:T(8,128)(2,1)S(1)} %bitcast.18), kind=kOutput, calls=%fused_computation.5 | convolution fusion | flops 3774611456 | bytes 27787264 | tf_op jit(solution)/shard_map/dot_general | solution.py:314
  251.1 123.9 %shard_map.47 = bf16[1024,1792]{1,0:T(8,128)(2,1)} custom-call(f32[1024,1792]{1,0:T(8,128)} %fusion.3.prior_ref, bf16[1024,1792]{1,0:T(8,128)(2,1)} %bitcast.17), custom_call_target="tpu_custom_call" | custom-call | flops 11010048 | bytes 22020096 | tf_op jit(solution)/shard_map/pallas_call | solution.py:97
  375.1 4.1 %copy.6 = bf16[1024,1792]{1,0:T(8,128)(2,1)} copy(bf16[1024,1792]{1,0:T(8,128)(2,1)} %shard_map.47) | data formatting | bytes 7340032
Async XLA Ops:
  212.8 4.6 %copy-start = (bf16[4,8,128,1024]{3,2,1,0:T(8,128)(2,1)S(1)}, bf16[4,8,128,1024]{3,2,1,0:T(8,128)(2,1)}, u32[]{:S(2)}) copy-start(bf16[4,8,128,1024]{3,2,1,0:T(8,128)(2,1)} %get-tuple-element.9) | copy-start | bytes 25165828
  229.1 10.1 %copy-start.1 = (bf16[1,2,4,128,1792]{4,3,2,1,0:T(8,128)(2,1)S(1)}, bf16[1,2,4,128,1792]{4,3,2,1,0:T(8,128)(2,1)}, u32[]{:S(2)}) copy-start(bf16[1,2,4,128,1792]{4,3,2,1,0:T(8,128)(2,1)} %get-tuple-element.11) | copy-start | bytes 11010052
  229.1 10.1 %copy-start.3 = (bf16[1,8,128,1024]{3,2,1,0:T(8,128)(2,1)S(1)}, bf16[1,8,128,1024]{3,2,1,0:T(8,128)(2,1)}, u32[]{:S(2)}) copy-start(bf16[1,8,128,1024]{3,2,1,0:T(8,128)(2,1)} %get-tuple-element.13) | copy-start | bytes 6291460
  239.2 4.2 %copy-start.2 = (bf16[1,8,128,1024]{3,2,1,0:T(8,128)(2,1)S(1)}, bf16[1,8,128,1024]{3,2,1,0:T(8,128)(2,1)}, u32[]{:S(2)}) copy-start(bf16[1,8,128,1024]{3,2,1,0:T(8,128)(2,1)} %get-tuple-element.14) | copy-start | bytes 6291460
  239.2 4.2 %copy-start.4 = (f32[1024,1792]{1,0:T(8,128)S(1)}, f32[1024,1792]{1,0:T(8,128)}, u32[]{:S(2)}) copy-start(f32[1024,1792]{1,0:T(8,128)} %fusion.8) | copy-start | bytes 22020100

commit v10 on v8

--- a/solution.py
+++ b/solution.py
@@ -14,11 +14,14 @@
 smoothing = 0.05
 
 
-def mp_merge_kernel(prior_ref, w_ref, out_ref, recv_p, recv_w, recv1, recv2, send_sem, recv_sem):
+def mp_merge_kernel(prior_ref, w_ref, out_ref, recv_p, recv_w, part, recv2,
+                    send_sem, recv_sem, s2_send, s2_recv, s3_send, s3_recv):
     c = lax.axis_index("c")
     z = lax.axis_index("zl")
     rows = prior_ref.shape[0]
     half, quarter = rows // 2, rows // 4
+    nb = s2_send.shape[0]
+    blk = quarter // nb
     step = 32
     core = {"c": 1 - c}
     chip = {"zl": 1 - z}
@@ -30,68 +33,89 @@
 
     mine = pl.multiple_of(c * half, half)
     other = pl.multiple_of((1 - c) * half, half)
-    first = pltpu.make_async_remote_copy(
-        src_ref=prior_ref.at[pl.ds(other, half)], dst_ref=recv_p,
-        send_sem=send_sem.at[0], recv_sem=recv_sem.at[0], device_id=core, device_id_type=MESH)
-    first_w = pltpu.make_async_remote_copy(
-        src_ref=w_ref.at[pl.ds(other, half)], dst_ref=recv_w,
-        send_sem=send_sem.at[4], recv_sem=recv_sem.at[4], device_id=core, device_id_type=MESH)
-    first_w.start()
-    first.start()
-    first_w.wait_recv()
-    first.wait_recv()
-
-    def add_half(i, carry):
-        r = pl.multiple_of(i * step, step)
-        p_me = prior_ref[pl.ds(mine + r, step)]
-        p_ot = recv_p[pl.ds(r, step)]
-        n_me = p_me * w_ref[pl.ds(mine + r, step)].astype(jnp.float32)
-        n_ot = p_ot * recv_w[pl.ds(r, step)].astype(jnp.float32)
-        recv1[0, pl.ds(r, step)] = n_ot + n_me
-        recv1[1, pl.ds(r, step)] = p_ot + p_me
-        return carry
-
-    lax.fori_loop(0, half // step, add_half, 0)
-
     my_q = pl.multiple_of(z * quarter, quarter)
     far_q = pl.multiple_of((1 - z) * quarter, quarter)
-    second = pltpu.make_async_remote_copy(
-        src_ref=recv1.at[:, pl.ds(far_q, quarter)], dst_ref=recv2,
-        send_sem=send_sem.at[1], recv_sem=recv_sem.at[1], device_id=chip, device_id_type=MESH)
-    second.start()
-    second.wait_recv()
-
-    def merge(i, carry):
-        r = pl.multiple_of(i * step, step)
-        n = recv1[0, pl.ds(my_q + r, step)] + recv2[0, pl.ds(r, step)]
-        d = recv1[1, pl.ds(my_q + r, step)] + recv2[1, pl.ds(r, step)]
-        out_ref[pl.ds(mine + my_q + r, step)] = (n / d).astype(out_ref.dtype)
-        return carry
-
-    lax.fori_loop(0, quarter // step, merge, 0)
-
-    third = pltpu.make_async_remote_copy(
-        src_ref=out_ref.at[pl.ds(mine + my_q, quarter)], dst_ref=out_ref.at[pl.ds(mine + my_q, quarter)],
-        send_sem=send_sem.at[2], recv_sem=recv_sem.at[2], device_id=chip, device_id_type=MESH)
-    third.start()
-    pltpu.make_async_remote_copy(
-        src_ref=out_ref.at[pl.ds(mine + far_q, quarter)], dst_ref=out_ref.at[pl.ds(mine + far_q, quarter)],
-        send_sem=send_sem.at[2], recv_sem=recv_sem.at[2], device_id=chip, device_id_type=MESH).wait_recv()
+
+    def onchip(k, q):
+        cp = pltpu.make_async_remote_copy(
+            src_ref=prior_ref.at[pl.ds(other + q, quarter)], dst_ref=recv_p.at[pl.ds(q, quarter)],
+            send_sem=send_sem.at[k], recv_sem=recv_sem.at[k], device_id=core, device_id_type=MESH)
+        cw = pltpu.make_async_remote_copy(
+            src_ref=w_ref.at[pl.ds(other + q, quarter)], dst_ref=recv_w.at[pl.ds(q, quarter)],
+            send_sem=send_sem.at[2 + k], recv_sem=recv_sem.at[2 + k], device_id=core,
+            device_id_type=MESH)
+        return [cw, cp]
+
+    far_in = onchip(0, far_q)
+    near_in = onchip(1, my_q)
+    for cp in far_in + near_in:
+        cp.start()
+
+    def add(lo, count):
+        def body(i, carry):
+            r = pl.multiple_of(lo + i * step, step)
+            p_me = prior_ref[pl.ds(mine + r, step)]
+            p_ot = recv_p[pl.ds(r, step)]
+            n_me = p_me * w_ref[pl.ds(mine + r, step)].astype(jnp.float32)
+            n_ot = p_ot * recv_w[pl.ds(r, step)].astype(jnp.float32)
+            part[0, pl.ds(r, step)] = n_ot + n_me
+            part[1, pl.ds(r, step)] = p_ot + p_me
+            return carry
+
+        lax.fori_loop(0, count // step, body, 0)
+
+    def second(b, lo):
+        return pltpu.make_async_remote_copy(
+            src_ref=part.at[:, pl.ds(lo + b * blk, blk)], dst_ref=recv2.at[:, pl.ds(b * blk, blk)],
+            send_sem=s2_send.at[b], recv_sem=s2_recv.at[b], device_id=chip, device_id_type=MESH)
+
+    def third(b, q):
+        rows_b = pl.ds(mine + q + b * blk, blk)
+        return pltpu.make_async_remote_copy(
+            src_ref=out_ref.at[rows_b], dst_ref=out_ref.at[rows_b],
+            send_sem=s3_send.at[b], recv_sem=s3_recv.at[b], device_id=chip, device_id_type=MESH)
+
+    for cp in far_in:
+        cp.wait_recv()
+    sent2 = []
+    for b in range(nb):
+        add(far_q + b * blk, blk)
+        cp = second(b, far_q)
+        cp.start()
+        sent2.append(cp)
+    for cp in near_in:
+        cp.wait_recv()
+    add(my_q, quarter)
+
+    sent3 = []
+    for b in range(nb):
+        second(b, my_q).wait_recv()
+
+        def merge(i, carry):
+            r = pl.multiple_of(b * blk + i * step, step)
+            n = part[0, pl.ds(my_q + r, step)] + recv2[0, pl.ds(r, step)]
+            d = part[1, pl.ds(my_q + r, step)] + recv2[1, pl.ds(r, step)]
+            out_ref[pl.ds(mine + my_q + r, step)] = (n / d).astype(out_ref.dtype)
+            return carry
+
+        lax.fori_loop(0, blk // step, merge, 0)
+        cp = third(b, my_q)
+        cp.start()
+        sent3.append(cp)
+    for b in range(nb):
+        third(b, far_q).wait_recv()
     fourth = pltpu.make_async_remote_copy(
         src_ref=out_ref.at[pl.ds(mine, half)], dst_ref=out_ref.at[pl.ds(mine, half)],
-        send_sem=send_sem.at[3], recv_sem=recv_sem.at[3], device_id=core, device_id_type=MESH)
+        send_sem=send_sem.at[4], recv_sem=recv_sem.at[4], device_id=core, device_id_type=MESH)
     fourth.start()
     pltpu.make_async_remote_copy(
         src_ref=out_ref.at[pl.ds(other, half)], dst_ref=out_ref.at[pl.ds(other, half)],
-        send_sem=send_sem.at[3], recv_sem=recv_sem.at[3], device_id=core, device_id_type=MESH).wait_recv()
-    first.wait_send()
-    first_w.wait_send()
-    second.wait_send()
-    third.wait_send()
-    fourth.wait_send()
-
-
-def mp_merge(prior, w, cid):
+        send_sem=send_sem.at[4], recv_sem=recv_sem.at[4], device_id=core, device_id_type=MESH).wait_recv()
+    for cp in far_in + near_in + sent2 + sent3 + [fourth]:
+        cp.wait_send()
+
+
+def mp_merge(prior, w, cid, blocks=4):
     rows, cols = prior.shape
     vmem = pltpu.MemorySpace.VMEM
     return pl.pallas_call(
@@ -106,6 +130,10 @@
             pltpu.VMEM((2, rows // 4, cols), jnp.float32),
             pltpu.SemaphoreType.DMA((5,)),
             pltpu.SemaphoreType.DMA((5,)),
+            pltpu.SemaphoreType.DMA((blocks,)),
+            pltpu.SemaphoreType.DMA((blocks,)),
+            pltpu.SemaphoreType.DMA((blocks,)),
+            pltpu.SemaphoreType.DMA((blocks,)),
         ],
         compiler_params=pltpu.CompilerParams(
             collective_id=cid, has_side_effects=True, vmem_limit_bytes=60 * 1024 * 1024),

time: 335 us -> 328 us (0.979)
  Pallas kernels: 290 us -> 283 us
    pallas_call x1, Pallas kernels: 124 us -> 117 us  [mp_merge(): pl.pallas_call(mp_merge_kernel, out_shape=jax.ShapeDtypeStruct((rows, col...]
where the time goes in v10:
time: 328 us; the launch traced here: 327 us
  Pallas kernels  283 us (86%)
  matrix products  21.9 us (7%)
  local copies, waits for them, and re-layouts  20.4 us (6%)
    pallas_call x1, Pallas kernels, gather_all(): pl.pallas_call(gather_kernel, out_shape=(jax.ShapeDtypeStruct((nx, nj, to...  166 us
    pallas_call x1, Pallas kernels, mp_merge(): pl.pallas_call(mp_merge_kernel, out_shape=jax.ShapeDtypeStruct((rows, col...  117 us
    dot_general x3, matrix products, part(): lax.dot_general(act_all[lo:hi], grad_all[lo:hi], (((0,), (0,)), ((), ()))...  21.9 us
    slice x2, local copies, waits for them, and re-layouts, part(): grad_all[lo:hi]  9.24 us

profile of v10, /device:TPU:1, one launch (start us, length us, event | category | flops | bytes accessed | tf_op | source)
XLA Modules:
  0.0 327.4 jit_solution(13358379080768827195)
XLA Ops:
  0.0 165.6 %shard_map.46 = (bf16[4,8,128,1024]{3,2,1,0:T(8,128)(2,1)}, bf16[4,2,4,128,1792]{4,3,2,1,0:T(8,128)(2,1)}, s32[4,1,128]{2,1,0:T(1,128)}, bf16[8,128,1024]{2,1,0:T(8,128)(2,1)}, bf16[4,128,1792]{2,1,0:T(8,128)(2,1)}) custom-call(bf16[128,8192]{1,0:T(8,128)(2,1)} %bitcast.20, bf16[128,7168]{1,0:T(8,128)(2,1)} %bitcast.23, s32[1,128]{1,0:T(1,128)} %seq_ref.1), custom_call_target="tpu_custom_call" | custom-call | bytes 23068672 | tf_op jit(solution)/shard_map/pallas_call | solution.py:293
  165.6 1.3 fusion.5
  167.6 0.0 copy-start
  167.6 2.9 slice.40
  170.6 1.7 copy-done
  172.3 2.4 fusion.7
  174.7 3.7 %slice.42 = bf16[2,2,4,128,1792]{4,3,2,1,0:T(8,128)(2,1)S(1)} slice(bf16[4,2,4,128,1792]{4,3,2,1,0:T(8,128)(2,1)} %get-tuple-element.10), slice={[1:3], [0:2], [0:4], [0:128], [0:1792]} | slice | bytes 14680064 | tf_op jit(solution)/shard_map/slice | solution.py:336
  178.4 5.5 %fusion.6 = (bf16[1,2,4,128,1792]{4,3,2,1,0:T(8,128)(2,1)}, bf16[1,2,4,128,1792]{4,3,2,1,0:T(8,128)(2,1)S(1)}) fusion(bf16[4,2,4,128,1792]{4,3,2,1,0:T(8,128)(2,1)} %get-tuple-element.10), kind=kLoop, calls=%fused_computation.9 | loop fusion | bytes 14680064 | tf_op jit(solution)/shard_map/slice | solution.py:336
  183.9 0.0 copy-start.1
  183.9 0.0 copy-start.3
  183.9 10.0 %fusion.8 = f32[1024,1792]{1,0:T(8,128)} fusion(bf16[2048,1024]{1,0:T(8,128)(2,1)S(1)} %bitcast.16, bf16[2048,1792]{1,0:T(8,128)(2,1)S(1)} %bitcast.15), kind=kOutput, calls=%fused_computation.11 | convolution fusion | flops 7516192768 | bytes 18874368 | tf_op jit(solution)/shard_map/dot_general | solution.py:335
  194.0 0.0 copy-done.1
  194.0 0.0 copy-done.3
  194.0 0.0 copy-start.2
  194.0 0.0 copy-start.4
  194.0 4.2 %fusion.9 = f32[1024,1792]{1,0:T(8,128)S(1)} fusion(bf16[1024,1024]{1,0:T(8,128)(2,1)S(1)} %bitcast.22, bf16[1024,1792]{1,0:T(8,128)(2,1)S(1)} %bitcast.19), kind=kOutput, calls=%fused_computation.12 | convolution fusion | flops 3758096384 | bytes 13107200 | tf_op jit(solution)/shard_map/dot_general | solution.py:335
  198.1 0.0 copy-done.2
  198.2 0.0 copy-done.4
  198.2 7.7 %fusion.3.prior_ref = f32[1024,1792]{1,0:T(8,128)} fusion(f32[1024,1792]{1,0:T(8,128)S(1)} %copy-done.4, f32[1024,1792]{1,0:T(8,128)S(1)} %fusion.9, pred[]{:T(512)S(6)} %gt.3, bf16[1024,1024]{1,0:T(8,128)(2,1)S(1)} %bitcast.21, bf16[1024,1792]{1,0:T(8,128)(2,1)S(1)} %bitcast.18), kind=kOutput, calls=%fused_computation.5 | convolution fusion | flops 3774611456 | bytes 27787264 | tf_op jit(solution)/shard_map/dot_general | solution.py:335
  205.9 117.4 %shard_map.47 = bf16[1024,1792]{1,0:T(8,128)(2,1)} custom-call(f32[1024,1792]{1,0:T(8,128)} %fusion.3.prior_ref, bf16[1024,1792]{1,0:T(8,128)(2,1)} %bitcast.17), custom_call_target="tpu_custom_call" | custom-call | flops 11010048 | bytes 22020096 | tf_op jit(solution)/shard_map/pallas_call | solution.py:121
  323.3 4.1 %copy.6 = bf16[1024,1792]{1,0:T(8,128)(2,1)} copy(bf16[1024,1792]{1,0:T(8,128)(2,1)} %shard_map.47) | data formatting | bytes 7340032
Async XLA Ops:
  167.6 4.6 %copy-start = (bf16[4,8,128,1024]{3,2,1,0:T(8,128)(2,1)S(1)}, bf16[4,8,128,1024]{3,2,1,0:T(8,128)(2,1)}, u32[]{:S(2)}) copy-start(bf16[4,8,128,1024]{3,2,1,0:T(8,128)(2,1)} %get-tuple-element.9) | copy-start | bytes 25165828
  183.9 10.1 %copy-start.1 = (bf16[1,2,4,128,1792]{4,3,2,1,0:T(8,128)(2,1)S(1)}, bf16[1,2,4,128,1792]{4,3,2,1,0:T(8,128)(2,1)}, u32[]{:S(2)}) copy-start(bf16[1,2,4,128,1792]{4,3,2,1,0:T(8,128)(2,1)} %get-tuple-element.11) | copy-start | bytes 11010052
  183.9 10.1 %copy-start.3 = (bf16[1,8,128,1024]{3,2,1,0:T(8,128)(2,1)S(1)}, bf16[1,8,128,1024]{3,2,1,0:T(8,128)(2,1)}, u32[]{:S(2)}) copy-start(bf16[1,8,128,1024]{3,2,1,0:T(8,128)(2,1)} %get-tuple-element.13) | copy-start | bytes 6291460
  194.0 4.2 %copy-start.2 = (bf16[1,8,128,1024]{3,2,1,0:T(8,128)(2,1)S(1)}, bf16[1,8,128,1024]{3,2,1,0:T(8,128)(2,1)}, u32[]{:S(2)}) copy-start(bf16[1,8,128,1024]{3,2,1,0:T(8,128)(2,1)} %get-tuple-element.14) | copy-start | bytes 6291460
  194.0 4.2 %copy-start.4 = (f32[1024,1792]{1,0:T(8,128)S(1)}, f32[1024,1792]{1,0:T(8,128)}, u32[]{:S(2)}) copy-start(f32[1024,1792]{1,0:T(8,128)} %fusion.8) | copy-start | bytes 22020100

commit v11 on v10

--- a/solution.py
+++ b/solution.py
@@ -168,7 +168,8 @@
 
 
 def gather_kernel(act_in, grad_in, seq_ref, act_out, grad_out, seq_out, act_ref, grad_ref,
-                  send, recv, local, seq_send, seq_recv, p0_send, p0_recv, q0_send, q0_recv):
+                  send, recv, local, seq_send, seq_recv, p0_send, p0_recv, q0_send, q0_recv,
+                  z_send, z_recv):
     nx = 4
     ny = 4
     x = lax.axis_index("x")
@@ -214,10 +215,23 @@
         pltpu.make_async_copy(
             grad_in.at[:, pl.ds(pl.multiple_of(x * cw, 128), cw)], grad_ref.at[x], local.at[4]),
     ]
+    def zs(s, src_block, xs, zs_):
+        return pltpu.make_async_remote_copy(
+            src_ref=src_block, dst_ref=grad_out.at[xs, zs_, y], send_sem=z_send.at[s],
+            recv_sem=z_recv.at[s], device_id={"zh": 1 - zh}, device_id_type=MESH)
+
+    own_cols = grad_in.at[:, pl.ds(pl.multiple_of(x * cw, 128), cw)]
+    swap_out = [zs(0, own_cols, x, zh)]
+    swap_in = [zs(s, own_cols, lax.rem(x + nx - s, nx), 1 - zh) for s in range(nx)]
+    swap_out[0].start()
     for c in own0 + q0_out + p0_out:
         c.start()
-    for c in q0_in:
-        c.wait_recv()
+    for s, c in enumerate(q0_in, start=1):
+        c.wait_recv()
+        xs = lax.rem(x + nx - s, nx)
+        piece = zs(s, grad_ref.at[xs], xs, zh)
+        piece.start()
+        swap_out.append(piece)
     own0[1].wait()
 
     sems = (send, recv)
@@ -227,12 +241,6 @@
         "y", y, ny, grad_ref, lambda i, p: grad_out.at[p, zh, i], sems, 4)
     p_first, p_arrive, p_relay, p_land = ring_copies(
         "y", y, ny, grad_out.at[:, 1 - zh, y], lambda i, p: grad_out.at[p, 1 - zh, i], sems, 8)
-    swap = pltpu.make_async_remote_copy(
-        src_ref=grad_ref, dst_ref=grad_out.at[:, zh, y], send_sem=send.at[12],
-        recv_sem=recv.at[12], device_id={"zh": 1 - zh}, device_id_type=MESH)
-    swap_in = pltpu.make_async_remote_copy(
-        src_ref=grad_ref, dst_ref=grad_out.at[:, 1 - zh, y], send_sem=send.at[12],
-        recv_sem=recv.at[12], device_id={"zh": 1 - zh}, device_id_type=MESH)
 
     own = [
         pltpu.make_async_copy(act_ref, act_out.at[x], local.at[0]),
@@ -247,7 +255,6 @@
 
     seq_first = [sc(seq_ref, seq_out.at[x], 0, xr), sc(seq_ref, seq_out.at[x], 1, xl)]
 
-    swap.start()
     for c in g_first + seq_first + [own[1], own[2]]:
         c.start()
     for c in p0_in:
@@ -267,7 +274,8 @@
         c.wait_recv()
     for c in g_relay:
         c.start()
-    swap_in.wait_recv()
+    for c in swap_in:
+        c.wait_recv()
     for c in p_first:
         c.start()
     for c in p_arrive:
@@ -280,7 +288,8 @@
     for c in a_first + a_relay + g_first + g_relay + p_first + p_relay + seq_first:
         c.wait_send()
     seq_relay.wait_send()
-    swap.wait_send()
+    for c in swap_out:
+        c.wait_send()
     for c in p0_out + q0_out:
         c.wait_send()
     for c in own:
@@ -311,6 +320,8 @@
             pltpu.SemaphoreType.DMA((nj,)),
             pltpu.SemaphoreType.DMA((nx,)),
             pltpu.SemaphoreType.DMA((nx,)),
+            pltpu.SemaphoreType.DMA((nx,)),
+            pltpu.SemaphoreType.DMA((nx,)),
         ],
         compiler_params=pltpu.CompilerParams(collective_id=1, has_side_effects=True),
         cost_estimate=pl.CostEstimate(

time: 328 us -> 331 us (level)
  no operation moved by 1% of the time
where the time goes in v11:
time: 331 us; the launch traced here: 330 us
  Pallas kernels  286 us (86%)
  matrix products  21.9 us (7%)
  local copies, waits for them, and re-layouts  20.4 us (6%)
    pallas_call x1, Pallas kernels, gather_all(): pl.pallas_call(gather_kernel, out_shape=(jax.ShapeDtypeStruct((nx, nj, to...  169 us
    pallas_call x1, Pallas kernels, mp_merge(): pl.pallas_call(mp_merge_kernel, out_shape=jax.ShapeDtypeStruct((rows, col...  117 us
    dot_general x3, matrix products, part(): lax.dot_general(act_all[lo:hi], grad_all[lo:hi], (((0,), (0,)), ((), ()))...  21.9 us
    slice x2, local copies, waits for them, and re-layouts, part(): grad_all[lo:hi]  9.24 us

profile of v11, /device:TPU:1, one launch (start us, length us, event | category | flops | bytes accessed | tf_op | source)
XLA Modules:
  0.0 330.3 jit_solution(9475089768954845434)
XLA Ops:
  0.0 168.5 %shard_map.46 = (bf16[4,8,128,1024]{3,2,1,0:T(8,128)(2,1)}, bf16[4,2,4,128,1792]{4,3,2,1,0:T(8,128)(2,1)}, s32[4,1,128]{2,1,0:T(1,128)}, bf16[8,128,1024]{2,1,0:T(8,128)(2,1)}, bf16[4,128,1792]{2,1,0:T(8,128)(2,1)}) custom-call(bf16[128,8192]{1,0:T(8,128)(2,1)} %bitcast.20, bf16[128,7168]{1,0:T(8,128)(2,1)} %bitcast.23, s32[1,128]{1,0:T(1,128)} %seq_ref.1), custom_call_target="tpu_custom_call" | custom-call | bytes 23068672 | tf_op jit(solution)/shard_map/pallas_call | solution.py:302
  168.5 1.3 fusion.5
  170.5 0.0 copy-start
  170.5 2.9 slice.40
  173.5 1.7 copy-done
  175.2 2.4 fusion.7
  177.6 3.7 %slice.42 = bf16[2,2,4,128,1792]{4,3,2,1,0:T(8,128)(2,1)S(1)} slice(bf16[4,2,4,128,1792]{4,3,2,1,0:T(8,128)(2,1)} %get-tuple-element.10), slice={[1:3], [0:2], [0:4], [0:128], [0:1792]} | slice | bytes 14680064 | tf_op jit(solution)/shard_map/slice | solution.py:347
  181.3 5.5 %fusion.6 = (bf16[1,2,4,128,1792]{4,3,2,1,0:T(8,128)(2,1)}, bf16[1,2,4,128,1792]{4,3,2,1,0:T(8,128)(2,1)S(1)}) fusion(bf16[4,2,4,128,1792]{4,3,2,1,0:T(8,128)(2,1)} %get-tuple-element.10), kind=kLoop, calls=%fused_computation.9 | loop fusion | bytes 14680064 | tf_op jit(solution)/shard_map/slice | solution.py:347
  186.8 0.0 copy-start.1
  186.8 0.0 copy-start.3
  186.8 10.0 %fusion.8 = f32[1024,1792]{1,0:T(8,128)} fusion(bf16[2048,1024]{1,0:T(8,128)(2,1)S(1)} %bitcast.16, bf16[2048,1792]{1,0:T(8,128)(2,1)S(1)} %bitcast.15), kind=kOutput, calls=%fused_computation.11 | convolution fusion | flops 7516192768 | bytes 18874368 | tf_op jit(solution)/shard_map/dot_general | solution.py:346
  196.9 0.0 copy-done.1
  196.9 0.0 copy-done.3
  196.9 0.0 copy-start.2
  196.9 0.0 copy-start.4
  196.9 4.2 %fusion.9 = f32[1024,1792]{1,0:T(8,128)S(1)} fusion(bf16[1024,1024]{1,0:T(8,128)(2,1)S(1)} %bitcast.22, bf16[1024,1792]{1,0:T(8,128)(2,1)S(1)} %bitcast.19), kind=kOutput, calls=%fused_computation.12 | convolution fusion | flops 3758096384 | bytes 13107200 | tf_op jit(solution)/shard_map/dot_general | solution.py:346
  201.1 0.0 copy-done.2
  201.1 0.0 copy-done.4
  201.1 7.7 %fusion.3.prior_ref = f32[1024,1792]{1,0:T(8,128)} fusion(f32[1024,1792]{1,0:T(8,128)S(1)} %copy-done.4, f32[1024,1792]{1,0:T(8,128)S(1)} %fusion.9, pred[]{:T(512)S(6)} %gt.3, bf16[1024,1024]{1,0:T(8,128)(2,1)S(1)} %bitcast.21, bf16[1024,1792]{1,0:T(8,128)(2,1)S(1)} %bitcast.18), kind=kOutput, calls=%fused_computation.5 | convolution fusion | flops 3774611456 | bytes 27787264 | tf_op jit(solution)/shard_map/dot_general | solution.py:346
  208.8 117.4 %shard_map.47 = bf16[1024,1792]{1,0:T(8,128)(2,1)} custom-call(f32[1024,1792]{1,0:T(8,128)} %fusion.3.prior_ref, bf16[1024,1792]{1,0:T(8,128)(2,1)} %bitcast.17), custom_call_target="tpu_custom_call" | custom-call | flops 11010048 | bytes 22020096 | tf_op jit(solution)/shard_map/pallas_call | solution.py:121
  326.2 4.1 %copy.6 = bf16[1024,1792]{1,0:T(8,128)(2,1)} copy(bf16[1024,1792]{1,0:T(8,128)(2,1)} %shard_map.47) | data formatting | bytes 7340032
Async XLA Ops:
  170.5 4.6 %copy-start = (bf16[4,8,128,1024]{3,2,1,0:T(8,128)(2,1)S(1)}, bf16[4,8,128,1024]{3,2,1,0:T(8,128)(2,1)}, u32[]{:S(2)}) copy-start(bf16[4,8,128,1024]{3,2,1,0:T(8,128)(2,1)} %get-tuple-element.9) | copy-start | bytes 25165828
  186.8 10.1 %copy-start.1 = (bf16[1,2,4,128,1792]{4,3,2,1,0:T(8,128)(2,1)S(1)}, bf16[1,2,4,128,1792]{4,3,2,1,0:T(8,128)(2,1)}, u32[]{:S(2)}) copy-start(bf16[1,2,4,128,1792]{4,3,2,1,0:T(8,128)(2,1)} %get-tuple-element.11) | copy-start | bytes 11010052
  186.8 10.1 %copy-start.3 = (bf16[1,8,128,1024]{3,2,1,0:T(8,128)(2,1)S(1)}, bf16[1,8,128,1024]{3,2,1,0:T(8,128)(2,1)}, u32[]{:S(2)}) copy-start(bf16[1,8,128,1024]{3,2,1,0:T(8,128)(2,1)} %get-tuple-element.13) | copy-start | bytes 6291460
  196.9 4.2 %copy-start.2 = (bf16[1,8,128,1024]{3,2,1,0:T(8,128)(2,1)S(1)}, bf16[1,8,128,1024]{3,2,1,0:T(8,128)(2,1)}, u32[]{:S(2)}) copy-start(bf16[1,8,128,1024]{3,2,1,0:T(8,128)(2,1)} %get-tuple-element.14) | copy-start | bytes 6291460
  196.9 4.2 %copy-start.4 = (f32[1024,1792]{1,0:T(8,128)S(1)}, f32[1024,1792]{1,0:T(8,128)}, u32[]{:S(2)}) copy-start(f32[1024,1792]{1,0:T(8,128)} %fusion.8) | copy-start | bytes 22020100

commit v12 on v10

--- a/solution.py
+++ b/solution.py
@@ -15,7 +15,7 @@
 
 
 def mp_merge_kernel(prior_ref, w_ref, out_ref, recv_p, recv_w, part, recv2,
-                    send_sem, recv_sem, s2_send, s2_recv, s3_send, s3_recv):
+                    send_sem, recv_sem, s2_send, s2_recv, s3_send, s3_recv, f_send, f_recv):
     c = lax.axis_index("c")
     z = lax.axis_index("zl")
     rows = prior_ref.shape[0]
@@ -46,9 +46,23 @@
             device_id_type=MESH)
         return [cw, cp]
 
-    far_in = onchip(0, far_q)
+    def onchip_block(b):
+        rows_b = pl.ds(far_q + b * blk, blk)
+        cp = pltpu.make_async_remote_copy(
+            src_ref=prior_ref.at[pl.ds(other + far_q + b * blk, blk)], dst_ref=recv_p.at[rows_b],
+            send_sem=f_send.at[b], recv_sem=f_recv.at[b], device_id=core, device_id_type=MESH)
+        cw = pltpu.make_async_remote_copy(
+            src_ref=w_ref.at[pl.ds(other + far_q + b * blk, blk)], dst_ref=recv_w.at[rows_b],
+            send_sem=f_send.at[nb + b], recv_sem=f_recv.at[nb + b], device_id=core,
+            device_id_type=MESH)
+        return [cw, cp]
+
+    far_in = [onchip_block(b) for b in range(nb)]
     near_in = onchip(1, my_q)
-    for cp in far_in + near_in:
+    for pair in far_in:
+        for cp in pair:
+            cp.start()
+    for cp in near_in:
         cp.start()
 
     def add(lo, count):
@@ -75,10 +89,10 @@
             src_ref=out_ref.at[rows_b], dst_ref=out_ref.at[rows_b],
             send_sem=s3_send.at[b], recv_sem=s3_recv.at[b], device_id=chip, device_id_type=MESH)
 
-    for cp in far_in:
-        cp.wait_recv()
     sent2 = []
     for b in range(nb):
+        for cp in far_in[b]:
+            cp.wait_recv()
         add(far_q + b * blk, blk)
         cp = second(b, far_q)
         cp.start()
@@ -111,11 +125,11 @@
     pltpu.make_async_remote_copy(
         src_ref=out_ref.at[pl.ds(other, half)], dst_ref=out_ref.at[pl.ds(other, half)],
         send_sem=send_sem.at[4], recv_sem=recv_sem.at[4], device_id=core, device_id_type=MESH).wait_recv()
-    for cp in far_in + near_in + sent2 + sent3 + [fourth]:
+    for cp in sum(far_in, []) + near_in + sent2 + sent3 + [fourth]:
         cp.wait_send()
 
 
-def mp_merge(prior, w, cid, blocks=4):
+def mp_merge(prior, w, cid, blocks=8):
     rows, cols = prior.shape
     vmem = pltpu.MemorySpace.VMEM
     return pl.pallas_call(
@@ -134,6 +148,8 @@
             pltpu.SemaphoreType.DMA((blocks,)),
             pltpu.SemaphoreType.DMA((blocks,)),
             pltpu.SemaphoreType.DMA((blocks,)),
+            pltpu.SemaphoreType.DMA((2 * blocks,)),
+            pltpu.SemaphoreType.DMA((2 * blocks,)),
         ],
         compiler_params=pltpu.CompilerParams(
             collective_id=cid, has_side_effects=True, vmem_limit_bytes=60 * 1024 * 1024),

time: 328 us -> 325 us (level)
  no operation moved by 1% of the time
where the time goes in v12:
time: 325 us; the launch traced here: 324 us
  Pallas kernels  280 us (86%)
  matrix products  21.9 us (7%)
  local copies, waits for them, and re-layouts  20.4 us (6%)
    pallas_call x1, Pallas kernels, gather_all(): pl.pallas_call(gather_kernel, out_shape=(jax.ShapeDtypeStruct((nx, nj, to...  166 us
    pallas_call x1, Pallas kernels, mp_merge(): pl.pallas_call(mp_merge_kernel, out_shape=jax.ShapeDtypeStruct((rows, col...  114 us
    dot_general x3, matrix products, part(): lax.dot_general(act_all[lo:hi], grad_all[lo:hi], (((0,), (0,)), ((), ()))...  21.9 us
    slice x2, local copies, waits for them, and re-layouts, part(): grad_all[lo:hi]  9.24 us

profile of v12, /device:TPU:1, one launch (start us, length us, event | category | flops | bytes accessed | tf_op | source)
XLA Modules:
  0.0 324.3 jit_solution(14782995918413582607)
XLA Ops:
  0.0 165.6 %shard_map.46 = (bf16[4,8,128,1024]{3,2,1,0:T(8,128)(2,1)}, bf16[4,2,4,128,1792]{4,3,2,1,0:T(8,128)(2,1)}, s32[4,1,128]{2,1,0:T(1,128)}, bf16[8,128,1024]{2,1,0:T(8,128)(2,1)}, bf16[4,128,1792]{2,1,0:T(8,128)(2,1)}) custom-call(bf16[128,8192]{1,0:T(8,128)(2,1)} %bitcast.20, bf16[128,7168]{1,0:T(8,128)(2,1)} %bitcast.23, s32[1,128]{1,0:T(1,128)} %seq_ref.1), custom_call_target="tpu_custom_call" | custom-call | bytes 23068672 | tf_op jit(solution)/shard_map/pallas_call | solution.py:309
  165.6 1.3 fusion.5
  167.6 0.0 copy-start
  167.6 2.9 slice.40
  170.6 1.7 copy-done
  172.3 2.4 fusion.7
  174.7 3.7 %slice.42 = bf16[2,2,4,128,1792]{4,3,2,1,0:T(8,128)(2,1)S(1)} slice(bf16[4,2,4,128,1792]{4,3,2,1,0:T(8,128)(2,1)} %get-tuple-element.10), slice={[1:3], [0:2], [0:4], [0:128], [0:1792]} | slice | bytes 14680064 | tf_op jit(solution)/shard_map/slice | solution.py:352
  178.4 5.5 %fusion.6 = (bf16[1,2,4,128,1792]{4,3,2,1,0:T(8,128)(2,1)}, bf16[1,2,4,128,1792]{4,3,2,1,0:T(8,128)(2,1)S(1)}) fusion(bf16[4,2,4,128,1792]{4,3,2,1,0:T(8,128)(2,1)} %get-tuple-element.10), kind=kLoop, calls=%fused_computation.9 | loop fusion | bytes 14680064 | tf_op jit(solution)/shard_map/slice | solution.py:352
  183.9 0.0 copy-start.1
  183.9 0.0 copy-start.3
  183.9 10.0 %fusion.8 = f32[1024,1792]{1,0:T(8,128)} fusion(bf16[2048,1024]{1,0:T(8,128)(2,1)S(1)} %bitcast.16, bf16[2048,1792]{1,0:T(8,128)(2,1)S(1)} %bitcast.15), kind=kOutput, calls=%fused_computation.11 | convolution fusion | flops 7516192768 | bytes 18874368 | tf_op jit(solution)/shard_map/dot_general | solution.py:351
  194.0 0.0 copy-done.1
  194.0 0.0 copy-done.3
  194.0 0.0 copy-start.2
  194.0 0.0 copy-start.4
  194.0 4.2 %fusion.9 = f32[1024,1792]{1,0:T(8,128)S(1)} fusion(bf16[1024,1024]{1,0:T(8,128)(2,1)S(1)} %bitcast.22, bf16[1024,1792]{1,0:T(8,128)(2,1)S(1)} %bitcast.19), kind=kOutput, calls=%fused_computation.12 | convolution fusion | flops 3758096384 | bytes 13107200 | tf_op jit(solution)/shard_map/dot_general | solution.py:351
  198.1 0.0 copy-done.2
  198.2 0.0 copy-done.4
  198.2 7.7 %fusion.3.prior_ref = f32[1024,1792]{1,0:T(8,128)} fusion(f32[1024,1792]{1,0:T(8,128)S(1)} %copy-done.4, f32[1024,1792]{1,0:T(8,128)S(1)} %fusion.9, pred[]{:T(512)S(6)} %gt.3, bf16[1024,1024]{1,0:T(8,128)(2,1)S(1)} %bitcast.21, bf16[1024,1792]{1,0:T(8,128)(2,1)S(1)} %bitcast.18), kind=kOutput, calls=%fused_computation.5 | convolution fusion | flops 3774611456 | bytes 27787264 | tf_op jit(solution)/shard_map/dot_general | solution.py:351
  205.9 114.3 %shard_map.47 = bf16[1024,1792]{1,0:T(8,128)(2,1)} custom-call(f32[1024,1792]{1,0:T(8,128)} %fusion.3.prior_ref, bf16[1024,1792]{1,0:T(8,128)(2,1)} %bitcast.17), custom_call_target="tpu_custom_call" | custom-call | flops 11010048 | bytes 22020096 | tf_op jit(solution)/shard_map/pallas_call | solution.py:135
  320.2 4.1 %copy.6 = bf16[1024,1792]{1,0:T(8,128)(2,1)} copy(bf16[1024,1792]{1,0:T(8,128)(2,1)} %shard_map.47) | data formatting | bytes 7340032
Async XLA Ops:
  167.6 4.6 %copy-start = (bf16[4,8,128,1024]{3,2,1,0:T(8,128)(2,1)S(1)}, bf16[4,8,128,1024]{3,2,1,0:T(8,128)(2,1)}, u32[]{:S(2)}) copy-start(bf16[4,8,128,1024]{3,2,1,0:T(8,128)(2,1)} %get-tuple-element.9) | copy-start | bytes 25165828
  183.9 10.1 %copy-start.1 = (bf16[1,2,4,128,1792]{4,3,2,1,0:T(8,128)(2,1)S(1)}, bf16[1,2,4,128,1792]{4,3,2,1,0:T(8,128)(2,1)}, u32[]{:S(2)}) copy-start(bf16[1,2,4,128,1792]{4,3,2,1,0:T(8,128)(2,1)} %get-tuple-element.11) | copy-start | bytes 11010052
  183.9 10.1 %copy-start.3 = (bf16[1,8,128,1024]{3,2,1,0:T(8,128)(2,1)S(1)}, bf16[1,8,128,1024]{3,2,1,0:T(8,128)(2,1)}, u32[]{:S(2)}) copy-start(bf16[1,8,128,1024]{3,2,1,0:T(8,128)(2,1)} %get-tuple-element.13) | copy-start | bytes 6291460
  194.0 4.2 %copy-start.2 = (bf16[1,8,128,1024]{3,2,1,0:T(8,128)(2,1)S(1)}, bf16[1,8,128,1024]{3,2,1,0:T(8,128)(2,1)}, u32[]{:S(2)}) copy-start(bf16[1,8,128,1024]{3,2,1,0:T(8,128)(2,1)} %get-tuple-element.14) | copy-start | bytes 6291460
  194.0 4.2 %copy-start.4 = (f32[1024,1792]{1,0:T(8,128)S(1)}, f32[1024,1792]{1,0:T(8,128)}, u32[]{:S(2)}) copy-start(f32[1024,1792]{1,0:T(8,128)} %fusion.8) | copy-start | bytes 22020100

commit v13 on v12

--- a/solution.py
+++ b/solution.py
@@ -15,7 +15,8 @@
 
 
 def mp_merge_kernel(prior_ref, w_ref, out_ref, recv_p, recv_w, part, recv2,
-                    send_sem, recv_sem, s2_send, s2_recv, s3_send, s3_recv, f_send, f_recv):
+                    send_sem, recv_sem, s2_send, s2_recv, s3_send, s3_recv, f_send, f_recv,
+                    t_send, t_recv):
     c = lax.axis_index("c")
     z = lax.axis_index("zl")
     rows = prior_ref.shape[0]
@@ -101,7 +102,14 @@
         cp.wait_recv()
     add(my_q, quarter)
 
+    def fourth(k, lo):
+        rows_k = pl.ds(lo, blk)
+        return pltpu.make_async_remote_copy(
+            src_ref=out_ref.at[rows_k], dst_ref=out_ref.at[rows_k],
+            send_sem=t_send.at[k], recv_sem=t_recv.at[k], device_id=core, device_id_type=MESH)
+
     sent3 = []
+    sent4 = []
     for b in range(nb):
         second(b, my_q).wait_recv()
 
@@ -116,16 +124,18 @@
         cp = third(b, my_q)
         cp.start()
         sent3.append(cp)
+        cp = fourth(b, mine + my_q + b * blk)
+        cp.start()
+        sent4.append(cp)
     for b in range(nb):
         third(b, far_q).wait_recv()
-    fourth = pltpu.make_async_remote_copy(
-        src_ref=out_ref.at[pl.ds(mine, half)], dst_ref=out_ref.at[pl.ds(mine, half)],
-        send_sem=send_sem.at[4], recv_sem=recv_sem.at[4], device_id=core, device_id_type=MESH)
-    fourth.start()
-    pltpu.make_async_remote_copy(
-        src_ref=out_ref.at[pl.ds(other, half)], dst_ref=out_ref.at[pl.ds(other, half)],
-        send_sem=send_sem.at[4], recv_sem=recv_sem.at[4], device_id=core, device_id_type=MESH).wait_recv()
-    for cp in sum(far_in, []) + near_in + sent2 + sent3 + [fourth]:
+        cp = fourth(nb + b, mine + far_q + b * blk)
+        cp.start()
+        sent4.append(cp)
+    for b in range(nb):
+        fourth(b, other + my_q + b * blk).wait_recv()
+        fourth(nb + b, other + far_q + b * blk).wait_recv()
+    for cp in sum(far_in, []) + near_in + sent2 + sent3 + sent4:
         cp.wait_send()
 
 
@@ -148,6 +158,8 @@
             pltpu.SemaphoreType.DMA((blocks,)),
             pltpu.SemaphoreType.DMA((blocks,)),
             pltpu.SemaphoreType.DMA((blocks,)),
+            pltpu.SemaphoreType.DMA((2 * blocks,)),
+            pltpu.SemaphoreType.DMA((2 * blocks,)),
             pltpu.SemaphoreType.DMA((2 * blocks,)),
             pltpu.SemaphoreType.DMA((2 * blocks,)),
         ],

time: 325 us -> 322 us (level)
  no operation moved by 1% of the time
where the time goes in v13:
time: 322 us
  Pallas kernels  278 us (86%)
  matrix products  21.9 us (7%)
  local copies, waits for them, and re-layouts  20.4 us (6%)
    pallas_call x1, Pallas kernels, gather_all(): pl.pallas_call(gather_kernel, out_shape=(jax.ShapeDtypeStruct((nx, nj, to...  166 us
    pallas_call x1, Pallas kernels, mp_merge(): pl.pallas_call(mp_merge_kernel, out_shape=jax.ShapeDtypeStruct((rows, col...  112 us
    dot_general x3, matrix products, part(): lax.dot_general(act_all[lo:hi], grad_all[lo:hi], (((0,), (0,)), ((), ()))...  21.9 us
    slice x2, local copies, waits for them, and re-layouts, part(): grad_all[lo:hi]  9.24 us

profile of v13, /device:TPU:1, one launch (start us, length us, event | category | flops | bytes accessed | tf_op | source)
XLA Modules:
  0.0 322.2 jit_solution(15837604854747550888)
XLA Ops:
  0.0 165.6 %shard_map.46 = (bf16[4,8,128,1024]{3,2,1,0:T(8,128)(2,1)}, bf16[4,2,4,128,1792]{4,3,2,1,0:T(8,128)(2,1)}, s32[4,1,128]{2,1,0:T(1,128)}, bf16[8,128,1024]{2,1,0:T(8,128)(2,1)}, bf16[4,128,1792]{2,1,0:T(8,128)(2,1)}) custom-call(bf16[128,8192]{1,0:T(8,128)(2,1)} %bitcast.20, bf16[128,7168]{1,0:T(8,128)(2,1)} %bitcast.23, s32[1,128]{1,0:T(1,128)} %seq_ref.1), custom_call_target="tpu_custom_call" | custom-call | bytes 23068672 | tf_op jit(solution)/shard_map/pallas_call | solution.py:321
  165.6 1.3 fusion.5
  167.6 0.0 copy-start
  167.6 2.9 slice.40
  170.6 1.7 copy-done
  172.3 2.4 fusion.7
  174.7 3.7 %slice.42 = bf16[2,2,4,128,1792]{4,3,2,1,0:T(8,128)(2,1)S(1)} slice(bf16[4,2,4,128,1792]{4,3,2,1,0:T(8,128)(2,1)} %get-tuple-element.10), slice={[1:3], [0:2], [0:4], [0:128], [0:1792]} | slice | bytes 14680064 | tf_op jit(solution)/shard_map/slice | solution.py:364
  178.4 5.5 %fusion.6 = (bf16[1,2,4,128,1792]{4,3,2,1,0:T(8,128)(2,1)}, bf16[1,2,4,128,1792]{4,3,2,1,0:T(8,128)(2,1)S(1)}) fusion(bf16[4,2,4,128,1792]{4,3,2,1,0:T(8,128)(2,1)} %get-tuple-element.10), kind=kLoop, calls=%fused_computation.9 | loop fusion | bytes 14680064 | tf_op jit(solution)/shard_map/slice | solution.py:364
  183.9 0.0 copy-start.1
  183.9 0.0 copy-start.3
  183.9 10.0 %fusion.8 = f32[1024,1792]{1,0:T(8,128)} fusion(bf16[2048,1024]{1,0:T(8,128)(2,1)S(1)} %bitcast.16, bf16[2048,1792]{1,0:T(8,128)(2,1)S(1)} %bitcast.15), kind=kOutput, calls=%fused_computation.11 | convolution fusion | flops 7516192768 | bytes 18874368 | tf_op jit(solution)/shard_map/dot_general | solution.py:363
  194.0 0.0 copy-done.1
  194.0 0.0 copy-done.3
  194.0 0.0 copy-start.2
  194.0 0.0 copy-start.4
  194.0 4.2 %fusion.9 = f32[1024,1792]{1,0:T(8,128)S(1)} fusion(bf16[1024,1024]{1,0:T(8,128)(2,1)S(1)} %bitcast.22, bf16[1024,1792]{1,0:T(8,128)(2,1)S(1)} %bitcast.19), kind=kOutput, calls=%fused_computation.12 | convolution fusion | flops 3758096384 | bytes 13107200 | tf_op jit(solution)/shard_map/dot_general | solution.py:363
  198.1 0.0 copy-done.2
  198.2 0.0 copy-done.4
  198.2 7.7 %fusion.3.prior_ref = f32[1024,1792]{1,0:T(8,128)} fusion(f32[1024,1792]{1,0:T(8,128)S(1)} %copy-done.4, f32[1024,1792]{1,0:T(8,128)S(1)} %fusion.9, pred[]{:T(512)S(6)} %gt.3, bf16[1024,1024]{1,0:T(8,128)(2,1)S(1)} %bitcast.21, bf16[1024,1792]{1,0:T(8,128)(2,1)S(1)} %bitcast.18), kind=kOutput, calls=%fused_computation.5 | convolution fusion | flops 3774611456 | bytes 27787264 | tf_op jit(solution)/shard_map/dot_general | solution.py:363
  205.9 112.2 %shard_map.47 = bf16[1024,1792]{1,0:T(8,128)(2,1)} custom-call(f32[1024,1792]{1,0:T(8,128)} %fusion.3.prior_ref, bf16[1024,1792]{1,0:T(8,128)(2,1)} %bitcast.17), custom_call_target="tpu_custom_call" | custom-call | flops 11010048 | bytes 22020096 | tf_op jit(solution)/shard_map/pallas_call | solution.py:145
  318.1 4.1 %copy.6 = bf16[1024,1792]{1,0:T(8,128)(2,1)} copy(bf16[1024,1792]{1,0:T(8,128)(2,1)} %shard_map.47) | data formatting | bytes 7340032
Async XLA Ops:
  167.6 4.6 %copy-start = (bf16[4,8,128,1024]{3,2,1,0:T(8,128)(2,1)S(1)}, bf16[4,8,128,1024]{3,2,1,0:T(8,128)(2,1)}, u32[]{:S(2)}) copy-start(bf16[4,8,128,1024]{3,2,1,0:T(8,128)(2,1)} %get-tuple-element.9) | copy-start | bytes 25165828
  183.9 10.1 %copy-start.1 = (bf16[1,2,4,128,1792]{4,3,2,1,0:T(8,128)(2,1)S(1)}, bf16[1,2,4,128,1792]{4,3,2,1,0:T(8,128)(2,1)}, u32[]{:S(2)}) copy-start(bf16[1,2,4,128,1792]{4,3,2,1,0:T(8,128)(2,1)} %get-tuple-element.11) | copy-start | bytes 11010052
  183.9 10.1 %copy-start.3 = (bf16[1,8,128,1024]{3,2,1,0:T(8,128)(2,1)S(1)}, bf16[1,8,128,1024]{3,2,1,0:T(8,128)(2,1)}, u32[]{:S(2)}) copy-start(bf16[1,8,128,1024]{3,2,1,0:T(8,128)(2,1)} %get-tuple-element.13) | copy-start | bytes 6291460
  194.0 4.2 %copy-start.2 = (bf16[1,8,128,1024]{3,2,1,0:T(8,128)(2,1)S(1)}, bf16[1,8,128,1024]{3,2,1,0:T(8,128)(2,1)}, u32[]{:S(2)}) copy-start(bf16[1,8,128,1024]{3,2,1,0:T(8,128)(2,1)} %get-tuple-element.14) | copy-start | bytes 6291460
  194.0 4.2 %copy-start.4 = (f32[1024,1792]{1,0:T(8,128)S(1)}, f32[1024,1792]{1,0:T(8,128)}, u32[]{:S(2)}) copy-start(f32[1024,1792]{1,0:T(8,128)} %fusion.8) | copy-start | bytes 22020100

commit v14 on v13

--- a/solution.py
+++ b/solution.py
@@ -278,10 +278,21 @@
     swap.start()
     for c in g_first + seq_first + [own[1], own[2]]:
         c.start()
+    swap_in.wait_recv()
+    for c in p_first:
+        c.start()
+    for c in g_arrive:
+        c.wait_recv()
+    for c in g_relay:
+        c.start()
     for c in p0_in:
         c.wait_recv()
     own0[0].wait()
     for c in a_first + [own[0]]:
+        c.start()
+    for c in p_arrive:
+        c.wait_recv()
+    for c in p_relay:
         c.start()
     for c in a_arrive:
         c.wait_recv()
@@ -290,17 +301,6 @@
     seq_relay = sc(seq_out.at[xr], seq_out.at[xr], 2, xl)
     seq_relay.start()
     for c in a_relay:
-        c.start()
-    for c in g_arrive:
-        c.wait_recv()
-    for c in g_relay:
-        c.start()
-    swap_in.wait_recv()
-    for c in p_first:
-        c.start()
-    for c in p_arrive:
-        c.wait_recv()
-    for c in p_relay:
         c.start()
     for c in a_land + g_land + p_land:
         c.wait_recv()

time: 322 us -> 314 us (0.975)
  Pallas kernels: 278 us -> 270 us
    pallas_call x1, Pallas kernels: 166 us -> 159 us  [gather_all(): pl.pallas_call(gather_kernel, out_shape=(jax.ShapeDtypeStruct((nx, nj, to...]
where the time goes in v14:
time: 314 us
  Pallas kernels  270 us (86%)
  matrix products  21.9 us (7%)
  local copies, waits for them, and re-layouts  20.4 us (6%)
    pallas_call x1, Pallas kernels, gather_all(): pl.pallas_call(gather_kernel, out_shape=(jax.ShapeDtypeStruct((nx, nj, to...  159 us
    pallas_call x1, Pallas kernels, mp_merge(): pl.pallas_call(mp_merge_kernel, out_shape=jax.ShapeDtypeStruct((rows, col...  111 us
    dot_general x3, matrix products, part(): lax.dot_general(act_all[lo:hi], grad_all[lo:hi], (((0,), (0,)), ((), ()))...  21.9 us
    slice x2, local copies, waits for them, and re-layouts, part(): grad_all[lo:hi]  9.24 us

profile of v14, /device:TPU:1, one launch (start us, length us, event | category | flops | bytes accessed | tf_op | source)
XLA Modules:
  0.0 314.2 jit_solution(6031017986026025160)
XLA Ops:
  0.0 158.6 %shard_map.46 = (bf16[4,8,128,1024]{3,2,1,0:T(8,128)(2,1)}, bf16[4,2,4,128,1792]{4,3,2,1,0:T(8,128)(2,1)}, s32[4,1,128]{2,1,0:T(1,128)}, bf16[8,128,1024]{2,1,0:T(8,128)(2,1)}, bf16[4,128,1792]{2,1,0:T(8,128)(2,1)}) custom-call(bf16[128,8192]{1,0:T(8,128)(2,1)} %bitcast.20, bf16[128,7168]{1,0:T(8,128)(2,1)} %bitcast.23, s32[1,128]{1,0:T(1,128)} %seq_ref.1), custom_call_target="tpu_custom_call" | custom-call | bytes 23068672 | tf_op jit(solution)/shard_map/pallas_call | solution.py:321
  158.6 1.3 fusion.5
  160.6 0.0 copy-start
  160.6 2.9 slice.40
  163.6 1.7 copy-done
  165.3 2.4 fusion.7
  167.7 3.7 %slice.42 = bf16[2,2,4,128,1792]{4,3,2,1,0:T(8,128)(2,1)S(1)} slice(bf16[4,2,4,128,1792]{4,3,2,1,0:T(8,128)(2,1)} %get-tuple-element.10), slice={[1:3], [0:2], [0:4], [0:128], [0:1792]} | slice | bytes 14680064 | tf_op jit(solution)/shard_map/slice | solution.py:364
  171.4 5.5 %fusion.6 = (bf16[1,2,4,128,1792]{4,3,2,1,0:T(8,128)(2,1)}, bf16[1,2,4,128,1792]{4,3,2,1,0:T(8,128)(2,1)S(1)}) fusion(bf16[4,2,4,128,1792]{4,3,2,1,0:T(8,128)(2,1)} %get-tuple-element.10), kind=kLoop, calls=%fused_computation.9 | loop fusion | bytes 14680064 | tf_op jit(solution)/shard_map/slice | solution.py:364
  176.9 0.0 copy-start.1
  176.9 0.0 copy-start.3
  176.9 10.1 %fusion.8 = f32[1024,1792]{1,0:T(8,128)} fusion(bf16[2048,1024]{1,0:T(8,128)(2,1)S(1)} %bitcast.16, bf16[2048,1792]{1,0:T(8,128)(2,1)S(1)} %bitcast.15), kind=kOutput, calls=%fused_computation.11 | convolution fusion | flops 7516192768 | bytes 18874368 | tf_op jit(solution)/shard_map/dot_general | solution.py:363
  187.0 0.0 copy-done.1
  187.0 0.0 copy-done.3
  187.0 0.0 copy-start.2
  187.0 0.0 copy-start.4
  187.0 4.2 %fusion.9 = f32[1024,1792]{1,0:T(8,128)S(1)} fusion(bf16[1024,1024]{1,0:T(8,128)(2,1)S(1)} %bitcast.22, bf16[1024,1792]{1,0:T(8,128)(2,1)S(1)} %bitcast.19), kind=kOutput, calls=%fused_computation.12 | convolution fusion | flops 3758096384 | bytes 13107200 | tf_op jit(solution)/shard_map/dot_general | solution.py:363
  191.2 0.0 copy-done.2
  191.2 0.0 copy-done.4
  191.2 7.7 %fusion.3.prior_ref = f32[1024,1792]{1,0:T(8,128)} fusion(f32[1024,1792]{1,0:T(8,128)S(1)} %copy-done.4, f32[1024,1792]{1,0:T(8,128)S(1)} %fusion.9, pred[]{:T(512)S(6)} %gt.3, bf16[1024,1024]{1,0:T(8,128)(2,1)S(1)} %bitcast.21, bf16[1024,1792]{1,0:T(8,128)(2,1)S(1)} %bitcast.18), kind=kOutput, calls=%fused_computation.5 | convolution fusion | flops 3774611456 | bytes 27787264 | tf_op jit(solution)/shard_map/dot_general | solution.py:363
  198.9 111.1 %shard_map.47 = bf16[1024,1792]{1,0:T(8,128)(2,1)} custom-call(f32[1024,1792]{1,0:T(8,128)} %fusion.3.prior_ref, bf16[1024,1792]{1,0:T(8,128)(2,1)} %bitcast.17), custom_call_target="tpu_custom_call" | custom-call | flops 11010048 | bytes 22020096 | tf_op jit(solution)/shard_map/pallas_call | solution.py:145
  310.1 4.1 %copy.6 = bf16[1024,1792]{1,0:T(8,128)(2,1)} copy(bf16[1024,1792]{1,0:T(8,128)(2,1)} %shard_map.47) | data formatting | bytes 7340032
Async XLA Ops:
  160.6 4.6 %copy-start = (bf16[4,8,128,1024]{3,2,1,0:T(8,128)(2,1)S(1)}, bf16[4,8,128,1024]{3,2,1,0:T(8,128)(2,1)}, u32[]{:S(2)}) copy-start(bf16[4,8,128,1024]{3,2,1,0:T(8,128)(2,1)} %get-tuple-element.9) | copy-start | bytes 25165828
  176.9 10.1 %copy-start.1 = (bf16[1,2,4,128,1792]{4,3,2,1,0:T(8,128)(2,1)S(1)}, bf16[1,2,4,128,1792]{4,3,2,1,0:T(8,128)(2,1)}, u32[]{:S(2)}) copy-start(bf16[1,2,4,128,1792]{4,3,2,1,0:T(8,128)(2,1)} %get-tuple-element.11) | copy-start | bytes 11010052
  176.9 10.1 %copy-start.3 = (bf16[1,8,128,1024]{3,2,1,0:T(8,128)(2,1)S(1)}, bf16[1,8,128,1024]{3,2,1,0:T(8,128)(2,1)}, u32[]{:S(2)}) copy-start(bf16[1,8,128,1024]{3,2,1,0:T(8,128)(2,1)} %get-tuple-element.13) | copy-start | bytes 6291460
  187.0 4.2 %copy-start.2 = (bf16[1,8,128,1024]{3,2,1,0:T(8,128)(2,1)S(1)}, bf16[1,8,128,1024]{3,2,1,0:T(8,128)(2,1)}, u32[]{:S(2)}) copy-start(bf16[1,8,128,1024]{3,2,1,0:T(8,128)(2,1)} %get-tuple-element.14) | copy-start | bytes 6291460
  187.0 4.2 %copy-start.4 = (f32[1024,1792]{1,0:T(8,128)S(1)}, f32[1024,1792]{1,0:T(8,128)}, u32[]{:S(2)}) copy-start(f32[1024,1792]{1,0:T(8,128)} %fusion.8) | copy-start | bytes 22020100

commit v15 on v14

--- a/solution.py
+++ b/solution.py
@@ -242,7 +242,7 @@
         pltpu.make_async_copy(
             grad_in.at[:, pl.ds(pl.multiple_of(x * cw, 128), cw)], grad_ref.at[x], local.at[4]),
     ]
-    for c in own0 + q0_out + p0_out:
+    for c in own0 + q0_out:
         c.start()
     for c in q0_in:
         c.wait_recv()
@@ -277,6 +277,8 @@
 
     swap.start()
     for c in g_first + seq_first + [own[1], own[2]]:
+        c.start()
+    for c in p0_out:
         c.start()
     swap_in.wait_recv()
     for c in p_first:

time: 314 us -> 334 us (1.064)
  Pallas kernels: 270 us -> 288 us
    pallas_call x1, Pallas kernels: 159 us -> 176 us  [gather_all(): pl.pallas_call(gather_kernel, out_shape=(jax.ShapeDtypeStruct((nx, nj, to...]
where the time goes in v15:
time: 334 us; the launch traced here: 333 us
  Pallas kernels  288 us (86%)
  matrix products  21.9 us (7%)
  local copies, waits for them, and re-layouts  20.4 us (6%)
    pallas_call x1, Pallas kernels, gather_all(): pl.pallas_call(gather_kernel, out_shape=(jax.ShapeDtypeStruct((nx, nj, to...  176 us
    pallas_call x1, Pallas kernels, mp_merge(): pl.pallas_call(mp_merge_kernel, out_shape=jax.ShapeDtypeStruct((rows, col...  112 us
    dot_general x3, matrix products, part(): lax.dot_general(act_all[lo:hi], grad_all[lo:hi], (((0,), (0,)), ((), ()))...  21.9 us
    slice x2, local copies, waits for them, and re-layouts, part(): grad_all[lo:hi]  9.24 us

profile of v15, /device:TPU:1, one launch (start us, length us, event | category | flops | bytes accessed | tf_op | source)
XLA Modules:
  0.0 332.6 jit_solution(16788704943333550182)
XLA Ops:
  0.0 176.0 %shard_map.46 = (bf16[4,8,128,1024]{3,2,1,0:T(8,128)(2,1)}, bf16[4,2,4,128,1792]{4,3,2,1,0:T(8,128)(2,1)}, s32[4,1,128]{2,1,0:T(1,128)}, bf16[8,128,1024]{2,1,0:T(8,128)(2,1)}, bf16[4,128,1792]{2,1,0:T(8,128)(2,1)}) custom-call(bf16[128,8192]{1,0:T(8,128)(2,1)} %bitcast.20, bf16[128,7168]{1,0:T(8,128)(2,1)} %bitcast.23, s32[1,128]{1,0:T(1,128)} %seq_ref.1), custom_call_target="tpu_custom_call" | custom-call | bytes 23068672 | tf_op jit(solution)/shard_map/pallas_call | solution.py:323
  176.0 1.3 fusion.5
  178.0 0.0 copy-start
  178.0 2.9 slice.40
  180.9 1.7 copy-done
  182.6 2.4 fusion.7
  185.0 3.7 %slice.42 = bf16[2,2,4,128,1792]{4,3,2,1,0:T(8,128)(2,1)S(1)} slice(bf16[4,2,4,128,1792]{4,3,2,1,0:T(8,128)(2,1)} %get-tuple-element.10), slice={[1:3], [0:2], [0:4], [0:128], [0:1792]} | slice | bytes 14680064 | tf_op jit(solution)/shard_map/slice | solution.py:366
  188.8 5.5 %fusion.6 = (bf16[1,2,4,128,1792]{4,3,2,1,0:T(8,128)(2,1)}, bf16[1,2,4,128,1792]{4,3,2,1,0:T(8,128)(2,1)S(1)}) fusion(bf16[4,2,4,128,1792]{4,3,2,1,0:T(8,128)(2,1)} %get-tuple-element.10), kind=kLoop, calls=%fused_computation.9 | loop fusion | bytes 14680064 | tf_op jit(solution)/shard_map/slice | solution.py:366
  194.3 0.0 copy-start.1
  194.3 0.0 copy-start.3
  194.3 10.0 %fusion.8 = f32[1024,1792]{1,0:T(8,128)} fusion(bf16[2048,1024]{1,0:T(8,128)(2,1)S(1)} %bitcast.16, bf16[2048,1792]{1,0:T(8,128)(2,1)S(1)} %bitcast.15), kind=kOutput, calls=%fused_computation.11 | convolution fusion | flops 7516192768 | bytes 18874368 | tf_op jit(solution)/shard_map/dot_general | solution.py:365
  204.3 0.0 copy-done.1
  204.3 0.0 copy-done.3
  204.3 0.0 copy-start.2
  204.3 0.0 copy-start.4
  204.3 4.2 %fusion.9 = f32[1024,1792]{1,0:T(8,128)S(1)} fusion(bf16[1024,1024]{1,0:T(8,128)(2,1)S(1)} %bitcast.22, bf16[1024,1792]{1,0:T(8,128)(2,1)S(1)} %bitcast.19), kind=kOutput, calls=%fused_computation.12 | convolution fusion | flops 3758096384 | bytes 13107200 | tf_op jit(solution)/shard_map/dot_general | solution.py:365
  208.5 0.0 copy-done.2
  208.5 0.0 copy-done.4
  208.5 7.7 %fusion.3.prior_ref = f32[1024,1792]{1,0:T(8,128)} fusion(f32[1024,1792]{1,0:T(8,128)S(1)} %copy-done.4, f32[1024,1792]{1,0:T(8,128)S(1)} %fusion.9, pred[]{:T(512)S(6)} %gt.3, bf16[1024,1024]{1,0:T(8,128)(2,1)S(1)} %bitcast.21, bf16[1024,1792]{1,0:T(8,128)(2,1)S(1)} %bitcast.18), kind=kOutput, calls=%fused_computation.5 | convolution fusion | flops 3774611456 | bytes 27787264 | tf_op jit(solution)/shard_map/dot_general | solution.py:365
  216.2 112.2 %shard_map.47 = bf16[1024,1792]{1,0:T(8,128)(2,1)} custom-call(f32[1024,1792]{1,0:T(8,128)} %fusion.3.prior_ref, bf16[1024,1792]{1,0:T(8,128)(2,1)} %bitcast.17), custom_call_target="tpu_custom_call" | custom-call | flops 11010048 | bytes 22020096 | tf_op jit(solution)/shard_map/pallas_call | solution.py:145
  328.4 4.1 %copy.6 = bf16[1024,1792]{1,0:T(8,128)(2,1)} copy(bf16[1024,1792]{1,0:T(8,128)(2,1)} %shard_map.47) | data formatting | bytes 7340032
Async XLA Ops:
  178.0 4.6 %copy-start = (bf16[4,8,128,1024]{3,2,1,0:T(8,128)(2,1)S(1)}, bf16[4,8,128,1024]{3,2,1,0:T(8,128)(2,1)}, u32[]{:S(2)}) copy-start(bf16[4,8,128,1024]{3,2,1,0:T(8,128)(2,1)} %get-tuple-element.9) | copy-start | bytes 25165828
  194.3 10.1 %copy-start.1 = (bf16[1,2,4,128,1792]{4,3,2,1,0:T(8,128)(2,1)S(1)}, bf16[1,2,4,128,1792]{4,3,2,1,0:T(8,128)(2,1)}, u32[]{:S(2)}) copy-start(bf16[1,2,4,128,1792]{4,3,2,1,0:T(8,128)(2,1)} %get-tuple-element.11) | copy-start | bytes 11010052
  194.3 10.1 %copy-start.3 = (bf16[1,8,128,1024]{3,2,1,0:T(8,128)(2,1)S(1)}, bf16[1,8,128,1024]{3,2,1,0:T(8,128)(2,1)}, u32[]{:S(2)}) copy-start(bf16[1,8,128,1024]{3,2,1,0:T(8,128)(2,1)} %get-tuple-element.13) | copy-start | bytes 6291460
  204.3 4.2 %copy-start.2 = (bf16[1,8,128,1024]{3,2,1,0:T(8,128)(2,1)S(1)}, bf16[1,8,128,1024]{3,2,1,0:T(8,128)(2,1)}, u32[]{:S(2)}) copy-start(bf16[1,8,128,1024]{3,2,1,0:T(8,128)(2,1)} %get-tuple-element.14) | copy-start | bytes 6291460
  204.3 4.2 %copy-start.4 = (f32[1024,1792]{1,0:T(8,128)S(1)}, f32[1024,1792]{1,0:T(8,128)}, u32[]{:S(2)}) copy-start(f32[1024,1792]{1,0:T(8,128)} %fusion.8) | copy-start | bytes 22020100

commit v16 on v14

--- a/solution.py
+++ b/solution.py
@@ -278,17 +278,17 @@
     swap.start()
     for c in g_first + seq_first + [own[1], own[2]]:
         c.start()
+    for c in p0_in:
+        c.wait_recv()
+    own0[0].wait()
+    for c in a_first + [own[0]]:
+        c.start()
     swap_in.wait_recv()
     for c in p_first:
         c.start()
     for c in g_arrive:
         c.wait_recv()
     for c in g_relay:
-        c.start()
-    for c in p0_in:
-        c.wait_recv()
-    own0[0].wait()
-    for c in a_first + [own[0]]:
         c.start()
     for c in p_arrive:
         c.wait_recv()

time: 314 us -> 314 us (level)
  no operation moved by 1% of the time
where the time goes in v16:
time: 314 us
  Pallas kernels  270 us (86%)
  matrix products  21.9 us (7%)
  local copies, waits for them, and re-layouts  20.4 us (6%)
    pallas_call x1, Pallas kernels, gather_all(): pl.pallas_call(gather_kernel, out_shape=(jax.ShapeDtypeStruct((nx, nj, to...  159 us
    pallas_call x1, Pallas kernels, mp_merge(): pl.pallas_call(mp_merge_kernel, out_shape=jax.ShapeDtypeStruct((rows, col...  111 us
    dot_general x3, matrix products, part(): lax.dot_general(act_all[lo:hi], grad_all[lo:hi], (((0,), (0,)), ((), ()))...  21.9 us
    slice x2, local copies, waits for them, and re-layouts, part(): grad_all[lo:hi]  9.24 us

profile of v16, /device:TPU:1, one launch (start us, length us, event | category | flops | bytes accessed | tf_op | source)
XLA Modules:
  0.0 314.2 jit_solution(14971656552434862147)
XLA Ops:
  0.0 158.6 %shard_map.46 = (bf16[4,8,128,1024]{3,2,1,0:T(8,128)(2,1)}, bf16[4,2,4,128,1792]{4,3,2,1,0:T(8,128)(2,1)}, s32[4,1,128]{2,1,0:T(1,128)}, bf16[8,128,1024]{2,1,0:T(8,128)(2,1)}, bf16[4,128,1792]{2,1,0:T(8,128)(2,1)}) custom-call(bf16[128,8192]{1,0:T(8,128)(2,1)} %bitcast.20, bf16[128,7168]{1,0:T(8,128)(2,1)} %bitcast.23, s32[1,128]{1,0:T(1,128)} %seq_ref.1), custom_call_target="tpu_custom_call" | custom-call | bytes 23068672 | tf_op jit(solution)/shard_map/pallas_call | solution.py:321
  158.6 1.3 fusion.5
  160.6 0.0 copy-start
  160.6 2.9 slice.40
  163.6 1.7 copy-done
  165.3 2.4 fusion.7
  167.7 3.7 %slice.42 = bf16[2,2,4,128,1792]{4,3,2,1,0:T(8,128)(2,1)S(1)} slice(bf16[4,2,4,128,1792]{4,3,2,1,0:T(8,128)(2,1)} %get-tuple-element.10), slice={[1:3], [0:2], [0:4], [0:128], [0:1792]} | slice | bytes 14680064 | tf_op jit(solution)/shard_map/slice | solution.py:364
  171.4 5.5 %fusion.6 = (bf16[1,2,4,128,1792]{4,3,2,1,0:T(8,128)(2,1)}, bf16[1,2,4,128,1792]{4,3,2,1,0:T(8,128)(2,1)S(1)}) fusion(bf16[4,2,4,128,1792]{4,3,2,1,0:T(8,128)(2,1)} %get-tuple-element.10), kind=kLoop, calls=%fused_computation.9 | loop fusion | bytes 14680064 | tf_op jit(solution)/shard_map/slice | solution.py:364
  176.9 0.0 copy-start.1
  176.9 0.0 copy-start.3
  176.9 10.1 %fusion.8 = f32[1024,1792]{1,0:T(8,128)} fusion(bf16[2048,1024]{1,0:T(8,128)(2,1)S(1)} %bitcast.16, bf16[2048,1792]{1,0:T(8,128)(2,1)S(1)} %bitcast.15), kind=kOutput, calls=%fused_computation.11 | convolution fusion | flops 7516192768 | bytes 18874368 | tf_op jit(solution)/shard_map/dot_general | solution.py:363
  187.0 0.0 copy-done.1
  187.0 0.0 copy-done.3
  187.0 0.0 copy-start.2
  187.0 0.0 copy-start.4
  187.0 4.2 %fusion.9 = f32[1024,1792]{1,0:T(8,128)S(1)} fusion(bf16[1024,1024]{1,0:T(8,128)(2,1)S(1)} %bitcast.22, bf16[1024,1792]{1,0:T(8,128)(2,1)S(1)} %bitcast.19), kind=kOutput, calls=%fused_computation.12 | convolution fusion | flops 3758096384 | bytes 13107200 | tf_op jit(solution)/shard_map/dot_general | solution.py:363
  191.2 0.0 copy-done.2
  191.2 0.0 copy-done.4
  191.2 7.7 %fusion.3.prior_ref = f32[1024,1792]{1,0:T(8,128)} fusion(f32[1024,1792]{1,0:T(8,128)S(1)} %copy-done.4, f32[1024,1792]{1,0:T(8,128)S(1)} %fusion.9, pred[]{:T(512)S(6)} %gt.3, bf16[1024,1024]{1,0:T(8,128)(2,1)S(1)} %bitcast.21, bf16[1024,1792]{1,0:T(8,128)(2,1)S(1)} %bitcast.18), kind=kOutput, calls=%fused_computation.5 | convolution fusion | flops 3774611456 | bytes 27787264 | tf_op jit(solution)/shard_map/dot_general | solution.py:363
  198.9 111.1 %shard_map.47 = bf16[1024,1792]{1,0:T(8,128)(2,1)} custom-call(f32[1024,1792]{1,0:T(8,128)} %fusion.3.prior_ref, bf16[1024,1792]{1,0:T(8,128)(2,1)} %bitcast.17), custom_call_target="tpu_custom_call" | custom-call | flops 11010048 | bytes 22020096 | tf_op jit(solution)/shard_map/pallas_call | solution.py:145
  310.1 4.1 %copy.6 = bf16[1024,1792]{1,0:T(8,128)(2,1)} copy(bf16[1024,1792]{1,0:T(8,128)(2,1)} %shard_map.47) | data formatting | bytes 7340032
Async XLA Ops:
  160.6 4.6 %copy-start = (bf16[4,8,128,1024]{3,2,1,0:T(8,128)(2,1)S(1)}, bf16[4,8,128,1024]{3,2,1,0:T(8,128)(2,1)}, u32[]{:S(2)}) copy-start(bf16[4,8,128,1024]{3,2,1,0:T(8,128)(2,1)} %get-tuple-element.9) | copy-start | bytes 25165828
  176.9 10.1 %copy-start.1 = (bf16[1,2,4,128,1792]{4,3,2,1,0:T(8,128)(2,1)S(1)}, bf16[1,2,4,128,1792]{4,3,2,1,0:T(8,128)(2,1)}, u32[]{:S(2)}) copy-start(bf16[1,2,4,128,1792]{4,3,2,1,0:T(8,128)(2,1)} %get-tuple-element.11) | copy-start | bytes 11010052
  176.9 10.1 %copy-start.3 = (bf16[1,8,128,1024]{3,2,1,0:T(8,128)(2,1)S(1)}, bf16[1,8,128,1024]{3,2,1,0:T(8,128)(2,1)}, u32[]{:S(2)}) copy-start(bf16[1,8,128,1024]{3,2,1,0:T(8,128)(2,1)} %get-tuple-element.13) | copy-start | bytes 6291460
  187.0 4.2 %copy-start.2 = (bf16[1,8,128,1024]{3,2,1,0:T(8,128)(2,1)S(1)}, bf16[1,8,128,1024]{3,2,1,0:T(8,128)(2,1)}, u32[]{:S(2)}) copy-start(bf16[1,8,128,1024]{3,2,1,0:T(8,128)(2,1)} %get-tuple-element.14) | copy-start | bytes 6291460
  187.0 4.2 %copy-start.4 = (f32[1024,1792]{1,0:T(8,128)S(1)}, f32[1024,1792]{1,0:T(8,128)}, u32[]{:S(2)}) copy-start(f32[1024,1792]{1,0:T(8,128)} %fusion.8) | copy-start | bytes 22020100

commit v17 on v16

--- a/solution.py
+++ b/solution.py
@@ -290,18 +290,18 @@
         c.wait_recv()
     for c in g_relay:
         c.start()
+    for c in a_arrive:
+        c.wait_recv()
+    for c in a_relay:
+        c.start()
     for c in p_arrive:
         c.wait_recv()
     for c in p_relay:
         c.start()
-    for c in a_arrive:
-        c.wait_recv()
     sc(seq_ref, seq_out.at[xl], 0, xl).wait_recv()
     sc(seq_ref, seq_out.at[xr], 1, xr).wait_recv()
     seq_relay = sc(seq_out.at[xr], seq_out.at[xr], 2, xl)
     seq_relay.start()
-    for c in a_relay:
-        c.start()
     for c in a_land + g_land + p_land:
         c.wait_recv()
     sc(seq_out.at[lax.rem(x + 2, nx)], seq_out.at[lax.rem(x + 2, nx)], 2, xr).wait_recv()

time: 314 us -> 314 us (level)
  no operation moved by 1% of the time
where the time goes in v17:
time: 314 us
  Pallas kernels  270 us (86%)
  matrix products  21.9 us (7%)
  local copies, waits for them, and re-layouts  20.4 us (6%)
    pallas_call x1, Pallas kernels, gather_all(): pl.pallas_call(gather_kernel, out_shape=(jax.ShapeDtypeStruct((nx, nj, to...  159 us
    pallas_call x1, Pallas kernels, mp_merge(): pl.pallas_call(mp_merge_kernel, out_shape=jax.ShapeDtypeStruct((rows, col...  111 us
    dot_general x3, matrix products, part(): lax.dot_general(act_all[lo:hi], grad_all[lo:hi], (((0,), (0,)), ((), ()))...  21.9 us
    slice x2, local copies, waits for them, and re-layouts, part(): grad_all[lo:hi]  9.24 us

profile of v17, /device:TPU:1, one launch (start us, length us, event | category | flops | bytes accessed | tf_op | source)
XLA Modules:
  0.0 314.2 jit_solution(15745380654684492874)
XLA Ops:
  0.0 158.6 %shard_map.46 = (bf16[4,8,128,1024]{3,2,1,0:T(8,128)(2,1)}, bf16[4,2,4,128,1792]{4,3,2,1,0:T(8,128)(2,1)}, s32[4,1,128]{2,1,0:T(1,128)}, bf16[8,128,1024]{2,1,0:T(8,128)(2,1)}, bf16[4,128,1792]{2,1,0:T(8,128)(2,1)}) custom-call(bf16[128,8192]{1,0:T(8,128)(2,1)} %bitcast.20, bf16[128,7168]{1,0:T(8,128)(2,1)} %bitcast.23, s32[1,128]{1,0:T(1,128)} %seq_ref.1), custom_call_target="tpu_custom_call" | custom-call | bytes 23068672 | tf_op jit(solution)/shard_map/pallas_call | solution.py:321
  158.6 1.3 fusion.5
  160.6 0.0 copy-start
  160.6 2.9 slice.40
  163.6 1.7 copy-done
  165.3 2.4 fusion.7
  167.7 3.7 %slice.42 = bf16[2,2,4,128,1792]{4,3,2,1,0:T(8,128)(2,1)S(1)} slice(bf16[4,2,4,128,1792]{4,3,2,1,0:T(8,128)(2,1)} %get-tuple-element.10), slice={[1:3], [0:2], [0:4], [0:128], [0:1792]} | slice | bytes 14680064 | tf_op jit(solution)/shard_map/slice | solution.py:364
  171.4 5.5 %fusion.6 = (bf16[1,2,4,128,1792]{4,3,2,1,0:T(8,128)(2,1)}, bf16[1,2,4,128,1792]{4,3,2,1,0:T(8,128)(2,1)S(1)}) fusion(bf16[4,2,4,128,1792]{4,3,2,1,0:T(8,128)(2,1)} %get-tuple-element.10), kind=kLoop, calls=%fused_computation.9 | loop fusion | bytes 14680064 | tf_op jit(solution)/shard_map/slice | solution.py:364
  176.9 0.0 copy-start.1
  176.9 0.0 copy-start.3
  176.9 10.1 %fusion.8 = f32[1024,1792]{1,0:T(8,128)} fusion(bf16[2048,1024]{1,0:T(8,128)(2,1)S(1)} %bitcast.16, bf16[2048,1792]{1,0:T(8,128)(2,1)S(1)} %bitcast.15), kind=kOutput, calls=%fused_computation.11 | convolution fusion | flops 7516192768 | bytes 18874368 | tf_op jit(solution)/shard_map/dot_general | solution.py:363
  187.0 0.0 copy-done.1
  187.0 0.0 copy-done.3
  187.0 0.0 copy-start.2
  187.0 0.0 copy-start.4
  187.0 4.2 %fusion.9 = f32[1024,1792]{1,0:T(8,128)S(1)} fusion(bf16[1024,1024]{1,0:T(8,128)(2,1)S(1)} %bitcast.22, bf16[1024,1792]{1,0:T(8,128)(2,1)S(1)} %bitcast.19), kind=kOutput, calls=%fused_computation.12 | convolution fusion | flops 3758096384 | bytes 13107200 | tf_op jit(solution)/shard_map/dot_general | solution.py:363
  191.2 0.0 copy-done.2
  191.2 0.0 copy-done.4
  191.2 7.7 %fusion.3.prior_ref = f32[1024,1792]{1,0:T(8,128)} fusion(f32[1024,1792]{1,0:T(8,128)S(1)} %copy-done.4, f32[1024,1792]{1,0:T(8,128)S(1)} %fusion.9, pred[]{:T(512)S(6)} %gt.3, bf16[1024,1024]{1,0:T(8,128)(2,1)S(1)} %bitcast.21, bf16[1024,1792]{1,0:T(8,128)(2,1)S(1)} %bitcast.18), kind=kOutput, calls=%fused_computation.5 | convolution fusion | flops 3774611456 | bytes 27787264 | tf_op jit(solution)/shard_map/dot_general | solution.py:363
  198.9 111.1 %shard_map.47 = bf16[1024,1792]{1,0:T(8,128)(2,1)} custom-call(f32[1024,1792]{1,0:T(8,128)} %fusion.3.prior_ref, bf16[1024,1792]{1,0:T(8,128)(2,1)} %bitcast.17), custom_call_target="tpu_custom_call" | custom-call | flops 11010048 | bytes 22020096 | tf_op jit(solution)/shard_map/pallas_call | solution.py:145
  310.1 4.1 %copy.6 = bf16[1024,1792]{1,0:T(8,128)(2,1)} copy(bf16[1024,1792]{1,0:T(8,128)(2,1)} %shard_map.47) | data formatting | bytes 7340032
Async XLA Ops:
  160.6 4.6 %copy-start = (bf16[4,8,128,1024]{3,2,1,0:T(8,128)(2,1)S(1)}, bf16[4,8,128,1024]{3,2,1,0:T(8,128)(2,1)}, u32[]{:S(2)}) copy-start(bf16[4,8,128,1024]{3,2,1,0:T(8,128)(2,1)} %get-tuple-element.9) | copy-start | bytes 25165828
  176.9 10.1 %copy-start.1 = (bf16[1,2,4,128,1792]{4,3,2,1,0:T(8,128)(2,1)S(1)}, bf16[1,2,4,128,1792]{4,3,2,1,0:T(8,128)(2,1)}, u32[]{:S(2)}) copy-start(bf16[1,2,4,128,1792]{4,3,2,1,0:T(8,128)(2,1)} %get-tuple-element.11) | copy-start | bytes 11010052
  176.9 10.1 %copy-start.3 = (bf16[1,8,128,1024]{3,2,1,0:T(8,128)(2,1)S(1)}, bf16[1,8,128,1024]{3,2,1,0:T(8,128)(2,1)}, u32[]{:S(2)}) copy-start(bf16[1,8,128,1024]{3,2,1,0:T(8,128)(2,1)} %get-tuple-element.13) | copy-start | bytes 6291460
  187.0 4.2 %copy-start.2 = (bf16[1,8,128,1024]{3,2,1,0:T(8,128)(2,1)S(1)}, bf16[1,8,128,1024]{3,2,1,0:T(8,128)(2,1)}, u32[]{:S(2)}) copy-start(bf16[1,8,128,1024]{3,2,1,0:T(8,128)(2,1)} %get-tuple-element.14) | copy-start | bytes 6291460
  187.0 4.2 %copy-start.4 = (f32[1024,1792]{1,0:T(8,128)S(1)}, f32[1024,1792]{1,0:T(8,128)}, u32[]{:S(2)}) copy-start(f32[1024,1792]{1,0:T(8,128)} %fusion.8) | copy-start | bytes 22020100

commit v18 on v17

--- a/solution.py
+++ b/solution.py
@@ -23,7 +23,7 @@
     half, quarter = rows // 2, rows // 4
     nb = s2_send.shape[0]
     blk = quarter // nb
-    step = 32
+    step = min(32, blk)
     core = {"c": 1 - c}
     chip = {"zl": 1 - z}
 
@@ -139,7 +139,7 @@
         cp.wait_send()
 
 
-def mp_merge(prior, w, cid, blocks=8):
+def mp_merge(prior, w, cid, blocks=16):
     rows, cols = prior.shape
     vmem = pltpu.MemorySpace.VMEM
     return pl.pallas_call(

time: 314 us -> 315 us (level)
  no operation moved by 1% of the time
where the time goes in v18:
time: 315 us
  Pallas kernels  270 us (86%)
  matrix products  21.9 us (7%)
  local copies, waits for them, and re-layouts  20.4 us (6%)
    pallas_call x1, Pallas kernels, gather_all(): pl.pallas_call(gather_kernel, out_shape=(jax.ShapeDtypeStruct((nx, nj, to...  159 us
    pallas_call x1, Pallas kernels, mp_merge(): pl.pallas_call(mp_merge_kernel, out_shape=jax.ShapeDtypeStruct((rows, col...  112 us
    dot_general x3, matrix products, part(): lax.dot_general(act_all[lo:hi], grad_all[lo:hi], (((0,), (0,)), ((), ()))...  21.9 us
    slice x2, local copies, waits for them, and re-layouts, part(): grad_all[lo:hi]  9.24 us

profile of v18, /device:TPU:1, one launch (start us, length us, event | category | flops | bytes accessed | tf_op | source)
XLA Modules:
  0.0 314.7 jit_solution(2327871737114311208)
XLA Ops:
  0.0 158.6 %shard_map.46 = (bf16[4,8,128,1024]{3,2,1,0:T(8,128)(2,1)}, bf16[4,2,4,128,1792]{4,3,2,1,0:T(8,128)(2,1)}, s32[4,1,128]{2,1,0:T(1,128)}, bf16[8,128,1024]{2,1,0:T(8,128)(2,1)}, bf16[4,128,1792]{2,1,0:T(8,128)(2,1)}) custom-call(bf16[128,8192]{1,0:T(8,128)(2,1)} %bitcast.20, bf16[128,7168]{1,0:T(8,128)(2,1)} %bitcast.23, s32[1,128]{1,0:T(1,128)} %seq_ref.1), custom_call_target="tpu_custom_call" | custom-call | bytes 23068672 | tf_op jit(solution)/shard_map/pallas_call | solution.py:321
  158.6 1.3 fusion.5
  160.6 0.0 copy-start
  160.6 2.9 slice.40
  163.6 1.7 copy-done
  165.3 2.4 fusion.7
  167.7 3.7 %slice.42 = bf16[2,2,4,128,1792]{4,3,2,1,0:T(8,128)(2,1)S(1)} slice(bf16[4,2,4,128,1792]{4,3,2,1,0:T(8,128)(2,1)} %get-tuple-element.10), slice={[1:3], [0:2], [0:4], [0:128], [0:1792]} | slice | bytes 14680064 | tf_op jit(solution)/shard_map/slice | solution.py:364
  171.4 5.5 %fusion.6 = (bf16[1,2,4,128,1792]{4,3,2,1,0:T(8,128)(2,1)}, bf16[1,2,4,128,1792]{4,3,2,1,0:T(8,128)(2,1)S(1)}) fusion(bf16[4,2,4,128,1792]{4,3,2,1,0:T(8,128)(2,1)} %get-tuple-element.10), kind=kLoop, calls=%fused_computation.9 | loop fusion | bytes 14680064 | tf_op jit(solution)/shard_map/slice | solution.py:364
  176.9 0.0 copy-start.1
  176.9 0.0 copy-start.3
  176.9 10.1 %fusion.8 = f32[1024,1792]{1,0:T(8,128)} fusion(bf16[2048,1024]{1,0:T(8,128)(2,1)S(1)} %bitcast.16, bf16[2048,1792]{1,0:T(8,128)(2,1)S(1)} %bitcast.15), kind=kOutput, calls=%fused_computation.11 | convolution fusion | flops 7516192768 | bytes 18874368 | tf_op jit(solution)/shard_map/dot_general | solution.py:363
  187.0 0.0 copy-done.1
  187.0 0.0 copy-done.3
  187.0 0.0 copy-start.2
  187.0 0.0 copy-start.4
  187.0 4.2 %fusion.9 = f32[1024,1792]{1,0:T(8,128)S(1)} fusion(bf16[1024,1024]{1,0:T(8,128)(2,1)S(1)} %bitcast.22, bf16[1024,1792]{1,0:T(8,128)(2,1)S(1)} %bitcast.19), kind=kOutput, calls=%fused_computation.12 | convolution fusion | flops 3758096384 | bytes 13107200 | tf_op jit(solution)/shard_map/dot_general | solution.py:363
  191.2 0.0 copy-done.2
  191.2 0.0 copy-done.4
  191.2 7.7 %fusion.3.prior_ref = f32[1024,1792]{1,0:T(8,128)} fusion(f32[1024,1792]{1,0:T(8,128)S(1)} %copy-done.4, f32[1024,1792]{1,0:T(8,128)S(1)} %fusion.9, pred[]{:T(512)S(6)} %gt.3, bf16[1024,1024]{1,0:T(8,128)(2,1)S(1)} %bitcast.21, bf16[1024,1792]{1,0:T(8,128)(2,1)S(1)} %bitcast.18), kind=kOutput, calls=%fused_computation.5 | convolution fusion | flops 3774611456 | bytes 27787264 | tf_op jit(solution)/shard_map/dot_general | solution.py:363
  198.9 111.7 %shard_map.47 = bf16[1024,1792]{1,0:T(8,128)(2,1)} custom-call(f32[1024,1792]{1,0:T(8,128)} %fusion.3.prior_ref, bf16[1024,1792]{1,0:T(8,128)(2,1)} %bitcast.17), custom_call_target="tpu_custom_call" | custom-call | flops 11010048 | bytes 22020096 | tf_op jit(solution)/shard_map/pallas_call | solution.py:145
  310.6 4.1 %copy.6 = bf16[1024,1792]{1,0:T(8,128)(2,1)} copy(bf16[1024,1792]{1,0:T(8,128)(2,1)} %shard_map.47) | data formatting | bytes 7340032
Async XLA Ops:
  160.6 4.6 %copy-start = (bf16[4,8,128,1024]{3,2,1,0:T(8,128)(2,1)S(1)}, bf16[4,8,128,1024]{3,2,1,0:T(8,128)(2,1)}, u32[]{:S(2)}) copy-start(bf16[4,8,128,1024]{3,2,1,0:T(8,128)(2,1)} %get-tuple-element.9) | copy-start | bytes 25165828
  176.9 10.1 %copy-start.1 = (bf16[1,2,4,128,1792]{4,3,2,1,0:T(8,128)(2,1)S(1)}, bf16[1,2,4,128,1792]{4,3,2,1,0:T(8,128)(2,1)}, u32[]{:S(2)}) copy-start(bf16[1,2,4,128,1792]{4,3,2,1,0:T(8,128)(2,1)} %get-tuple-element.11) | copy-start | bytes 11010052
  176.9 10.1 %copy-start.3 = (bf16[1,8,128,1024]{3,2,1,0:T(8,128)(2,1)S(1)}, bf16[1,8,128,1024]{3,2,1,0:T(8,128)(2,1)}, u32[]{:S(2)}) copy-start(bf16[1,8,128,1024]{3,2,1,0:T(8,128)(2,1)} %get-tuple-element.13) | copy-start | bytes 6291460
  187.0 4.2 %copy-start.2 = (bf16[1,8,128,1024]{3,2,1,0:T(8,128)(2,1)S(1)}, bf16[1,8,128,1024]{3,2,1,0:T(8,128)(2,1)}, u32[]{:S(2)}) copy-start(bf16[1,8,128,1024]{3,2,1,0:T(8,128)(2,1)} %get-tuple-element.14) | copy-start | bytes 6291460
  187.0 4.2 %copy-start.4 = (f32[1024,1792]{1,0:T(8,128)S(1)}, f32[1024,1792]{1,0:T(8,128)}, u32[]{:S(2)}) copy-start(f32[1024,1792]{1,0:T(8,128)} %fusion.8) | copy-start | bytes 22020100

commit v19 on v17

--- a/solution.py
+++ b/solution.py
@@ -242,7 +242,7 @@
         pltpu.make_async_copy(
             grad_in.at[:, pl.ds(pl.multiple_of(x * cw, 128), cw)], grad_ref.at[x], local.at[4]),
     ]
-    for c in own0 + q0_out + p0_out:
+    for c in own0 + p0_out + q0_out:
         c.start()
     for c in q0_in:
         c.wait_recv()

time: 314 us -> 314 us (level)
  no operation moved by 1% of the time
where the time goes in v19:
time: 314 us
  Pallas kernels  270 us (86%)
  matrix products  21.9 us (7%)
  local copies, waits for them, and re-layouts  20.4 us (6%)
    pallas_call x1, Pallas kernels, gather_all(): pl.pallas_call(gather_kernel, out_shape=(jax.ShapeDtypeStruct((nx, nj, to...  159 us
    pallas_call x1, Pallas kernels, mp_merge(): pl.pallas_call(mp_merge_kernel, out_shape=jax.ShapeDtypeStruct((rows, col...  111 us
    dot_general x3, matrix products, part(): lax.dot_general(act_all[lo:hi], grad_all[lo:hi], (((0,), (0,)), ((), ()))...  21.9 us
    slice x2, local copies, waits for them, and re-layouts, part(): grad_all[lo:hi]  9.24 us

profile of v19, /device:TPU:1, one launch (start us, length us, event | category | flops | bytes accessed | tf_op | source)
XLA Modules:
  0.0 314.2 jit_solution(4343615775557833245)
XLA Ops:
  0.0 158.6 %shard_map.46 = (bf16[4,8,128,1024]{3,2,1,0:T(8,128)(2,1)}, bf16[4,2,4,128,1792]{4,3,2,1,0:T(8,128)(2,1)}, s32[4,1,128]{2,1,0:T(1,128)}, bf16[8,128,1024]{2,1,0:T(8,128)(2,1)}, bf16[4,128,1792]{2,1,0:T(8,128)(2,1)}) custom-call(bf16[128,8192]{1,0:T(8,128)(2,1)} %bitcast.20, bf16[128,7168]{1,0:T(8,128)(2,1)} %bitcast.23, s32[1,128]{1,0:T(1,128)} %seq_ref.1), custom_call_target="tpu_custom_call" | custom-call | bytes 23068672 | tf_op jit(solution)/shard_map/pallas_call | solution.py:321
  158.6 1.3 fusion.5
  160.6 0.0 copy-start
  160.6 2.9 slice.40
  163.6 1.7 copy-done
  165.3 2.4 fusion.7
  167.7 3.7 %slice.42 = bf16[2,2,4,128,1792]{4,3,2,1,0:T(8,128)(2,1)S(1)} slice(bf16[4,2,4,128,1792]{4,3,2,1,0:T(8,128)(2,1)} %get-tuple-element.10), slice={[1:3], [0:2], [0:4], [0:128], [0:1792]} | slice | bytes 14680064 | tf_op jit(solution)/shard_map/slice | solution.py:364
  171.4 5.5 %fusion.6 = (bf16[1,2,4,128,1792]{4,3,2,1,0:T(8,128)(2,1)}, bf16[1,2,4,128,1792]{4,3,2,1,0:T(8,128)(2,1)S(1)}) fusion(bf16[4,2,4,128,1792]{4,3,2,1,0:T(8,128)(2,1)} %get-tuple-element.10), kind=kLoop, calls=%fused_computation.9 | loop fusion | bytes 14680064 | tf_op jit(solution)/shard_map/slice | solution.py:364
  176.9 0.0 copy-start.1
  176.9 0.0 copy-start.3
  176.9 10.1 %fusion.8 = f32[1024,1792]{1,0:T(8,128)} fusion(bf16[2048,1024]{1,0:T(8,128)(2,1)S(1)} %bitcast.16, bf16[2048,1792]{1,0:T(8,128)(2,1)S(1)} %bitcast.15), kind=kOutput, calls=%fused_computation.11 | convolution fusion | flops 7516192768 | bytes 18874368 | tf_op jit(solution)/shard_map/dot_general | solution.py:363
  187.0 0.0 copy-done.1
  187.0 0.0 copy-done.3
  187.0 0.0 copy-start.2
  187.0 0.0 copy-start.4
  187.0 4.2 %fusion.9 = f32[1024,1792]{1,0:T(8,128)S(1)} fusion(bf16[1024,1024]{1,0:T(8,128)(2,1)S(1)} %bitcast.22, bf16[1024,1792]{1,0:T(8,128)(2,1)S(1)} %bitcast.19), kind=kOutput, calls=%fused_computation.12 | convolution fusion | flops 3758096384 | bytes 13107200 | tf_op jit(solution)/shard_map/dot_general | solution.py:363
  191.2 0.0 copy-done.2
  191.2 0.0 copy-done.4
  191.2 7.7 %fusion.3.prior_ref = f32[1024,1792]{1,0:T(8,128)} fusion(f32[1024,1792]{1,0:T(8,128)S(1)} %copy-done.4, f32[1024,1792]{1,0:T(8,128)S(1)} %fusion.9, pred[]{:T(512)S(6)} %gt.3, bf16[1024,1024]{1,0:T(8,128)(2,1)S(1)} %bitcast.21, bf16[1024,1792]{1,0:T(8,128)(2,1)S(1)} %bitcast.18), kind=kOutput, calls=%fused_computation.5 | convolution fusion | flops 3774611456 | bytes 27787264 | tf_op jit(solution)/shard_map/dot_general | solution.py:363
  198.9 111.1 %shard_map.47 = bf16[1024,1792]{1,0:T(8,128)(2,1)} custom-call(f32[1024,1792]{1,0:T(8,128)} %fusion.3.prior_ref, bf16[1024,1792]{1,0:T(8,128)(2,1)} %bitcast.17), custom_call_target="tpu_custom_call" | custom-call | flops 11010048 | bytes 22020096 | tf_op jit(solution)/shard_map/pallas_call | solution.py:145
  310.1 4.1 %copy.6 = bf16[1024,1792]{1,0:T(8,128)(2,1)} copy(bf16[1024,1792]{1,0:T(8,128)(2,1)} %shard_map.47) | data formatting | bytes 7340032
Async XLA Ops:
  160.6 4.6 %copy-start = (bf16[4,8,128,1024]{3,2,1,0:T(8,128)(2,1)S(1)}, bf16[4,8,128,1024]{3,2,1,0:T(8,128)(2,1)}, u32[]{:S(2)}) copy-start(bf16[4,8,128,1024]{3,2,1,0:T(8,128)(2,1)} %get-tuple-element.9) | copy-start | bytes 25165828
  176.9 10.1 %copy-start.1 = (bf16[1,2,4,128,1792]{4,3,2,1,0:T(8,128)(2,1)S(1)}, bf16[1,2,4,128,1792]{4,3,2,1,0:T(8,128)(2,1)}, u32[]{:S(2)}) copy-start(bf16[1,2,4,128,1792]{4,3,2,1,0:T(8,128)(2,1)} %get-tuple-element.11) | copy-start | bytes 11010052
  176.9 10.1 %copy-start.3 = (bf16[1,8,128,1024]{3,2,1,0:T(8,128)(2,1)S(1)}, bf16[1,8,128,1024]{3,2,1,0:T(8,128)(2,1)}, u32[]{:S(2)}) copy-start(bf16[1,8,128,1024]{3,2,1,0:T(8,128)(2,1)} %get-tuple-element.13) | copy-start | bytes 6291460
  187.0 4.2 %copy-start.2 = (bf16[1,8,128,1024]{3,2,1,0:T(8,128)(2,1)S(1)}, bf16[1,8,128,1024]{3,2,1,0:T(8,128)(2,1)}, u32[]{:S(2)}) copy-start(bf16[1,8,128,1024]{3,2,1,0:T(8,128)(2,1)} %get-tuple-element.14) | copy-start | bytes 6291460
  187.0 4.2 %copy-start.4 = (f32[1024,1792]{1,0:T(8,128)S(1)}, f32[1024,1792]{1,0:T(8,128)}, u32[]{:S(2)}) copy-start(f32[1024,1792]{1,0:T(8,128)} %fusion.8) | copy-start | bytes 22020100
